TPU v7x, 32 devices: a whole 2x2x4 slice. The times are simulated.
32 devices in a mesh: section: 8 (over y, x, core), slab: 4 (over z).
Axes of the slice: x: 2, y: 2, z: 4, core: 2. Of those that a mesh axis runs over, the one named last changes fastest.
Arguments:
- fwd_states: bfloat16 [8, 128, 8, 512], P('section', None, 'slab'), may hold values from -6 to 6
- back_states: bfloat16 [8, 128, 8, 512], P('section', None, 'slab'), may hold values from -6 to 6
- back_grads: bfloat16 [8, 128, 8, 512], P('section', None, 'slab'), may hold values from -6 to 6
- batch_in: bfloat16 [128, 8, 512], P(None, 'slab'), may hold values from -6 to 6
- head_state: bfloat16 [128, 8, 512], P(None, 'slab'), may hold values from -6 to 6
- head_grad: bfloat16 [128, 8, 512], P(None, 'slab'), may hold values from -6 to 6
- couplings: bfloat16 [8, 4, 27, 64, 64], P('section'), may hold values from -0.15625 to 0.15625
Outputs:
- fwd_out: bfloat16 [8, 128, 8, 512], P('section', None, 'slab')
- back_in: bfloat16 [8, 128, 8, 512], P('section', None, 'slab')
- back_grad: bfloat16 [8, 128, 8, 512], P('section', None, 'slab')
All inputs are finite; a program needn't handle non-finite values.
Results may differ from a plain program's by a relative error of at most 0.006.
Values may be sent and summed in bfloat16 or wider, within the bound.
No kernel may reach another device: no remote copies, remote signals or barrier semaphores. Data moves between devices by JAX's collectives and lax.ppermute only.
A program may use at most 128 MiB of HBM per device.

v0:
```python
import functools

import jax
import jax.numpy as jnp
from jax import lax
from jax.experimental import pallas as pl
from jax.experimental.pallas import tpu as pltpu
from jax.sharding import PartitionSpec as P

WID = 32
PAIRS = 2
LANES = 128
F32 = jnp.float32
BF16 = jnp.bfloat16


def dot(a, b):
    return jnp.dot(a, b, preferred_element_type=F32)


def slab_place():
    z = lax.axis_index("slab")
    return z > 0, z < lax.axis_size("slab") - 1


def is_odd():
    return lax.rem(lax.axis_index("section"), 2) == 1


def pick(flag, yes, no):
    return jnp.where(jnp.full(no.shape, flag), yes, no)


def keep(flag, value):
    return jnp.where(jnp.full(value.shape, flag), value, jnp.zeros((), value.dtype))


def prepare(kernels_ref, *out_refs):
    count = 2 * PAIRS
    taps, half = kernels_ref.shape[2], kernels_ref.shape[3]
    row = lax.broadcasted_iota(jnp.int32, (half, half), 0)
    col = lax.broadcasted_iota(jnp.int32, (half, half), 1)
    unit = jnp.where(row == col, 1.0, 0.0).astype(BF16)
    for q in range(count):
        mine = [kernels_ref[0, q, k] for k in range(taps)]
        turned = [
            lax.dot_general(unit, m, (((1,), (1,)), ((), ())), preferred_element_type=F32).astype(BF16)
            for m in mine
        ]
        for b in range(3):
            pieces = [mine[9 * a + 3 * b + c] for a in range(3) for c in range(3)]
            out_refs[q][b * half : (b + 1) * half, :] = jnp.concatenate(pieces, axis=1)
            pieces = [turned[26 - (9 * a + 3 * b + c)] for a in range(3) for c in range(3)]
            out_refs[count + q][b * half : (b + 1) * half, :] = jnp.concatenate(pieces, axis=1)


def shuffle(tiles, planes, chans, back):
    size = tiles * planes * chans
    row = lax.broadcasted_iota(jnp.int32, (size, size), 1 if back else 0)
    col = lax.broadcasted_iota(jnp.int32, (size, size), 0 if back else 1)
    tp, c = row // chans, row % chans
    tile, plane = tp // planes, tp % planes
    return jnp.where(col == c * (tiles * planes) + tile * planes + plane, 1.0, 0.0).astype(BF16)


def chunk_sizes(planes, cells):
    tiles = cells // LANES
    return tiles, 256 // (tiles * planes)


def split_planes(raw, half, planes, cells):
    tiles, chans = chunk_sizes(planes, cells)
    rows = tiles * planes * chans
    matrix = shuffle(tiles, planes, chans, False)
    chunks = raw.shape[0] // rows
    parts = {}
    for g in range(0, chunks, 2):
        both = jnp.concatenate([raw[g * rows : (g + 1) * rows], raw[(g + 1) * rows : (g + 2) * rows]], axis=1)
        got = dot(matrix, both).astype(BF16)
        for i in range(2):
            for p in range(planes):
                pieces = [
                    got[(t * planes + p) * chans : (t * planes + p + 1) * chans, i * LANES : (i + 1) * LANES]
                    for t in range(tiles)
                ]
                parts[g + i, p] = jnp.concatenate(pieces, axis=1)
    per = half // chans
    count = chunks // per
    return [
        [jnp.concatenate([parts[h * per + j, p] for j in range(per)], axis=0) for p in range(planes)]
        for h in range(count)
    ]


def join_planes(values, out_ref, base):
    planes, (half, cells) = len(values), values[0].shape
    tiles, chans = chunk_sizes(planes, cells)
    rows = tiles * planes * chans
    matrix = shuffle(tiles, planes, chans, True)
    for g in range(0, half // chans, 2):
        sides = []
        for i in range(2):
            lines = slice((g + i) * chans, (g + i + 1) * chans)
            sides.append(
                jnp.concatenate(
                    [
                        values[p][lines, t * LANES : (t + 1) * LANES]
                        for t in range(tiles)
                        for p in range(planes)
                    ],
                    axis=0,
                )
            )
        got = dot(matrix, jnp.concatenate(sides, axis=1)).astype(BF16)
        for i in range(2):
            start = base + (g + i) * rows
            out_ref[start : start + rows, :] = got[:, i * LANES : (i + 1) * LANES]


def lay(stack_ref, slot, plane):
    half, cells = plane.shape
    base = slot * 3 * half
    wide = plane.astype(F32)
    column = lax.broadcasted_iota(jnp.int32, wide.shape, 1) % WID
    left = jnp.where(column > 0, pltpu.roll(wide, 1, 1), 0.0)
    right = jnp.where(column < WID - 1, pltpu.roll(wide, cells - 1, 1), 0.0)
    stack_ref[base : base + half, :] = left.astype(BF16)
    stack_ref[base + half : base + 2 * half, :] = plane.astype(BF16)
    stack_ref[base + 2 * half : base + 3 * half, :] = right.astype(BF16)


def conv(stack_ref, slot, weight_ref):
    half = weight_ref.shape[0] // 3
    cells = stack_ref.shape[1]
    begin = (slot - 1) * 3 * half
    total = dot(weight_ref[...], stack_ref[begin : begin + 9 * half, :])
    cell = lax.broadcasted_iota(jnp.int32, (half, cells), 1)
    above = jnp.where(cell >= WID, pltpu.roll(total[:half], WID, 1), 0.0)
    below = jnp.where(cell < cells - WID, pltpu.roll(total[2 * half :], cells - WID, 1), 0.0)
    return above + total[half : 2 * half] + below


def sigmoid(z):
    return jax.nn.sigmoid(z)


def rows_of(ref, index, half):
    return ref[index * half : (index + 1) * half, :]


def unpack_state(edge, wide_half, half, planes, cells, got_ref, edge_ref, own_ref, up_ref, down_ref):
    at = lax.axis_index("section")
    last = lax.axis_size("section") - 1
    at_edge = at == (last if edge else 0)
    raw = pick(at_edge, edge_ref[...], got_ref[...])
    parts = split_planes(raw, half, planes, cells)
    for h in range(2):
        for p in range(planes):
            own_ref[(h * planes + p) * half : (h * planes + p + 1) * half, :] = parts[h][p]
    other = parts[1 - wide_half]
    odd = is_odd()
    base = 0
    if wide_half is not None:
        for p in range(planes):
            up_ref[p * half : (p + 1) * half, :] = parts[wide_half][p]
            down_ref[p * half : (p + 1) * half, :] = parts[wide_half][p]
        base = planes * half
    up_ref[base : base + half, :] = pick(odd, other[0], other[planes - 1])
    down_ref[base : base + half, :] = pick(odd, other[planes - 1], other[0])


def unpack_grad(half, planes, cells, got_ref, edge_ref, own_ref, up_ref, down_ref):
    at_edge = lax.axis_index("section") == lax.axis_size("section") - 1
    raw = pick(at_edge, edge_ref[...], got_ref[...])
    parts = split_planes(raw, half, planes, cells)
    for h in range(2):
        for p in range(planes):
            own_ref[(h * planes + p) * half : (h * planes + p + 1) * half, :] = parts[h][p]
    odd = is_odd()
    up_ref[...] = pick(odd, parts[1][0], parts[1][planes - 1])
    down_ref[...] = pick(odd, parts[1][planes - 1], parts[1][0])


def halos(up_ref, down_ref, index, half):
    has_low, has_high = slab_place()
    odd = is_odd()
    first, second = rows_of(up_ref, index, half), rows_of(down_ref, index, half)
    low = keep(has_low, pick(odd, second, first))
    high = keep(has_high, pick(odd, first, second))
    return low, high


def forward_first(half, planes, own_ref, up_ref, down_ref, f_ref, g_ref, mid_ref, send_ref, s0, s1):
    has_low, has_high = slab_place()
    for p in range(planes):
        low, high = halos(up_ref, down_ref, p, half)
        lay(s0, p, low)
        lay(s0, 2 * planes + p, high)
        lay(s0, planes + p, rows_of(own_ref, planes + p, half))
    low, high = halos(up_ref, down_ref, planes, half)
    firsts = [low] + [rows_of(own_ref, p, half) for p in range(planes)] + [high]
    for j in range(planes + 2):
        z = conv(s0, planes - 1 + j, f_ref)
        y = (firsts[j].astype(F32) + z * sigmoid(z)).astype(BF16)
        if j == 0:
            y = keep(has_low, y)
        if j == planes + 1:
            y = keep(has_high, y)
        mid_ref[j * half : (j + 1) * half, :] = y
        lay(s1, j, y)
    for p in range(planes):
        z = conv(s1, 1 + p, g_ref)
        y = (rows_of(own_ref, planes + p, half).astype(F32) + z * sigmoid(z)).astype(BF16)
        send_ref[p * half : (p + 1) * half, :] = y


def forward_second(half, planes, mid_ref, own_ref, up_ref, down_ref, f_ref, g_ref, out_ref, s0, s1):
    has_low, has_high = slab_place()
    for p in range(planes):
        low, high = halos(up_ref, down_ref, p, half)
        lay(s0, p, low)
        lay(s0, 2 * planes + p, high)
        lay(s0, planes + p, rows_of(own_ref, p, half))
    tops = []
    for j in range(planes + 2):
        z = conv(s0, planes - 1 + j, f_ref)
        y = (rows_of(mid_ref, j, half).astype(F32) + z * sigmoid(z)).astype(BF16)
        if j == 0:
            y = keep(has_low, y)
        elif j == planes + 1:
            y = keep(has_high, y)
        else:
            tops.append(y)
        lay(s1, j, y)
    bottoms = []
    for p in range(planes):
        z = conv(s1, 1 + p, g_ref)
        bottoms.append((rows_of(own_ref, p, half).astype(F32) + z * sigmoid(z)).astype(BF16))
    join_planes(tops, out_ref, 0)
    join_planes(bottoms, out_ref, out_ref.shape[0] // 2)


def turn(z, low_value, grad):
    sig = sigmoid(z)
    second = (low_value.astype(F32) - z * sig).astype(BF16)
    inner = (sig * (1.0 + z * (1.0 - sig)) * grad).astype(BF16)
    return second, inner


def backward_first(
    half, planes, y_ref, g_ref, yu_ref, yd_ref, gu_ref, gd_ref, wg_ref, wf_ref, tg_ref,
    send_ref, second_ref, low_grad_ref, carry_ref, s0, s1, s2,
):
    has_low, has_high = slab_place()
    for p in range(planes):
        low, high = halos(yu_ref, yd_ref, p, half)
        lay(s0, p, low)
        lay(s0, 2 * planes + p, high)
        lay(s0, planes + p, rows_of(y_ref, p, half))
    low, high = halos(yu_ref, yd_ref, planes, half)
    lowers = [low] + [rows_of(y_ref, planes + p, half) for p in range(planes)] + [high]
    low, high = halos(gu_ref, gd_ref, 0, half)
    grads = [low] + [rows_of(g_ref, planes + p, half) for p in range(planes)] + [high]
    for j in range(planes + 2):
        z = conv(s0, planes - 1 + j, wg_ref)
        second, inner = turn(z, lowers[j], grads[j].astype(F32))
        if j == 0:
            second, inner = keep(has_low, second), keep(has_low, inner)
        if j == planes + 1:
            second, inner = keep(has_high, second), keep(has_high, inner)
        second_ref[j * half : (j + 1) * half, :] = second
        low_grad_ref[j * half : (j + 1) * half, :] = grads[j]
        lay(s1, j, second)
        lay(s2, j, inner)
    for p in range(planes):
        z = conv(s1, 1 + p, wf_ref)
        carry = rows_of(g_ref, p, half).astype(F32) + conv(s2, 1 + p, tg_ref)
        first, inner = turn(z, rows_of(y_ref, p, half), carry)
        carry_ref[p * half : (p + 1) * half, :] = carry
        send_ref[p * half : (p + 1) * half, :] = first
        send_ref[(planes + p) * half : (planes + p + 1) * half, :] = inner


def backward_second(
    half, planes, mine_ref, up_ref, down_ref, second_ref, low_grad_ref, carry_ref,
    tf_ref, wg_ref, wf_ref, tg_ref,
    state_ref, inner_ref, low_ref, top_ref, out_up_ref, out_down_ref, s0, s1, s2, s3,
):
    has_low, has_high = slab_place()
    odd = is_odd()
    for p in range(planes):
        low, high = halos(up_ref, down_ref, p, half)
        lay(s0, p, low)
        lay(s0, 2 * planes + p, high)
        lay(s0, planes + p, rows_of(mine_ref, p, half))
        low, high = halos(up_ref, down_ref, planes + p, half)
        lay(s2, p, low)
        lay(s2, 2 * planes + p, high)
        lay(s2, planes + p, rows_of(mine_ref, planes + p, half))
    for j in range(planes + 2):
        grad = rows_of(low_grad_ref, j, half).astype(F32) + conv(s2, planes - 1 + j, tf_ref)
        z = conv(s0, planes - 1 + j, wg_ref)
        second, inner = turn(z, rows_of(second_ref, j, half), grad)
        if j == 0:
            second, inner = keep(has_low, second), keep(has_low, inner)
        elif j == planes + 1:
            second, inner = keep(has_high, second), keep(has_high, inner)
        else:
            low_ref[(j - 1) * half : j * half, :] = grad
            state_ref[(planes + j - 1) * half : (planes + j) * half, :] = second
        lay(s1, j, second)
        lay(s3, j, inner)
    inners = []
    for p in range(planes):
        z = conv(s1, 1 + p, wf_ref)
        carry = rows_of(carry_ref, p, half) + conv(s3, 1 + p, tg_ref)
        first, inner = turn(z, rows_of(mine_ref, p, half), carry)
        state_ref[p * half : (p + 1) * half, :] = first
        top_ref[p * half : (p + 1) * half, :] = carry.astype(BF16)
        inner_ref[p * half : (p + 1) * half, :] = inner
        inners.append(inner)
    out_up_ref[...] = pick(odd, inners[0], inners[planes - 1])
    out_down_ref[...] = pick(odd, inners[planes - 1], inners[0])


def backward_third(half, planes, inner_ref, up_ref, down_ref, low_ref, top_ref, tf_ref, out_ref, s0):
    low, high = halos(up_ref, down_ref, 0, half)
    lay(s0, 0, low)
    lay(s0, planes + 1, high)
    for p in range(planes):
        lay(s0, 1 + p, rows_of(inner_ref, p, half))
    lows = [(rows_of(low_ref, p, half) + conv(s0, 1 + p, tf_ref)).astype(BF16) for p in range(planes)]
    join_planes([rows_of(top_ref, p, half) for p in range(planes)], out_ref, 0)
    join_planes(lows, out_ref, out_ref.shape[0] // 2)


def pack_state(half, planes, state_ref, out_ref):
    for h in range(2):
        join_planes(
            [rows_of(state_ref, h * planes + p, half) for p in range(planes)], out_ref, h * out_ref.shape[0] // 2
        )


def call(body, name, outs, scratch, flops, *args):
    in_place = pl.BlockSpec(memory_space=pltpu.VMEM)
    return pl.pallas_call(
        body,
        name=name,
        out_shape=[jax.ShapeDtypeStruct(shape, dtype) for shape, dtype in outs],
        in_specs=[in_place] * len(args),
        out_specs=[in_place] * len(outs),
        scratch_shapes=[pltpu.VMEM(shape, BF16) for shape in scratch],
        cost_estimate=pl.CostEstimate(flops=flops, bytes_accessed=1 << 20, transcendentals=0),
    )(*args)


def raw_view(block):
    chans, planes, cells = block.shape
    tiles = cells // LANES
    return block.reshape(chans, planes, tiles, LANES).transpose(0, 2, 1, 3).reshape(-1, LANES)


def from_raw(raw, chans, planes, cells):
    tiles = cells // LANES
    return raw.reshape(chans, tiles, planes, LANES).transpose(0, 2, 1, 3).reshape(1, chans, planes, cells)


def round_trips(sections, slabs):
    ahead = []
    for s in range(0, sections, 2):
        order = [s * slabs + z for z in range(slabs)] + [(s + 1) * slabs + z for z in reversed(range(slabs))]
        ahead += list(zip(order, order[1:] + order[:1]))
    return ahead, [(b, a) for a, b in ahead]


def shards(fwd_states, back_states, back_grads, batch_in, head_state, head_grad, couplings):
    sections, slabs = lax.axis_size("section"), lax.axis_size("slab")
    ahead, behind = round_trips(sections, slabs)
    _, chans, planes, cells = fwd_states.shape
    half = chans // 2

    def swap(up, down):
        return lax.ppermute(up, ("section", "slab"), ahead), lax.ppermute(down, ("section", "slab"), behind)

    def along(value, step):
        return lax.ppermute(value, "section", [(s, (s + step) % sections) for s in range(sections)])

    got_y = along(raw_view(back_states[0]), -1)
    got_g = along(raw_view(back_grads[0]), -1)
    got_x = along(raw_view(fwd_states[0]), 1)

    def planes_of(count, dtype=BF16):
        return ((count * half, cells), dtype)

    unit = 2 * 9 * half * 3 * half * cells
    weights = call(
        prepare, "prepare", [((3 * half, 9 * half), BF16)] * (4 * PAIRS), [], unit, couplings
    )
    direct, turned = weights[: 2 * PAIRS], weights[2 * PAIRS :]

    sizes = (half, planes, cells)
    y_own, y_up, y_down = call(
        functools.partial(unpack_state, True, 0, *sizes), "unpack_y",
        [planes_of(2 * planes), planes_of(planes + 1), planes_of(planes + 1)], [], unit, got_y, raw_view(head_state),
    )
    g_own, g_up, g_down = call(
        functools.partial(unpack_grad, *sizes), "unpack_g",
        [planes_of(2 * planes), planes_of(1), planes_of(1)], [], unit, got_g, raw_view(head_grad),
    )
    x_own, x_up, x_down = call(
        functools.partial(unpack_state, False, 1, *sizes), "unpack_x",
        [planes_of(2 * planes), planes_of(planes + 1), planes_of(planes + 1)], [], unit, got_x, raw_view(batch_in),
    )
    yu, yd = swap(y_up, y_down)
    gu, gd = swap(g_up, g_down)
    xu, xd = swap(x_up, x_down)

    wide = ((3 * planes) * 3 * half, cells)
    near = ((planes + 2) * 3 * half, cells)
    send, second, low_grad, carry = call(
        functools.partial(backward_first, half, planes), "backward_first",
        [planes_of(2 * planes), planes_of(planes + 2), planes_of(planes + 2), planes_of(planes, F32)],
        [wide, near, near], 8 * unit,
        y_own, g_own, yu, yd, gu, gd, direct[3], direct[2], turned[3],
    )
    su, sd = swap(send, send)
    mid, low_own = call(
        functools.partial(forward_first, half, planes), "forward_first",
        [planes_of(planes + 2), planes_of(planes)], [wide, near], 6 * unit,
        x_own, xu, xd, direct[0], direct[1],
    )
    fu, fd = swap(low_own, low_own)
    state, inner, low, top, iu, id_ = call(
        functools.partial(backward_second, half, planes), "backward_second",
        [planes_of(2 * planes), planes_of(planes), planes_of(planes, F32), planes_of(planes), planes_of(1), planes_of(1)],
        [wide, near, wide, near], 12 * unit,
        send, su, sd, second, low_grad, carry, turned[2], direct[1], direct[0], turned[1],
    )
    iu, id_ = swap(iu, id_)
    raw_out = ((chans * planes * cells // LANES, LANES), BF16)
    (fwd_raw,) = call(
        functools.partial(forward_second, half, planes), "forward_second", [raw_out], [wide, near], 6 * unit,
        mid, low_own, fu, fd, direct[2], direct[3],
    )
    (state_raw,) = call(functools.partial(pack_state, half, planes), "pack_state", [raw_out], [], unit, state)
    (grad_raw,) = call(
        functools.partial(backward_third, half, planes), "backward_third", [raw_out], [near], 2 * unit,
        inner, iu, id_, low, top, turned[0],
    )
    shape = (chans, planes, cells)
    return from_raw(fwd_raw, *shape), from_raw(state_raw, *shape), from_raw(grad_raw, *shape)


def solution(mesh):
    return jax.shard_map(
        shards,
        mesh=mesh,
        in_specs=(
            P("section", None, "slab", None),
            P("section", None, "slab", None),
            P("section", None, "slab", None),
            P(None, "slab", None),
            P(None, "slab", None),
            P(None, "slab", None),
            P("section", None, None, None, None),
        ),
        out_specs=(
            P("section", None, "slab", None),
            P("section", None, "slab", None),
            P("section", None, "slab", None),
        ),
        check_vma=False,
    )
```

profile of v0, /device:TPU:0, one launch (start us, length us, event | category | flops | bytes accessed | tf_op | source)
XLA Modules:
  0.0 60.4 jit_solution(12178027875906861090)
XLA Ops:
  0.6 3.4 %collective-permute-start.5 = (bf16[1024,128]{1,0:T(8,128)(2,1)}, bf16[1024,128]{1,0:T(8,128)(2,1)S(1)}, u32[]{:S(2)}, u32[]{:S(2)}) collective-permute-start(bf16[1024,128]{1,0:T(8,128)(2,1)} %bitcast.50), channel_id=1, source_target_pairs={{0,28},{4,0},{8,4},{12,8},{16,12},{20,16},{24,20},{28,24},{1,29},{... | collective-permute-start | bytes 786440 | tf_op jit(solution)/shard_map/ppermute | solution.py:386
  4.0 0.7 %collective-permute-start.6 = (bf16[1024,128]{1,0:T(8,128)(2,1)}, bf16[1024,128]{1,0:T(8,128)(2,1)S(1)}, u32[]{:S(2)}, u32[]{:S(2)}) collective-permute-start(bf16[1024,128]{1,0:T(8,128)(2,1)} %bitcast.51), channel_id=1, source_target_pairs={{0,28},{4,0},{8,4},{12,8},{16,12},{20,16},{24,20},{28,24},{1,29},{... | collective-permute-start | bytes 786440 | tf_op jit(solution)/shard_map/ppermute | solution.py:386
  4.7 0.0 collective-permute-start
  4.7 6.2 %collective-permute-done.5.got_ref = bf16[1024,128]{1,0:T(8,128)(2,1)S(1)} collective-permute-done((bf16[1024,128]{1,0:T(8,128)(2,1)}, bf16[1024,128]{1,0:T(8,128)(2,1)S(1)}, u32[]{:S(2)}, u32[]{:S(2)}) %collective-permute-start.5) | collective-permute-done | bytes 262176 | tf_op jit(solution)/shard_map/ppermute | solution.py:386
  10.9 0.0 copy-start.2
  10.9 0.7 %copy-done.2 = bf16[1024,128]{1,0:T(8,128)(2,1)} copy-done((bf16[1024,128]{1,0:T(8,128)(2,1)}, bf16[1024,128]{1,0:T(8,128)(2,1)S(1)}, u32[]{:S(2)}) %copy-start.2) | copy-done | bytes 262168
  11.6 2.1 %unpack_y.1 = (bf16[256,512]{1,0:T(8,128)(2,1)}, bf16[192,512]{1,0:T(8,128)(2,1)}, bf16[192,512]{1,0:T(8,128)(2,1)}) custom-call(bf16[1024,128]{1,0:T(8,128)(2,1)} %copy-done.2, bf16[1024,128]{1,0:T(8,128)(2,1)} %bitcast.45), custom_call_target="tpu_custom_call" | custom-call | flops 113246208 | bytes 1048576 | tf_op jit(solution)/shard_map/unpack_y/pallas_call | solution.py:346
  13.7 1.6 %collective-permute-start.7 = (bf16[192,512]{1,0:T(8,128)(2,1)}, bf16[192,512]{1,0:T(8,128)(2,1)S(1)}, u32[]{:S(2)}, u32[]{:S(2)}) collective-permute-start(bf16[192,512]{1,0:T(8,128)(2,1)} %get-tuple-element.43), channel_id=1, source_target_pairs={{0,1},{1,2},{2,3},{3,7},{7,6},{6,5},{5,4},{4,0},{8,9},{9,10},{10,1... | collective-permute-start | bytes 589832 | tf_op jit(solution)/shard_map/ppermute | solution.py:383
  15.3 0.0 collective-permute-start.8
  15.3 0.0 collective-permute-done.6.got_ref
  15.3 0.0 copy-start.1
  15.3 0.7 %copy-done.1 = bf16[1024,128]{1,0:T(8,128)(2,1)} copy-done((bf16[1024,128]{1,0:T(8,128)(2,1)}, bf16[1024,128]{1,0:T(8,128)(2,1)S(1)}, u32[]{:S(2)}) %copy-start.1) | copy-done | bytes 262168
  16.0 2.1 %unpack_g.1 = (bf16[256,512]{1,0:T(8,128)(2,1)}, bf16[64,512]{1,0:T(8,128)(2,1)}, bf16[64,512]{1,0:T(8,128)(2,1)}) custom-call(bf16[1024,128]{1,0:T(8,128)(2,1)} %copy-done.1, bf16[1024,128]{1,0:T(8,128)(2,1)} %bitcast.46), custom_call_target="tpu_custom_call" | custom-call | flops 113246208 | bytes 1048576 | tf_op jit(solution)/shard_map/unpack_g/pallas_call | solution.py:346
  18.1 0.0 collective-permute-start.10
  18.1 2.0 %collective-permute-start.9 = (bf16[64,512]{1,0:T(8,128)(2,1)}, bf16[64,512]{1,0:T(8,128)(2,1)S(1)}, u32[]{:S(2)}, u32[]{:S(2)}) collective-permute-start(bf16[64,512]{1,0:T(8,128)(2,1)} %get-tuple-element.45), channel_id=1, source_target_pairs={{0,1},{1,2},{2,3},{3,7},{7,6},{6,5},{5,4},{4,0},{8,9},{9,10},{10,1... | collective-permute-start | bytes 196616 | tf_op jit(solution)/shard_map/ppermute | solution.py:383
  20.1 3.5 %prepare.1 = (bf16[192,576]{1,0:T(8,128)(2,1)}, bf16[192,576]{1,0:T(8,128)(2,1)}, bf16[192,576]{1,0:T(8,128)(2,1)}, bf16[192,576]{1,0:T(8,128)(2,1)}, bf16[192,5...) custom-call(bf16[1,4,27,64,64]{4,3,2,1,0:T(8,128)(2,1)} %kernels_ref.1), custom_call_target="tpu_custom_call" | custom-call | flops 113246208 | bytes 1048576 | tf_op jit(solution)/shard_map/prepare/pallas_call | solution.py:346
  23.6 0.0 collective-permute-done.got_ref
  23.6 0.0 copy-start
  23.6 0.7 %copy-done = bf16[1024,128]{1,0:T(8,128)(2,1)} copy-done((bf16[1024,128]{1,0:T(8,128)(2,1)}, bf16[1024,128]{1,0:T(8,128)(2,1)S(1)}, u32[]{:S(2)}) %copy-start) | copy-done | bytes 262168
  24.3 2.1 %unpack_x.1 = (bf16[256,512]{1,0:T(8,128)(2,1)}, bf16[192,512]{1,0:T(8,128)(2,1)}, bf16[192,512]{1,0:T(8,128)(2,1)}) custom-call(bf16[1024,128]{1,0:T(8,128)(2,1)} %copy-done, bf16[1024,128]{1,0:T(8,128)(2,1)} %bitcast.47), custom_call_target="tpu_custom_call" | custom-call | flops 113246208 | bytes 1048576 | tf_op jit(solution)/shard_map/unpack_x/pallas_call | solution.py:346
  26.4 2.0 %collective-permute-start.1 = (bf16[192,512]{1,0:T(8,128)(2,1)}, bf16[192,512]{1,0:T(8,128)(2,1)S(1)}, u32[]{:S(2)}, u32[]{:S(2)}) collective-permute-start(bf16[192,512]{1,0:T(8,128)(2,1)} %get-tuple-element.33), channel_id=1, source_target_pairs={{0,1},{1,2},{2,3},{3,7},{7,6},{6,5},{5,4},{4,0},{8,9},{9,10},{10,1... | collective-permute-start | bytes 589832 | tf_op jit(solution)/shard_map/ppermute | solution.py:383
  28.4 0.0 collective-permute-done.10.gd_ref
  28.4 0.0 collective-permute-start.2
  28.4 0.0 collective-permute-done.9.gu_ref
  28.4 0.0 copy-start.14
  28.4 0.0 collective-permute-done.7.yu_ref
  28.4 0.0 copy-start.7
  28.5 0.0 collective-permute-done.8.yd_ref
  28.5 0.0 copy-start.8
  28.5 0.6 copy-done.13
  29.0 0.0 copy-done.14
  29.1 0.1 copy-done.7
  29.1 0.1 copy-done.8
  29.2 4.2 %backward_first.1 = (bf16[256,512]{1,0:T(8,128)(2,1)}, bf16[256,512]{1,0:T(8,128)(2,1)}, bf16[256,512]{1,0:T(8,128)(2,1)}, f32[128,512]{1,0:T(8,128)}) custom-call(bf16[256,512]{1,0:T(8,128)(2,1)} %get-tuple-element.41.y_ref, bf16[256,512]{1,0:T(8,128)(2,1)} %get-tuple-element.42.g_ref, bf16[192,512]{1,0:T(8,128)(2,1)} %copy-done.7, ...), custom_call_target="tpu_custom_call" | custom-call | flops 905969664 | bytes 1048576 | tf_op jit(solution)/shard_map/backward_first/pallas_call | solution.py:346
  33.4 2.0 %collective-permute-start.11 = (bf16[256,512]{1,0:T(8,128)(2,1)}, bf16[256,512]{1,0:T(8,128)(2,1)S(1)}, u32[]{:S(2)}, u32[]{:S(2)}) collective-permute-start(bf16[256,512]{1,0:T(8,128)(2,1)} %get-tuple-element.48.mine_ref), channel_id=1, source_target_pairs={{0,1},{1,2},{2,3},{3,7},{7,6},{6,5},{5,4},{4,0},{8,9},{9,10},{10,1... | collective-permute-start | bytes 786440 | tf_op jit(solution)/shard_map/ppermute | solution.py:383
  35.4 0.0 collective-permute-start.12
  35.4 0.0 collective-permute-done.1.up_ref
  35.4 0.0 collective-permute-done.2.down_ref
  35.5 0.0 copy-start.10
  35.5 0.7 %copy-done.9 = bf16[192,512]{1,0:T(8,128)(2,1)} copy-done((bf16[192,512]{1,0:T(8,128)(2,1)}, bf16[192,512]{1,0:T(8,128)(2,1)S(1)}, u32[]{:S(2)}) %copy-start.9) | copy-done | bytes 196632
  36.1 0.1 copy-done.10
  36.2 3.5 %forward_first.1 = (bf16[256,512]{1,0:T(8,128)(2,1)}, bf16[128,512]{1,0:T(8,128)(2,1)}) custom-call(bf16[256,512]{1,0:T(8,128)(2,1)} %get-tuple-element.32.own_ref, bf16[192,512]{1,0:T(8,128)(2,1)} %copy-done.9, bf16[192,512]{1,0:T(8,128)(2,1)} %copy-done.10, bf16[192,576]{1,0:T(8,128)(2,1)} %get-tuple-element.35.f_ref.wf_ref, ...), custom_call_target="tpu_custom_call" | custom-call | flops 679477248 | bytes 1048576 | tf_op jit(solution)/shard_map/forward_first/pallas_call | solution.py:346
  39.7 2.0 %collective-permute-start.3 = (bf16[128,512]{1,0:T(8,128)(2,1)}, bf16[128,512]{1,0:T(8,128)(2,1)S(1)}, u32[]{:S(2)}, u32[]{:S(2)}) collective-permute-start(bf16[128,512]{1,0:T(8,128)(2,1)} %get-tuple-element.38.own_ref), channel_id=1, source_target_pairs={{0,1},{1,2},{2,3},{3,7},{7,6},{6,5},{5,4},{4,0},{8,9},{9,10},{10,1... | collective-permute-start | bytes 393224 | tf_op jit(solution)/shard_map/ppermute | solution.py:383
  41.7 0.0 collective-permute-start.4
  41.7 0.0 collective-permute-done.11.up_ref
  41.7 1.4 %collective-permute-done.12.down_ref = bf16[256,512]{1,0:T(8,128)(2,1)S(1)} collective-permute-done((bf16[256,512]{1,0:T(8,128)(2,1)}, bf16[256,512]{1,0:T(8,128)(2,1)S(1)}, u32[]{:S(2)}, u32[]{:S(2)}) %collective-permute-start.12) | collective-permute-done | bytes 262176 | tf_op jit(solution)/shard_map/ppermute | solution.py:383
  43.1 0.0 copy-done.5
  43.1 0.7 %copy-done.6 = bf16[256,512]{1,0:T(8,128)(2,1)} copy-done((bf16[256,512]{1,0:T(8,128)(2,1)}, bf16[256,512]{1,0:T(8,128)(2,1)S(1)}, u32[]{:S(2)}) %copy-start.6) | copy-done | bytes 262168
  43.8 5.0 %backward_second.1 = (bf16[256,512]{1,0:T(8,128)(2,1)}, bf16[128,512]{1,0:T(8,128)(2,1)}, f32[128,512]{1,0:T(8,128)}, bf16[128,512]{1,0:T(8,128)(2,1)}, bf16[64,...) custom-call(bf16[256,512]{1,0:T(8,128)(2,1)} %get-tuple-element.48.mine_ref, bf16[256,512]{1,0:T(8,128)(2,1)} %copy-done.5, ...), custom_call_target="tpu_custom_call" | custom-call | flops 1358954496 | bytes 1048576 | tf_op jit(solution)/shard_map/backward_second/pallas_call | solution.py:346
  48.8 1.9 %collective-permute-start.13 = (bf16[64,512]{1,0:T(8,128)(2,1)}, bf16[64,512]{1,0:T(8,128)(2,1)S(1)}, u32[]{:S(2)}, u32[]{:S(2)}) collective-permute-start(bf16[64,512]{1,0:T(8,128)(2,1)} %get-tuple-element.56), channel_id=1, source_target_pairs={{0,1},{1,2},{2,3},{3,7},{7,6},{6,5},{5,4},{4,0},{8,9},{9,10},{10,1... | collective-permute-start | bytes 196616 | tf_op jit(solution)/shard_map/ppermute | solution.py:383
  50.7 0.0 collective-permute-start.14
  50.7 0.0 collective-permute-done.3.up_ref
  50.7 0.0 collective-permute-done.4.down_ref
  50.7 0.0 copy-start.12
  50.7 0.6 %copy-done.11 = bf16[128,512]{1,0:T(8,128)(2,1)} copy-done((bf16[128,512]{1,0:T(8,128)(2,1)}, bf16[128,512]{1,0:T(8,128)(2,1)S(1)}, u32[]{:S(2)}) %copy-start.11) | copy-done | bytes 131096
  51.4 0.0 copy-done.12
  51.4 3.7 %forward_second.1 = bf16[1024,128]{1,0:T(8,128)(2,1)} custom-call(bf16[256,512]{1,0:T(8,128)(2,1)} %get-tuple-element.37.mid_ref, bf16[128,512]{1,0:T(8,128)(2,1)} %get-tuple-element.38.own_ref, bf16[128,512]{1,0:T(8,128)(2,1)} %copy-done.11, bf16[128,512]{1,0:T(8,128)(2,1)} %copy-done.12, bf16[192,576]{1,0:T(8,128)(2,1)} %get-tuple-element.39.f_ref.wf_ref, ...), custom_call_target="tpu_custom_call" | custom-call | flops 679477248 | bytes 1048576 | tf_op jit(solution)/shard_map/forward_second/pallas_call | solution.py:346
  55.1 1.9 %pack_state.1 = bf16[1024,128]{1,0:T(8,128)(2,1)} custom-call(bf16[256,512]{1,0:T(8,128)(2,1)} %get-tuple-element.54.state_ref), custom_call_target="tpu_custom_call" | custom-call | flops 113246208 | bytes 1048576 | tf_op jit(solution)/shard_map/pack_state/pallas_call | solution.py:346
  57.0 0.0 collective-permute-done.13.up_ref
  57.0 0.0 collective-permute-done.14.down_ref
  57.0 0.0 copy-start.4
  57.0 0.6 copy-done.3
  57.6 0.0 copy-done.4
  57.6 2.8 %backward_third.1 = bf16[1024,128]{1,0:T(8,128)(2,1)} custom-call(bf16[128,512]{1,0:T(8,128)(2,1)} %get-tuple-element.55.inner_ref, bf16[64,512]{1,0:T(8,128)(2,1)} %copy-done.3, bf16[64,512]{1,0:T(8,128)(2,1)} %copy-done.4, f32[128,512]{1,0:T(8,128)} %get-tuple-element.58.low_ref, bf16[128,512]{1,0:T(8,128)(2,1)} %get-tuple-element.59.top_ref, ...), custom_call_target="tpu_custom_call" | custom-call | flops 226492416 | bytes 1048576 | tf_op jit(solution)/shard_map/backward_third/pallas_call | solution.py:346
  (6 shorter events, 0.0 us)
Async XLA Ops:
  0.6 10.3 %collective-permute-start.5 = (bf16[1024,128]{1,0:T(8,128)(2,1)}, bf16[1024,128]{1,0:T(8,128)(2,1)S(1)}, u32[]{:S(2)}, u32[]{:S(2)}) collective-permute-start(bf16[1024,128]{1,0:T(8,128)(2,1)} %bitcast.50), channel_id=1, source_target_pairs={{0,28},{4,0},{8,4},{12,8},{16,12},{20,16},{24,20},{28,24},{1,29},{... | collective-permute-start | bytes 786440 | tf_op jit(solution)/shard_map/ppermute | solution.py:386
  4.0 11.3 %collective-permute-start.6 = (bf16[1024,128]{1,0:T(8,128)(2,1)}, bf16[1024,128]{1,0:T(8,128)(2,1)S(1)}, u32[]{:S(2)}, u32[]{:S(2)}) collective-permute-start(bf16[1024,128]{1,0:T(8,128)(2,1)} %bitcast.51), channel_id=1, source_target_pairs={{0,28},{4,0},{8,4},{12,8},{16,12},{20,16},{24,20},{28,24},{1,29},{... | collective-permute-start | bytes 786440 | tf_op jit(solution)/shard_map/ppermute | solution.py:386
  4.7 18.8 %collective-permute-start = (bf16[1024,128]{1,0:T(8,128)(2,1)}, bf16[1024,128]{1,0:T(8,128)(2,1)S(1)}, u32[]{:S(2)}, u32[]{:S(2)}) collective-permute-start(bf16[1024,128]{1,0:T(8,128)(2,1)} %bitcast.52), channel_id=1, source_target_pairs={{0,4},{4,8},{8,12},{12,16},{16,20},{20,24},{24,28},{28,0},{1,5},{5... | collective-permute-start | bytes 786440 | tf_op jit(solution)/shard_map/ppermute | solution.py:386
  10.9 0.7 %copy-start.2 = (bf16[1024,128]{1,0:T(8,128)(2,1)}, bf16[1024,128]{1,0:T(8,128)(2,1)S(1)}, u32[]{:S(2)}) copy-start(bf16[1024,128]{1,0:T(8,128)(2,1)S(1)} %collective-permute-done.5.got_ref) | copy-start | bytes 786436
  13.7 14.7 %collective-permute-start.7 = (bf16[192,512]{1,0:T(8,128)(2,1)}, bf16[192,512]{1,0:T(8,128)(2,1)S(1)}, u32[]{:S(2)}, u32[]{:S(2)}) collective-permute-start(bf16[192,512]{1,0:T(8,128)(2,1)} %get-tuple-element.43), channel_id=1, source_target_pairs={{0,1},{1,2},{2,3},{3,7},{7,6},{6,5},{5,4},{4,0},{8,9},{9,10},{10,1... | collective-permute-start | bytes 589832 | tf_op jit(solution)/shard_map/ppermute | solution.py:383
  15.3 13.2 %collective-permute-start.8 = (bf16[192,512]{1,0:T(8,128)(2,1)}, bf16[192,512]{1,0:T(8,128)(2,1)S(1)}, u32[]{:S(2)}, u32[]{:S(2)}) collective-permute-start(bf16[192,512]{1,0:T(8,128)(2,1)} %get-tuple-element.44), channel_id=1, source_target_pairs={{1,0},{2,1},{3,2},{7,3},{6,7},{5,6},{4,5},{0,4},{9,8},{10,9},{11,1... | collective-permute-start | bytes 589832 | tf_op jit(solution)/shard_map/ppermute | solution.py:383
  15.3 0.7 %copy-start.1 = (bf16[1024,128]{1,0:T(8,128)(2,1)}, bf16[1024,128]{1,0:T(8,128)(2,1)S(1)}, u32[]{:S(2)}) copy-start(bf16[1024,128]{1,0:T(8,128)(2,1)S(1)} %collective-permute-done.6.got_ref) | copy-start | bytes 786436
  18.1 10.3 %collective-permute-start.10 = (bf16[64,512]{1,0:T(8,128)(2,1)}, bf16[64,512]{1,0:T(8,128)(2,1)S(1)}, u32[]{:S(2)}, u32[]{:S(2)}) collective-permute-start(bf16[64,512]{1,0:T(8,128)(2,1)} %get-tuple-element.46), channel_id=1, source_target_pairs={{1,0},{2,1},{3,2},{7,3},{6,7},{5,6},{4,5},{0,4},{9,8},{10,9},{11,1... | collective-permute-start | bytes 196616 | tf_op jit(solution)/shard_map/ppermute | solution.py:383
  18.1 10.3 %collective-permute-start.9 = (bf16[64,512]{1,0:T(8,128)(2,1)}, bf16[64,512]{1,0:T(8,128)(2,1)S(1)}, u32[]{:S(2)}, u32[]{:S(2)}) collective-permute-start(bf16[64,512]{1,0:T(8,128)(2,1)} %get-tuple-element.45), channel_id=1, source_target_pairs={{0,1},{1,2},{2,3},{3,7},{7,6},{6,5},{5,4},{4,0},{8,9},{9,10},{10,1... | collective-permute-start | bytes 196616 | tf_op jit(solution)/shard_map/ppermute | solution.py:383
  23.6 0.7 %copy-start = (bf16[1024,128]{1,0:T(8,128)(2,1)}, bf16[1024,128]{1,0:T(8,128)(2,1)S(1)}, u32[]{:S(2)}) copy-start(bf16[1024,128]{1,0:T(8,128)(2,1)S(1)} %collective-permute-done.got_ref) | copy-start | bytes 786436
  26.4 9.1 %collective-permute-start.1 = (bf16[192,512]{1,0:T(8,128)(2,1)}, bf16[192,512]{1,0:T(8,128)(2,1)S(1)}, u32[]{:S(2)}, u32[]{:S(2)}) collective-permute-start(bf16[192,512]{1,0:T(8,128)(2,1)} %get-tuple-element.33), channel_id=1, source_target_pairs={{0,1},{1,2},{2,3},{3,7},{7,6},{6,5},{5,4},{4,0},{8,9},{9,10},{10,1... | collective-permute-start | bytes 589832 | tf_op jit(solution)/shard_map/ppermute | solution.py:383
  28.4 0.6 %copy-start.13 = (bf16[64,512]{1,0:T(8,128)(2,1)}, bf16[64,512]{1,0:T(8,128)(2,1)S(1)}, u32[]{:S(2)}) copy-start(bf16[64,512]{1,0:T(8,128)(2,1)S(1)} %collective-permute-done.10.gd_ref) | copy-start | bytes 196612
  28.4 7.0 %collective-permute-start.2 = (bf16[192,512]{1,0:T(8,128)(2,1)}, bf16[192,512]{1,0:T(8,128)(2,1)S(1)}, u32[]{:S(2)}, u32[]{:S(2)}) collective-permute-start(bf16[192,512]{1,0:T(8,128)(2,1)} %get-tuple-element.34), channel_id=1, source_target_pairs={{1,0},{2,1},{3,2},{7,3},{6,7},{5,6},{4,5},{0,4},{9,8},{10,9},{11,1... | collective-permute-start | bytes 589832 | tf_op jit(solution)/shard_map/ppermute | solution.py:383
  28.4 0.6 %copy-start.14 = (bf16[64,512]{1,0:T(8,128)(2,1)}, bf16[64,512]{1,0:T(8,128)(2,1)S(1)}, u32[]{:S(2)}) copy-start(bf16[64,512]{1,0:T(8,128)(2,1)S(1)} %collective-permute-done.9.gu_ref) | copy-start | bytes 196612
  28.4 0.7 %copy-start.7 = (bf16[192,512]{1,0:T(8,128)(2,1)}, bf16[192,512]{1,0:T(8,128)(2,1)S(1)}, u32[]{:S(2)}) copy-start(bf16[192,512]{1,0:T(8,128)(2,1)S(1)} %collective-permute-done.7.yu_ref) | copy-start | bytes 589828
  28.5 0.7 %copy-start.8 = (bf16[192,512]{1,0:T(8,128)(2,1)}, bf16[192,512]{1,0:T(8,128)(2,1)S(1)}, u32[]{:S(2)}) copy-start(bf16[192,512]{1,0:T(8,128)(2,1)S(1)} %collective-permute-done.8.yd_ref) | copy-start | bytes 589828
  33.4 8.3 %collective-permute-start.11 = (bf16[256,512]{1,0:T(8,128)(2,1)}, bf16[256,512]{1,0:T(8,128)(2,1)S(1)}, u32[]{:S(2)}, u32[]{:S(2)}) collective-permute-start(bf16[256,512]{1,0:T(8,128)(2,1)} %get-tuple-element.48.mine_ref), channel_id=1, source_target_pairs={{0,1},{1,2},{2,3},{3,7},{7,6},{6,5},{5,4},{4,0},{8,9},{9,10},{10,1... | collective-permute-start | bytes 786440 | tf_op jit(solution)/shard_map/ppermute | solution.py:383
  35.4 7.6 %collective-permute-start.12 = (bf16[256,512]{1,0:T(8,128)(2,1)}, bf16[256,512]{1,0:T(8,128)(2,1)S(1)}, u32[]{:S(2)}, u32[]{:S(2)}) collective-permute-start(bf16[256,512]{1,0:T(8,128)(2,1)} %get-tuple-element.48.mine_ref), channel_id=1, source_target_pairs={{1,0},{2,1},{3,2},{7,3},{6,7},{5,6},{4,5},{0,4},{9,8},{10,9},{11,1... | collective-permute-start | bytes 786440 | tf_op jit(solution)/shard_map/ppermute | solution.py:383
  35.4 0.7 %copy-start.9 = (bf16[192,512]{1,0:T(8,128)(2,1)}, bf16[192,512]{1,0:T(8,128)(2,1)S(1)}, u32[]{:S(2)}) copy-start(bf16[192,512]{1,0:T(8,128)(2,1)S(1)} %collective-permute-done.1.up_ref) | copy-start | bytes 589828
  35.5 0.7 %copy-start.10 = (bf16[192,512]{1,0:T(8,128)(2,1)}, bf16[192,512]{1,0:T(8,128)(2,1)S(1)}, u32[]{:S(2)}) copy-start(bf16[192,512]{1,0:T(8,128)(2,1)S(1)} %collective-permute-done.2.down_ref) | copy-start | bytes 589828
  39.7 11.1 %collective-permute-start.3 = (bf16[128,512]{1,0:T(8,128)(2,1)}, bf16[128,512]{1,0:T(8,128)(2,1)S(1)}, u32[]{:S(2)}, u32[]{:S(2)}) collective-permute-start(bf16[128,512]{1,0:T(8,128)(2,1)} %get-tuple-element.38.own_ref), channel_id=1, source_target_pairs={{0,1},{1,2},{2,3},{3,7},{7,6},{6,5},{5,4},{4,0},{8,9},{9,10},{10,1... | collective-permute-start | bytes 393224 | tf_op jit(solution)/shard_map/ppermute | solution.py:383
  41.7 9.0 %collective-permute-start.4 = (bf16[128,512]{1,0:T(8,128)(2,1)}, bf16[128,512]{1,0:T(8,128)(2,1)S(1)}, u32[]{:S(2)}, u32[]{:S(2)}) collective-permute-start(bf16[128,512]{1,0:T(8,128)(2,1)} %get-tuple-element.38.own_ref), channel_id=1, source_target_pairs={{1,0},{2,1},{3,2},{7,3},{6,7},{5,6},{4,5},{0,4},{9,8},{10,9},{11,1... | collective-permute-start | bytes 393224 | tf_op jit(solution)/shard_map/ppermute | solution.py:383
  41.7 1.4 %copy-start.5 = (bf16[256,512]{1,0:T(8,128)(2,1)}, bf16[256,512]{1,0:T(8,128)(2,1)S(1)}, u32[]{:S(2)}) copy-start(bf16[256,512]{1,0:T(8,128)(2,1)S(1)} %collective-permute-done.11.up_ref) | copy-start | bytes 786436
  43.1 0.7 %copy-start.6 = (bf16[256,512]{1,0:T(8,128)(2,1)}, bf16[256,512]{1,0:T(8,128)(2,1)S(1)}, u32[]{:S(2)}) copy-start(bf16[256,512]{1,0:T(8,128)(2,1)S(1)} %collective-permute-done.12.down_ref) | copy-start | bytes 786436
  48.8 8.2 %collective-permute-start.13 = (bf16[64,512]{1,0:T(8,128)(2,1)}, bf16[64,512]{1,0:T(8,128)(2,1)S(1)}, u32[]{:S(2)}, u32[]{:S(2)}) collective-permute-start(bf16[64,512]{1,0:T(8,128)(2,1)} %get-tuple-element.56), channel_id=1, source_target_pairs={{0,1},{1,2},{2,3},{3,7},{7,6},{6,5},{5,4},{4,0},{8,9},{9,10},{10,1... | collective-permute-start | bytes 196616 | tf_op jit(solution)/shard_map/ppermute | solution.py:383
  50.7 6.3 %collective-permute-start.14 = (bf16[64,512]{1,0:T(8,128)(2,1)}, bf16[64,512]{1,0:T(8,128)(2,1)S(1)}, u32[]{:S(2)}, u32[]{:S(2)}) collective-permute-start(bf16[64,512]{1,0:T(8,128)(2,1)} %get-tuple-element.57), channel_id=1, source_target_pairs={{1,0},{2,1},{3,2},{7,3},{6,7},{5,6},{4,5},{0,4},{9,8},{10,9},{11,1... | collective-permute-start | bytes 196616 | tf_op jit(solution)/shard_map/ppermute | solution.py:383
  50.7 0.7 %copy-start.11 = (bf16[128,512]{1,0:T(8,128)(2,1)}, bf16[128,512]{1,0:T(8,128)(2,1)S(1)}, u32[]{:S(2)}) copy-start(bf16[128,512]{1,0:T(8,128)(2,1)S(1)} %collective-permute-done.3.up_ref) | copy-start | bytes 393220
  50.7 0.7 %copy-start.12 = (bf16[128,512]{1,0:T(8,128)(2,1)}, bf16[128,512]{1,0:T(8,128)(2,1)S(1)}, u32[]{:S(2)}) copy-start(bf16[128,512]{1,0:T(8,128)(2,1)S(1)} %collective-permute-done.4.down_ref) | copy-start | bytes 393220
  57.0 0.6 %copy-start.3 = (bf16[64,512]{1,0:T(8,128)(2,1)}, bf16[64,512]{1,0:T(8,128)(2,1)S(1)}, u32[]{:S(2)}) copy-start(bf16[64,512]{1,0:T(8,128)(2,1)S(1)} %collective-permute-done.13.up_ref) | copy-start | bytes 196612
  57.0 0.6 %copy-start.4 = (bf16[64,512]{1,0:T(8,128)(2,1)}, bf16[64,512]{1,0:T(8,128)(2,1)S(1)}, u32[]{:S(2)}) copy-start(bf16[64,512]{1,0:T(8,128)(2,1)S(1)} %collective-permute-done.14.down_ref) | copy-start | bytes 196612
where the time goes:
time: 60.8 us; the launch traced here: 60.4 us
  Pallas kernels  30.8 us (51%)
  starting transfers between devices  15.7 us (26%)
  waiting for transfers between devices  7.57 us (12%)
  local copies, waits for them, and re-layouts  5.56 us (9%)
  between operations  0.76 us (1%)
    pallas_call x10, Pallas kernels, call(): pl.pallas_call(body, name=name, out_shape=[jax.ShapeDtypeStruct(shape, dt...  30.8 us
    ppermute x6, starting transfers between devices, swap(): lax.ppermute(up, ('section', 'slab'), ahead)  11.6 us
    ppermute x3, waiting for transfers between devices, along(): lax.ppermute(value, 'section', [(s, (s + step) % sections) for s in range...  6.17 us
    unnamed x30, local copies, waits for them, and re-layouts  5.56 us
    ppermute x3, starting transfers between devices, along(): lax.ppermute(value, 'section', [(s, (s + step) % sections) for s in range...  4.09 us
    ppermute x6, waiting for transfers between devices, swap(): lax.ppermute(down, ('section', 'slab'), behind)  1.39 us
  transfers between devices with their start and end apart: 15, of which 2 were waited for; matrix products, arithmetic and copies ran while one was open for 0% of the time, Pallas kernels for 46%

commit v1 on v0

--- a/solution.py
+++ b/solution.py
@@ -350,6 +350,7 @@
         in_specs=[in_place] * len(args),
         out_specs=[in_place] * len(outs),
         scratch_shapes=[pltpu.VMEM(shape, BF16) for shape in scratch],
+        compiler_params=pltpu.CompilerParams(vmem_limit_bytes=16 << 20),
         cost_estimate=pl.CostEstimate(flops=flops, bytes_accessed=1 << 20, transcendentals=0),
     )(*args)
 

time: 60.8 us -> 44.8 us (0.74)
  Pallas kernels: 30.8 us -> 12.9 us
  waiting for transfers between devices: 7.57 us -> 12.7 us
  local copies, waits for them, and re-layouts: 5.56 us -> 3.38 us
  starting transfers between devices: 15.7 us -> 14.9 us
    pallas_call x10, Pallas kernels: 30.8 us -> 12.9 us  [call(): pl.pallas_call(body, name=name, out_shape=[jax.ShapeDtypeStruct(shape, dt...]
    ppermute x6, waiting for transfers between devices: 1.39 us -> 6.37 us  [swap(): lax.ppermute(down, ('section', 'slab'), behind)]
    unnamed x30 -> x8, local copies, waits for them, and re-layouts: 5.56 us -> 3.38 us
    ppermute x6, starting transfers between devices: 11.6 us -> 10.5 us  [swap(): lax.ppermute(up, ('section', 'slab'), ahead)]
  transfers between devices with their start and end apart: 15 -> 15, of which waited for: 2 -> 5; matrix products, arithmetic and copies ran while one was open for 0% -> 0% of each run, Pallas kernels for 46% -> 25%
where the time goes in v1:
time: 44.8 us; the launch traced here: 44.5 us
  starting transfers between devices  14.9 us (33%)
  Pallas kernels  12.9 us (29%)
  waiting for transfers between devices  12.7 us (28%)
  local copies, waits for them, and re-layouts  3.38 us (8%)
  between operations  0.74 us (2%)
    pallas_call x10, Pallas kernels, call(): pl.pallas_call(body, name=name, out_shape=[jax.ShapeDtypeStruct(shape, dt...  12.9 us
    ppermute x6, starting transfers between devices, swap(): lax.ppermute(up, ('section', 'slab'), ahead)  10.5 us
    ppermute x6, waiting for transfers between devices, swap(): lax.ppermute(down, ('section', 'slab'), behind)  6.37 us
    ppermute x3, waiting for transfers between devices, along(): lax.ppermute(value, 'section', [(s, (s + step) % sections) for s in range...  6.17 us
    ppermute x3, starting transfers between devices, along(): lax.ppermute(value, 'section', [(s, (s + step) % sections) for s in range...  4.09 us
    unnamed x8, local copies, waits for them, and re-layouts  3.38 us
  transfers between devices with their start and end apart: 15, of which 5 were waited for; matrix products, arithmetic and copies ran while one was open for 0% of the time, Pallas kernels for 25%

profile of v1, /device:TPU:0, one launch (start us, length us, event | category | flops | bytes accessed | tf_op | source)
XLA Modules:
  0.0 44.5 jit_solution(16646738817605749848)
XLA Ops:
  0.6 3.4 %collective-permute-start.5 = (bf16[1024,128]{1,0:T(8,128)(2,1)}, bf16[1024,128]{1,0:T(8,128)(2,1)S(1)}, u32[]{:S(2)}, u32[]{:S(2)}) collective-permute-start(bf16[1024,128]{1,0:T(8,128)(2,1)} %bitcast.50), channel_id=1, source_target_pairs={{0,28},{4,0},{8,4},{12,8},{16,12},{20,16},{24,20},{28,24},{1,29},{... | collective-permute-start | bytes 786440 | tf_op jit(solution)/shard_map/ppermute | solution.py:387
  4.0 0.7 %collective-permute-start.6 = (bf16[1024,128]{1,0:T(8,128)(2,1)}, bf16[1024,128]{1,0:T(8,128)(2,1)S(1)}, u32[]{:S(2)}, u32[]{:S(2)}) collective-permute-start(bf16[1024,128]{1,0:T(8,128)(2,1)} %bitcast.51), channel_id=1, source_target_pairs={{0,28},{4,0},{8,4},{12,8},{16,12},{20,16},{24,20},{28,24},{1,29},{... | collective-permute-start | bytes 786440 | tf_op jit(solution)/shard_map/ppermute | solution.py:387
  4.7 0.0 collective-permute-start
  4.7 6.2 %collective-permute-done.5.got_ref = bf16[1024,128]{1,0:T(8,128)(2,1)S(1)} collective-permute-done((bf16[1024,128]{1,0:T(8,128)(2,1)}, bf16[1024,128]{1,0:T(8,128)(2,1)S(1)}, u32[]{:S(2)}, u32[]{:S(2)}) %collective-permute-start.5) | collective-permute-done | bytes 262176 | tf_op jit(solution)/shard_map/ppermute | solution.py:387
  10.9 0.0 copy-start.1
  10.9 0.9 %copy-done.1 = bf16[128,2,512]{2,1,0:T(2,128)(2,1)S(1)} copy-done((bf16[128,2,512]{2,1,0:T(2,128)(2,1)S(1)}, bf16[128,2,512]{2,1,0:T(2,128)(2,1)}, u32[]{:S(2)}) %copy-start.1) | copy-done | bytes 262168
  11.8 0.0 copy-start.3
  11.8 0.3 unpack_y.1
  12.1 1.6 %collective-permute-start.7 = (bf16[192,512]{1,0:T(8,128)(2,1)S(1)}, bf16[192,512]{1,0:T(8,128)(2,1)S(1)}, u32[]{:S(2)}, u32[]{:S(2)}) collective-permute-start(bf16[192,512]{1,0:T(8,128)(2,1)S(1)} %get-tuple-element.43), channel_id=1, source_target_pairs={{0,1},{1,2},{2,3},{3,7},{7,6},{6,5},{5,4},{4,0},{8,9},{9,10},{10,1... | collective-permute-start | bytes 589832 | tf_op jit(solution)/shard_map/ppermute | solution.py:384
  13.7 0.0 collective-permute-start.8
  13.7 0.0 collective-permute-done.6.got_ref
  13.7 0.0 copy-start.2
  13.7 0.9 %copy-done.2 = bf16[128,2,512]{2,1,0:T(2,128)(2,1)S(1)} copy-done((bf16[128,2,512]{2,1,0:T(2,128)(2,1)S(1)}, bf16[128,2,512]{2,1,0:T(2,128)(2,1)}, u32[]{:S(2)}) %copy-start.2) | copy-done | bytes 262168
  14.7 0.3 unpack_g.1
  14.9 0.2 collective-permute-start.10
  15.2 1.8 %collective-permute-start.9 = (bf16[64,512]{1,0:T(8,128)(2,1)S(1)}, bf16[64,512]{1,0:T(8,128)(2,1)S(1)}, u32[]{:S(2)}, u32[]{:S(2)}) collective-permute-start(bf16[64,512]{1,0:T(8,128)(2,1)S(1)} %get-tuple-element.45), channel_id=1, source_target_pairs={{0,1},{1,2},{2,3},{3,7},{7,6},{6,5},{5,4},{4,0},{8,9},{9,10},{10,1... | collective-permute-start | bytes 196616 | tf_op jit(solution)/shard_map/ppermute | solution.py:384
  17.0 0.0 copy-start
  17.0 1.5 %copy-done = bf16[1,4,27,64,64]{4,3,2,1,0:T(8,128)(2,1)S(1)} copy-done((bf16[1,4,27,64,64]{4,3,2,1,0:T(8,128)(2,1)S(1)}, bf16[1,4,27,64,64]{4,3,2,1,0:T(8,128)(2,1)}, u32[]{:S(2)}) %copy-start) | copy-done | bytes 884760
  18.5 1.1 %prepare.1 = (bf16[192,576]{1,0:T(8,128)(2,1)S(1)}, bf16[192,576]{1,0:T(8,128)(2,1)S(1)}, bf16[192,576]{1,0:T(8,128)(2,1)S(1)}, bf16[192,576]{1,0:T(8,128)(2,1)S...) custom-call(bf16[1,4,27,64,64]{4,3,2,1,0:T(8,128)(2,1)S(1)} %copy-done), custom_call_target="tpu_custom_call" | custom-call | flops 113246208 | bytes 1048576 | tf_op jit(solution)/shard_map/prepare/pallas_call | solution.py:346
  19.6 0.0 collective-permute-done.got_ref
  19.6 0.0 copy-done.3
  19.6 0.3 unpack_x.1
  19.9 2.0 %collective-permute-start.1 = (bf16[192,512]{1,0:T(8,128)(2,1)S(1)}, bf16[192,512]{1,0:T(8,128)(2,1)S(1)}, u32[]{:S(2)}, u32[]{:S(2)}) collective-permute-start(bf16[192,512]{1,0:T(8,128)(2,1)S(1)} %get-tuple-element.33), channel_id=1, source_target_pairs={{0,1},{1,2},{2,3},{3,7},{7,6},{6,5},{5,4},{4,0},{8,9},{9,10},{10,1... | collective-permute-start | bytes 589832 | tf_op jit(solution)/shard_map/ppermute | solution.py:384
  21.9 0.0 collective-permute-done.10.gd_ref
  21.9 0.0 collective-permute-start.2
  21.9 0.0 collective-permute-done.9.gu_ref
  21.9 0.0 collective-permute-done.7.yu_ref
  21.9 0.0 collective-permute-done.8.yd_ref
  22.0 2.0 %backward_first.1 = (bf16[256,512]{1,0:T(8,128)(2,1)S(1)}, bf16[256,512]{1,0:T(8,128)(2,1)S(1)}, bf16[256,512]{1,0:T(8,128)(2,1)S(1)}, f32[128,512]{1,0:T(8,128)S(1)}) custom-call(bf16[256,512]{1,0:T(8,128)(2,1)S(1)} %get-tuple-element.41.y_ref, bf16[256,512]{1,0:T(8,128)(2,1)S(1)} %get-tuple-element.42.g_ref, ...), custom_call_target="tpu_custom_call" | custom-call | flops 905969664 | bytes 1048576 | tf_op jit(solution)/shard_map/backward_first/pallas_call | solution.py:346
  24.0 2.0 %collective-permute-start.11 = (bf16[256,512]{1,0:T(8,128)(2,1)S(1)}, bf16[256,512]{1,0:T(8,128)(2,1)S(1)}, u32[]{:S(2)}, u32[]{:S(2)}) collective-permute-start(bf16[256,512]{1,0:T(8,128)(2,1)S(1)} %get-tuple-element.48.mine_ref), channel_id=1, source_target_pairs={{0,1},{1,2},{2,3},{3,7},{7,6},{6,5},{5,4},{4,0},{8,9},{9,10},{10,1... | collective-permute-start | bytes 786440 | tf_op jit(solution)/shard_map/ppermute | solution.py:384
  26.0 0.0 collective-permute-start.12
  26.0 0.2 collective-permute-done.1.up_ref
  26.1 3.5 %collective-permute-done.2.down_ref = bf16[192,512]{1,0:T(8,128)(2,1)S(1)} collective-permute-done((bf16[192,512]{1,0:T(8,128)(2,1)S(1)}, bf16[192,512]{1,0:T(8,128)(2,1)S(1)}, u32[]{:S(2)}, u32[]{:S(2)}) %collective-permute-start.2) | collective-permute-done | bytes 196640 | tf_op jit(solution)/shard_map/ppermute | solution.py:384
  29.6 1.5 %forward_first.1 = (bf16[256,512]{1,0:T(8,128)(2,1)S(1)}, bf16[128,512]{1,0:T(8,128)(2,1)S(1)}) custom-call(bf16[256,512]{1,0:T(8,128)(2,1)S(1)} %get-tuple-element.32.own_ref, bf16[192,512]{1,0:T(8,128)(2,1)S(1)} %collective-permute-done.1.up_ref, bf16[192,512]{1,0:T(8,128)(2,1)S(1)} %collective-permute-done.2.down_ref, ...), custom_call_target="tpu_custom_call" | custom-call | flops 679477248 | bytes 1048576 | tf_op jit(solution)/shard_map/forward_first/pallas_call | solution.py:346
  31.2 1.5 %collective-permute-start.3 = (bf16[128,512]{1,0:T(8,128)(2,1)S(1)}, bf16[128,512]{1,0:T(8,128)(2,1)S(1)}, u32[]{:S(2)}, u32[]{:S(2)}) collective-permute-start(bf16[128,512]{1,0:T(8,128)(2,1)S(1)} %get-tuple-element.38.own_ref), channel_id=1, source_target_pairs={{0,1},{1,2},{2,3},{3,7},{7,6},{6,5},{5,4},{4,0},{8,9},{9,10},{10,1... | collective-permute-start | bytes 393224 | tf_op jit(solution)/shard_map/ppermute | solution.py:384
  32.6 0.0 collective-permute-start.4
  32.6 0.0 collective-permute-done.11.up_ref
  32.6 2.0 %collective-permute-done.12.down_ref = bf16[256,512]{1,0:T(8,128)(2,1)S(1)} collective-permute-done((bf16[256,512]{1,0:T(8,128)(2,1)S(1)}, bf16[256,512]{1,0:T(8,128)(2,1)S(1)}, u32[]{:S(2)}, u32[]{:S(2)}) %collective-permute-start.12) | collective-permute-done | bytes 262176 | tf_op jit(solution)/shard_map/ppermute | solution.py:384
  34.6 2.5 %backward_second.1 = (bf16[256,512]{1,0:T(8,128)(2,1)S(1)}, bf16[128,512]{1,0:T(8,128)(2,1)S(1)}, f32[128,512]{1,0:T(8,128)S(1)}, bf16[128,512]{1,0:T(8,128)(2,1...) custom-call(bf16[256,512]{1,0:T(8,128)(2,1)S(1)} %get-tuple-element.48.mine_ref, ...), custom_call_target="tpu_custom_call" | custom-call | flops 1358954496 | bytes 1048576 | tf_op jit(solution)/shard_map/backward_second/pallas_call | solution.py:346
  37.1 1.6 %collective-permute-start.13 = (bf16[64,512]{1,0:T(8,128)(2,1)S(1)}, bf16[64,512]{1,0:T(8,128)(2,1)S(1)}, u32[]{:S(2)}, u32[]{:S(2)}) collective-permute-start(bf16[64,512]{1,0:T(8,128)(2,1)S(1)} %get-tuple-element.56), channel_id=1, source_target_pairs={{0,1},{1,2},{2,3},{3,7},{7,6},{6,5},{5,4},{4,0},{8,9},{9,10},{10,1... | collective-permute-start | bytes 196616 | tf_op jit(solution)/shard_map/ppermute | solution.py:384
  38.7 0.0 collective-permute-start.14
  38.7 0.0 collective-permute-done.3.up_ref
  38.7 0.0 collective-permute-done.4.down_ref
  38.7 2.4 %forward_second.1 = bf16[1024,128]{1,0:T(8,128)(2,1)} custom-call(bf16[256,512]{1,0:T(8,128)(2,1)S(1)} %get-tuple-element.37.mid_ref, bf16[128,512]{1,0:T(8,128)(2,1)S(1)} %get-tuple-element.38.own_ref, bf16[128,512]{1,0:T(8,128)(2,1)S(1)} %collective-permute-done.3.up_ref, bf16[128,512]{1,0:T(8,128)(2,1)S(1)} %collective-permute-done.4.down_ref, ...), custom_call_target="tpu_custom_call" | custom-call | flops 679477248 | bytes 1048576 | tf_op jit(solution)/shard_map/forward_second/pallas_call | solution.py:346
  41.1 0.9 %pack_state.1 = bf16[1024,128]{1,0:T(8,128)(2,1)} custom-call(bf16[256,512]{1,0:T(8,128)(2,1)S(1)} %get-tuple-element.54.state_ref), custom_call_target="tpu_custom_call" | custom-call | flops 113246208 | bytes 1048576 | tf_op jit(solution)/shard_map/pack_state/pallas_call | solution.py:346
  42.1 0.0 collective-permute-done.13.up_ref
  42.1 0.9 %collective-permute-done.14.down_ref = bf16[64,512]{1,0:T(8,128)(2,1)S(1)} collective-permute-done((bf16[64,512]{1,0:T(8,128)(2,1)S(1)}, bf16[64,512]{1,0:T(8,128)(2,1)S(1)}, u32[]{:S(2)}, u32[]{:S(2)}) %collective-permute-start.14) | collective-permute-done | bytes 65568 | tf_op jit(solution)/shard_map/ppermute | solution.py:384
  43.0 1.6 %backward_third.1 = bf16[1024,128]{1,0:T(8,128)(2,1)} custom-call(bf16[128,512]{1,0:T(8,128)(2,1)S(1)} %get-tuple-element.55.inner_ref, bf16[64,512]{1,0:T(8,128)(2,1)S(1)} %collective-permute-done.13.up_ref, bf16[64,512]{1,0:T(8,128)(2,1)S(1)} %collective-permute-done.14.down_ref, f32[128,512]{1,0:T(8,128)S(1)} %get-tuple-element.58.low_ref, ...), custom_call_target="tpu_custom_call" | custom-call | flops 226492416 | bytes 1048576 | tf_op jit(solution)/shard_map/backward_third/pallas_call | solution.py:346
Async XLA Ops:
  0.6 10.3 %collective-permute-start.5 = (bf16[1024,128]{1,0:T(8,128)(2,1)}, bf16[1024,128]{1,0:T(8,128)(2,1)S(1)}, u32[]{:S(2)}, u32[]{:S(2)}) collective-permute-start(bf16[1024,128]{1,0:T(8,128)(2,1)} %bitcast.50), channel_id=1, source_target_pairs={{0,28},{4,0},{8,4},{12,8},{16,12},{20,16},{24,20},{28,24},{1,29},{... | collective-permute-start | bytes 786440 | tf_op jit(solution)/shard_map/ppermute | solution.py:387
  4.0 9.7 %collective-permute-start.6 = (bf16[1024,128]{1,0:T(8,128)(2,1)}, bf16[1024,128]{1,0:T(8,128)(2,1)S(1)}, u32[]{:S(2)}, u32[]{:S(2)}) collective-permute-start(bf16[1024,128]{1,0:T(8,128)(2,1)} %bitcast.51), channel_id=1, source_target_pairs={{0,28},{4,0},{8,4},{12,8},{16,12},{20,16},{24,20},{28,24},{1,29},{... | collective-permute-start | bytes 786440 | tf_op jit(solution)/shard_map/ppermute | solution.py:387
  4.7 14.9 %collective-permute-start = (bf16[1024,128]{1,0:T(8,128)(2,1)}, bf16[1024,128]{1,0:T(8,128)(2,1)S(1)}, u32[]{:S(2)}, u32[]{:S(2)}) collective-permute-start(bf16[1024,128]{1,0:T(8,128)(2,1)} %bitcast.52), channel_id=1, source_target_pairs={{0,4},{4,8},{8,12},{12,16},{16,20},{20,24},{24,28},{28,0},{1,5},{5... | collective-permute-start | bytes 786440 | tf_op jit(solution)/shard_map/ppermute | solution.py:387
  10.9 0.9 %copy-start.1 = (bf16[128,2,512]{2,1,0:T(2,128)(2,1)S(1)}, bf16[128,2,512]{2,1,0:T(2,128)(2,1)}, u32[]{:S(2)}) copy-start(bf16[128,2,512]{2,1,0:T(2,128)(2,1)} %param.11) | copy-start | bytes 786436
  11.8 7.8 %copy-start.3 = (bf16[128,2,512]{2,1,0:T(2,128)(2,1)S(1)}, bf16[128,2,512]{2,1,0:T(2,128)(2,1)}, u32[]{:S(2)}) copy-start(bf16[128,2,512]{2,1,0:T(2,128)(2,1)} %param.10) | copy-start | bytes 786436
  12.1 9.8 %collective-permute-start.7 = (bf16[192,512]{1,0:T(8,128)(2,1)S(1)}, bf16[192,512]{1,0:T(8,128)(2,1)S(1)}, u32[]{:S(2)}, u32[]{:S(2)}) collective-permute-start(bf16[192,512]{1,0:T(8,128)(2,1)S(1)} %get-tuple-element.43), channel_id=1, source_target_pairs={{0,1},{1,2},{2,3},{3,7},{7,6},{6,5},{5,4},{4,0},{8,9},{9,10},{10,1... | collective-permute-start | bytes 589832 | tf_op jit(solution)/shard_map/ppermute | solution.py:384
  13.7 8.2 %collective-permute-start.8 = (bf16[192,512]{1,0:T(8,128)(2,1)S(1)}, bf16[192,512]{1,0:T(8,128)(2,1)S(1)}, u32[]{:S(2)}, u32[]{:S(2)}) collective-permute-start(bf16[192,512]{1,0:T(8,128)(2,1)S(1)} %get-tuple-element.44), channel_id=1, source_target_pairs={{1,0},{2,1},{3,2},{7,3},{6,7},{5,6},{4,5},{0,4},{9,8},{10,9},{11,1... | collective-permute-start | bytes 589832 | tf_op jit(solution)/shard_map/ppermute | solution.py:384
  13.7 1.0 %copy-start.2 = (bf16[128,2,512]{2,1,0:T(2,128)(2,1)S(1)}, bf16[128,2,512]{2,1,0:T(2,128)(2,1)}, u32[]{:S(2)}) copy-start(bf16[128,2,512]{2,1,0:T(2,128)(2,1)} %param.12) | copy-start | bytes 786436
  14.9 7.0 %collective-permute-start.10 = (bf16[64,512]{1,0:T(8,128)(2,1)S(1)}, bf16[64,512]{1,0:T(8,128)(2,1)S(1)}, u32[]{:S(2)}, u32[]{:S(2)}) collective-permute-start(bf16[64,512]{1,0:T(8,128)(2,1)S(1)} %get-tuple-element.46), channel_id=1, source_target_pairs={{1,0},{2,1},{3,2},{7,3},{6,7},{5,6},{4,5},{0,4},{9,8},{10,9},{11,1... | collective-permute-start | bytes 196616 | tf_op jit(solution)/shard_map/ppermute | solution.py:384
  15.2 6.7 %collective-permute-start.9 = (bf16[64,512]{1,0:T(8,128)(2,1)S(1)}, bf16[64,512]{1,0:T(8,128)(2,1)S(1)}, u32[]{:S(2)}, u32[]{:S(2)}) collective-permute-start(bf16[64,512]{1,0:T(8,128)(2,1)S(1)} %get-tuple-element.45), channel_id=1, source_target_pairs={{0,1},{1,2},{2,3},{3,7},{7,6},{6,5},{5,4},{4,0},{8,9},{9,10},{10,1... | collective-permute-start | bytes 196616 | tf_op jit(solution)/shard_map/ppermute | solution.py:384
  17.0 1.5 %copy-start = (bf16[1,4,27,64,64]{4,3,2,1,0:T(8,128)(2,1)S(1)}, bf16[1,4,27,64,64]{4,3,2,1,0:T(8,128)(2,1)}, u32[]{:S(2)}) copy-start(bf16[1,4,27,64,64]{4,3,2,1,0:T(8,128)(2,1)} %kernels_ref.1) | copy-start | bytes 2654212
  19.9 6.2 %collective-permute-start.1 = (bf16[192,512]{1,0:T(8,128)(2,1)S(1)}, bf16[192,512]{1,0:T(8,128)(2,1)S(1)}, u32[]{:S(2)}, u32[]{:S(2)}) collective-permute-start(bf16[192,512]{1,0:T(8,128)(2,1)S(1)} %get-tuple-element.33), channel_id=1, source_target_pairs={{0,1},{1,2},{2,3},{3,7},{7,6},{6,5},{5,4},{4,0},{8,9},{9,10},{10,1... | collective-permute-start | bytes 589832 | tf_op jit(solution)/shard_map/ppermute | solution.py:384
  21.9 7.7 %collective-permute-start.2 = (bf16[192,512]{1,0:T(8,128)(2,1)S(1)}, bf16[192,512]{1,0:T(8,128)(2,1)S(1)}, u32[]{:S(2)}, u32[]{:S(2)}) collective-permute-start(bf16[192,512]{1,0:T(8,128)(2,1)S(1)} %get-tuple-element.34), channel_id=1, source_target_pairs={{1,0},{2,1},{3,2},{7,3},{6,7},{5,6},{4,5},{0,4},{9,8},{10,9},{11,1... | collective-permute-start | bytes 589832 | tf_op jit(solution)/shard_map/ppermute | solution.py:384
  24.0 8.7 %collective-permute-start.11 = (bf16[256,512]{1,0:T(8,128)(2,1)S(1)}, bf16[256,512]{1,0:T(8,128)(2,1)S(1)}, u32[]{:S(2)}, u32[]{:S(2)}) collective-permute-start(bf16[256,512]{1,0:T(8,128)(2,1)S(1)} %get-tuple-element.48.mine_ref), channel_id=1, source_target_pairs={{0,1},{1,2},{2,3},{3,7},{7,6},{6,5},{5,4},{4,0},{8,9},{9,10},{10,1... | collective-permute-start | bytes 786440 | tf_op jit(solution)/shard_map/ppermute | solution.py:384
  26.0 8.6 %collective-permute-start.12 = (bf16[256,512]{1,0:T(8,128)(2,1)S(1)}, bf16[256,512]{1,0:T(8,128)(2,1)S(1)}, u32[]{:S(2)}, u32[]{:S(2)}) collective-permute-start(bf16[256,512]{1,0:T(8,128)(2,1)S(1)} %get-tuple-element.48.mine_ref), channel_id=1, source_target_pairs={{1,0},{2,1},{3,2},{7,3},{6,7},{5,6},{4,5},{0,4},{9,8},{10,9},{11,1... | collective-permute-start | bytes 786440 | tf_op jit(solution)/shard_map/ppermute | solution.py:384
  31.2 7.5 %collective-permute-start.3 = (bf16[128,512]{1,0:T(8,128)(2,1)S(1)}, bf16[128,512]{1,0:T(8,128)(2,1)S(1)}, u32[]{:S(2)}, u32[]{:S(2)}) collective-permute-start(bf16[128,512]{1,0:T(8,128)(2,1)S(1)} %get-tuple-element.38.own_ref), channel_id=1, source_target_pairs={{0,1},{1,2},{2,3},{3,7},{7,6},{6,5},{5,4},{4,0},{8,9},{9,10},{10,1... | collective-permute-start | bytes 393224 | tf_op jit(solution)/shard_map/ppermute | solution.py:384
  32.6 6.1 %collective-permute-start.4 = (bf16[128,512]{1,0:T(8,128)(2,1)S(1)}, bf16[128,512]{1,0:T(8,128)(2,1)S(1)}, u32[]{:S(2)}, u32[]{:S(2)}) collective-permute-start(bf16[128,512]{1,0:T(8,128)(2,1)S(1)} %get-tuple-element.38.own_ref), channel_id=1, source_target_pairs={{1,0},{2,1},{3,2},{7,3},{6,7},{5,6},{4,5},{0,4},{9,8},{10,9},{11,1... | collective-permute-start | bytes 393224 | tf_op jit(solution)/shard_map/ppermute | solution.py:384
  37.1 5.0 %collective-permute-start.13 = (bf16[64,512]{1,0:T(8,128)(2,1)S(1)}, bf16[64,512]{1,0:T(8,128)(2,1)S(1)}, u32[]{:S(2)}, u32[]{:S(2)}) collective-permute-start(bf16[64,512]{1,0:T(8,128)(2,1)S(1)} %get-tuple-element.56), channel_id=1, source_target_pairs={{0,1},{1,2},{2,3},{3,7},{7,6},{6,5},{5,4},{4,0},{8,9},{9,10},{10,1... | collective-permute-start | bytes 196616 | tf_op jit(solution)/shard_map/ppermute | solution.py:384
  38.7 4.3 %collective-permute-start.14 = (bf16[64,512]{1,0:T(8,128)(2,1)S(1)}, bf16[64,512]{1,0:T(8,128)(2,1)S(1)}, u32[]{:S(2)}, u32[]{:S(2)}) collective-permute-start(bf16[64,512]{1,0:T(8,128)(2,1)S(1)} %get-tuple-element.57), channel_id=1, source_target_pairs={{1,0},{2,1},{3,2},{7,3},{6,7},{5,6},{4,5},{0,4},{9,8},{10,9},{11,1... | collective-permute-start | bytes 196616 | tf_op jit(solution)/shard_map/ppermute | solution.py:384

commit v2 on v1

--- a/solution.py
+++ b/solution.py
@@ -7,6 +7,7 @@
 from jax.experimental.pallas import tpu as pltpu
 from jax.sharding import PartitionSpec as P
 
+
 WID = 32
 PAIRS = 2
 LANES = 128
@@ -35,8 +36,12 @@
     return jnp.where(jnp.full(value.shape, flag), value, jnp.zeros((), value.dtype))
 
 
-def prepare(kernels_ref, *out_refs):
+def prepare(planes, cells, kernels_ref, *refs):
     count = 2 * PAIRS
+    out_refs, (split_ref, join_ref) = refs[: 2 * count], refs[2 * count :]
+    tiles, chans = chunk_sizes(planes, cells)
+    split_ref[...] = shuffle(tiles, planes, chans, False)
+    join_ref[...] = shuffle(tiles, planes, chans, True)
     taps, half = kernels_ref.shape[2], kernels_ref.shape[3]
     row = lax.broadcasted_iota(jnp.int32, (half, half), 0)
     col = lax.broadcasted_iota(jnp.int32, (half, half), 1)
@@ -47,11 +52,15 @@
             lax.dot_general(unit, m, (((1,), (1,)), ((), ())), preferred_element_type=F32).astype(BF16)
             for m in mine
         ]
+        blank = jnp.zeros((half, 3 * half), BF16)
         for b in range(3):
-            pieces = [mine[9 * a + 3 * b + c] for a in range(3) for c in range(3)]
-            out_refs[q][b * half : (b + 1) * half, :] = jnp.concatenate(pieces, axis=1)
-            pieces = [turned[26 - (9 * a + 3 * b + c)] for a in range(3) for c in range(3)]
-            out_refs[count + q][b * half : (b + 1) * half, :] = jnp.concatenate(pieces, axis=1)
+            for kind, pieces in (
+                (0, [mine[9 * a + 3 * b + c] for a in range(3) for c in range(3)]),
+                (count, [turned[26 - (9 * a + 3 * b + c)] for a in range(3) for c in range(3)]),
+            ):
+                line = jnp.concatenate(pieces, axis=1)
+                for j, parts in ((0, [line, blank]), (1, [blank, line])):
+                    out_refs[kind + q][(3 * j + b) * half : (3 * j + b + 1) * half, :] = jnp.concatenate(parts, axis=1)
 
 
 def shuffle(tiles, planes, chans, back):
@@ -68,10 +77,9 @@
     return tiles, 256 // (tiles * planes)
 
 
-def split_planes(raw, half, planes, cells):
+def split_planes(raw, matrix, half, planes, cells):
     tiles, chans = chunk_sizes(planes, cells)
     rows = tiles * planes * chans
-    matrix = shuffle(tiles, planes, chans, False)
     chunks = raw.shape[0] // rows
     parts = {}
     for g in range(0, chunks, 2):
@@ -92,11 +100,10 @@
     ]
 
 
-def join_planes(values, out_ref, base):
+def join_planes(values, matrix, out_ref, base):
     planes, (half, cells) = len(values), values[0].shape
     tiles, chans = chunk_sizes(planes, cells)
     rows = tiles * planes * chans
-    matrix = shuffle(tiles, planes, chans, True)
     for g in range(0, half // chans, 2):
         sides = []
         for i in range(2):
@@ -130,14 +137,23 @@
 
 
 def conv(stack_ref, slot, weight_ref):
-    half = weight_ref.shape[0] // 3
+    half = weight_ref.shape[0] // 6
     cells = stack_ref.shape[1]
     begin = (slot - 1) * 3 * half
-    total = dot(weight_ref[...], stack_ref[begin : begin + 9 * half, :])
+    total = dot(weight_ref[...], stack_ref[begin : begin + 12 * half, :])
     cell = lax.broadcasted_iota(jnp.int32, (half, cells), 1)
-    above = jnp.where(cell >= WID, pltpu.roll(total[:half], WID, 1), 0.0)
-    below = jnp.where(cell < cells - WID, pltpu.roll(total[2 * half :], cells - WID, 1), 0.0)
-    return above + total[half : 2 * half] + below
+    results = []
+    for j in range(2):
+        rows = [total[(3 * j + b) * half : (3 * j + b + 1) * half] for b in range(3)]
+        above = jnp.where(cell >= WID, pltpu.roll(rows[0], WID, 1), 0.0)
+        below = jnp.where(cell < cells - WID, pltpu.roll(rows[2], cells - WID, 1), 0.0)
+        results.append(above + rows[1] + below)
+    return results
+
+
+def convs(stack_ref, slot, count, weight_ref):
+    for j in range(0, count, 2):
+        yield from conv(stack_ref, slot + j, weight_ref)
 
 
 def sigmoid(z):
@@ -148,12 +164,12 @@
     return ref[index * half : (index + 1) * half, :]
 
 
-def unpack_state(edge, wide_half, half, planes, cells, got_ref, edge_ref, own_ref, up_ref, down_ref):
+def unpack_state(edge, wide_half, half, planes, cells, got_ref, edge_ref, matrix_ref, own_ref, up_ref, down_ref):
     at = lax.axis_index("section")
     last = lax.axis_size("section") - 1
     at_edge = at == (last if edge else 0)
     raw = pick(at_edge, edge_ref[...], got_ref[...])
-    parts = split_planes(raw, half, planes, cells)
+    parts = split_planes(raw, matrix_ref[...], half, planes, cells)
     for h in range(2):
         for p in range(planes):
             own_ref[(h * planes + p) * half : (h * planes + p + 1) * half, :] = parts[h][p]
@@ -169,16 +185,18 @@
     down_ref[base : base + half, :] = pick(odd, other[planes - 1], other[0])
 
 
-def unpack_grad(half, planes, cells, got_ref, edge_ref, own_ref, up_ref, down_ref):
+def unpack_grad(part, half, planes, cells, got_ref, edge_ref, matrix_ref, own_ref, *send_refs):
     at_edge = lax.axis_index("section") == lax.axis_size("section") - 1
-    raw = pick(at_edge, edge_ref[...], got_ref[...])
-    parts = split_planes(raw, half, planes, cells)
-    for h in range(2):
-        for p in range(planes):
-            own_ref[(h * planes + p) * half : (h * planes + p + 1) * half, :] = parts[h][p]
-    odd = is_odd()
-    up_ref[...] = pick(odd, parts[1][0], parts[1][planes - 1])
-    down_ref[...] = pick(odd, parts[1][planes - 1], parts[1][0])
+    rows = got_ref.shape[0]
+    raw = pick(at_edge, edge_ref[part * rows : (part + 1) * rows, :], got_ref[...])
+    (parts,) = split_planes(raw, matrix_ref[...], half, planes, cells)
+    for p in range(planes):
+        own_ref[p * half : (p + 1) * half, :] = parts[p]
+    if send_refs:
+        up_ref, down_ref = send_refs
+        odd = is_odd()
+        up_ref[...] = pick(odd, parts[0], parts[planes - 1])
+        down_ref[...] = pick(odd, parts[planes - 1], parts[0])
 
 
 def halos(up_ref, down_ref, index, half):
@@ -199,8 +217,7 @@
         lay(s0, planes + p, rows_of(own_ref, planes + p, half))
     low, high = halos(up_ref, down_ref, planes, half)
     firsts = [low] + [rows_of(own_ref, p, half) for p in range(planes)] + [high]
-    for j in range(planes + 2):
-        z = conv(s0, planes - 1 + j, f_ref)
+    for j, z in enumerate(convs(s0, planes - 1, planes + 2, f_ref)):
         y = (firsts[j].astype(F32) + z * sigmoid(z)).astype(BF16)
         if j == 0:
             y = keep(has_low, y)
@@ -208,13 +225,12 @@
             y = keep(has_high, y)
         mid_ref[j * half : (j + 1) * half, :] = y
         lay(s1, j, y)
-    for p in range(planes):
-        z = conv(s1, 1 + p, g_ref)
+    for p, z in enumerate(convs(s1, 1, planes, g_ref)):
         y = (rows_of(own_ref, planes + p, half).astype(F32) + z * sigmoid(z)).astype(BF16)
         send_ref[p * half : (p + 1) * half, :] = y
 
 
-def forward_second(half, planes, mid_ref, own_ref, up_ref, down_ref, f_ref, g_ref, out_ref, s0, s1):
+def forward_second(half, planes, mid_ref, own_ref, up_ref, down_ref, f_ref, g_ref, join_ref, out_ref, s0, s1):
     has_low, has_high = slab_place()
     for p in range(planes):
         low, high = halos(up_ref, down_ref, p, half)
@@ -222,8 +238,7 @@
         lay(s0, 2 * planes + p, high)
         lay(s0, planes + p, rows_of(own_ref, p, half))
     tops = []
-    for j in range(planes + 2):
-        z = conv(s0, planes - 1 + j, f_ref)
+    for j, z in enumerate(convs(s0, planes - 1, planes + 2, f_ref)):
         y = (rows_of(mid_ref, j, half).astype(F32) + z * sigmoid(z)).astype(BF16)
         if j == 0:
             y = keep(has_low, y)
@@ -233,11 +248,10 @@
             tops.append(y)
         lay(s1, j, y)
     bottoms = []
-    for p in range(planes):
-        z = conv(s1, 1 + p, g_ref)
+    for p, z in enumerate(convs(s1, 1, planes, g_ref)):
         bottoms.append((rows_of(own_ref, p, half).astype(F32) + z * sigmoid(z)).astype(BF16))
-    join_planes(tops, out_ref, 0)
-    join_planes(bottoms, out_ref, out_ref.shape[0] // 2)
+    join_planes(tops, join_ref[...], out_ref, 0)
+    join_planes(bottoms, join_ref[...], out_ref, out_ref.shape[0] // 2)
 
 
 def turn(z, low_value, grad):
@@ -248,7 +262,7 @@
 
 
 def backward_first(
-    half, planes, y_ref, g_ref, yu_ref, yd_ref, gu_ref, gd_ref, wg_ref, wf_ref, tg_ref,
+    half, planes, y_ref, g1_ref, g2_ref, yu_ref, yd_ref, gu_ref, gd_ref, wg_ref, wf_ref, tg_ref,
     send_ref, second_ref, low_grad_ref, carry_ref, s0, s1, s2,
 ):
     has_low, has_high = slab_place()
@@ -260,9 +274,8 @@
     low, high = halos(yu_ref, yd_ref, planes, half)
     lowers = [low] + [rows_of(y_ref, planes + p, half) for p in range(planes)] + [high]
     low, high = halos(gu_ref, gd_ref, 0, half)
-    grads = [low] + [rows_of(g_ref, planes + p, half) for p in range(planes)] + [high]
-    for j in range(planes + 2):
-        z = conv(s0, planes - 1 + j, wg_ref)
+    grads = [low] + [rows_of(g2_ref, p, half) for p in range(planes)] + [high]
+    for j, z in enumerate(convs(s0, planes - 1, planes + 2, wg_ref)):
         second, inner = turn(z, lowers[j], grads[j].astype(F32))
         if j == 0:
             second, inner = keep(has_low, second), keep(has_low, inner)
@@ -272,9 +285,8 @@
         low_grad_ref[j * half : (j + 1) * half, :] = grads[j]
         lay(s1, j, second)
         lay(s2, j, inner)
-    for p in range(planes):
-        z = conv(s1, 1 + p, wf_ref)
-        carry = rows_of(g_ref, p, half).astype(F32) + conv(s2, 1 + p, tg_ref)
+    for p, (z, term) in enumerate(zip(convs(s1, 1, planes, wf_ref), convs(s2, 1, planes, tg_ref))):
+        carry = rows_of(g1_ref, p, half).astype(F32) + term
         first, inner = turn(z, rows_of(y_ref, p, half), carry)
         carry_ref[p * half : (p + 1) * half, :] = carry
         send_ref[p * half : (p + 1) * half, :] = first
@@ -297,9 +309,9 @@
         lay(s2, p, low)
         lay(s2, 2 * planes + p, high)
         lay(s2, planes + p, rows_of(mine_ref, planes + p, half))
-    for j in range(planes + 2):
-        grad = rows_of(low_grad_ref, j, half).astype(F32) + conv(s2, planes - 1 + j, tf_ref)
-        z = conv(s0, planes - 1 + j, wg_ref)
+    wide = (planes - 1, planes + 2)
+    for j, (term, z) in enumerate(zip(convs(s2, *wide, tf_ref), convs(s0, *wide, wg_ref))):
+        grad = rows_of(low_grad_ref, j, half).astype(F32) + term
         second, inner = turn(z, rows_of(second_ref, j, half), grad)
         if j == 0:
             second, inner = keep(has_low, second), keep(has_low, inner)
@@ -311,9 +323,8 @@
         lay(s1, j, second)
         lay(s3, j, inner)
     inners = []
-    for p in range(planes):
-        z = conv(s1, 1 + p, wf_ref)
-        carry = rows_of(carry_ref, p, half) + conv(s3, 1 + p, tg_ref)
+    for p, (z, term) in enumerate(zip(convs(s1, 1, planes, wf_ref), convs(s3, 1, planes, tg_ref))):
+        carry = rows_of(carry_ref, p, half) + term
         first, inner = turn(z, rows_of(mine_ref, p, half), carry)
         state_ref[p * half : (p + 1) * half, :] = first
         top_ref[p * half : (p + 1) * half, :] = carry.astype(BF16)
@@ -323,33 +334,48 @@
     out_down_ref[...] = pick(odd, inners[planes - 1], inners[0])
 
 
-def backward_third(half, planes, inner_ref, up_ref, down_ref, low_ref, top_ref, tf_ref, out_ref, s0):
+def backward_third(
+    half, planes, inner_ref, up_ref, down_ref, low_ref, top_ref, tf_ref, join_ref, fwd_ref, state_ref,
+    fwd_hbm, state_hbm, grad_hbm, s0, grad_ref, sems,
+):
+    fwd_copy = pltpu.make_async_copy(fwd_ref, fwd_hbm, sems.at[0])
+    state_copy = pltpu.make_async_copy(state_ref, state_hbm, sems.at[1])
+    fwd_copy.start()
+    state_copy.start()
     low, high = halos(up_ref, down_ref, 0, half)
     lay(s0, 0, low)
     lay(s0, planes + 1, high)
     for p in range(planes):
         lay(s0, 1 + p, rows_of(inner_ref, p, half))
-    lows = [(rows_of(low_ref, p, half) + conv(s0, 1 + p, tf_ref)).astype(BF16) for p in range(planes)]
-    join_planes([rows_of(top_ref, p, half) for p in range(planes)], out_ref, 0)
-    join_planes(lows, out_ref, out_ref.shape[0] // 2)
-
-
-def pack_state(half, planes, state_ref, out_ref):
+    middle = grad_ref.shape[0] // 2
+    join_planes([rows_of(top_ref, p, half) for p in range(planes)], join_ref[...], grad_ref, 0)
+    top_copy = pltpu.make_async_copy(grad_ref.at[:middle], grad_hbm.at[:middle], sems.at[2])
+    top_copy.start()
+    terms = convs(s0, 1, planes, tf_ref)
+    lows = [(rows_of(low_ref, p, half) + term).astype(BF16) for p, term in enumerate(terms)]
+    join_planes(lows, join_ref[...], grad_ref, middle)
+    low_copy = pltpu.make_async_copy(grad_ref.at[middle:], grad_hbm.at[middle:], sems.at[3])
+    low_copy.start()
+    fwd_copy.wait()
+    state_copy.wait()
+    top_copy.wait()
+    low_copy.wait()
+
+
+def pack_state(half, planes, state_ref, join_ref, out_ref):
     for h in range(2):
-        join_planes(
-            [rows_of(state_ref, h * planes + p, half) for p in range(planes)], out_ref, h * out_ref.shape[0] // 2
-        )
-
-
-def call(body, name, outs, scratch, flops, *args):
-    in_place = pl.BlockSpec(memory_space=pltpu.VMEM)
+        values = [rows_of(state_ref, h * planes + p, half) for p in range(planes)]
+        join_planes(values, join_ref[...], out_ref, h * out_ref.shape[0] // 2)
+
+
+def call(body, outs, scratch, flops, *args, far_out=False):
+    near, far = pl.BlockSpec(memory_space=pltpu.VMEM), pl.BlockSpec(memory_space=pltpu.HBM)
     return pl.pallas_call(
         body,
-        name=name,
         out_shape=[jax.ShapeDtypeStruct(shape, dtype) for shape, dtype in outs],
-        in_specs=[in_place] * len(args),
-        out_specs=[in_place] * len(outs),
-        scratch_shapes=[pltpu.VMEM(shape, BF16) for shape in scratch],
+        in_specs=[near] * len(args),
+        out_specs=[far if far_out else near] * len(outs),
+        scratch_shapes=[pltpu.VMEM(shape, BF16) if isinstance(shape, tuple) else shape for shape in scratch],
         compiler_params=pltpu.CompilerParams(vmem_limit_bytes=16 << 20),
         cost_estimate=pl.CostEstimate(flops=flops, bytes_accessed=1 << 20, transcendentals=0),
     )(*args)
@@ -381,36 +407,49 @@
     half = chans // 2
 
     def swap(up, down):
-        return lax.ppermute(up, ("section", "slab"), ahead), lax.ppermute(down, ("section", "slab"), behind)
+        from_up = lax.ppermute(up, ("section", "slab"), ahead)
+        from_down = lax.ppermute(down, ("section", "slab"), behind)
+        return from_up, from_down
 
     def along(value, step):
         return lax.ppermute(value, "section", [(s, (s + step) % sections) for s in range(sections)])
 
     got_y = along(raw_view(back_states[0]), -1)
-    got_g = along(raw_view(back_grads[0]), -1)
-    got_x = along(raw_view(fwd_states[0]), 1)
+    grads = raw_view(back_grads[0])
+    middle = grads.shape[0] // 2
+    grads_low, grads_high = grads[middle:], grads[:middle]
+    got_g2 = along(grads_low, -1)
+    got_g1 = along(grads_high, -1)
+    source, got_y = lax.optimization_barrier((raw_view(fwd_states[0]), got_y))
+    got_x = along(source, 1)
 
     def planes_of(count, dtype=BF16):
         return ((count * half, cells), dtype)
 
     unit = 2 * 9 * half * 3 * half * cells
-    weights = call(
-        prepare, "prepare", [((3 * half, 9 * half), BF16)] * (4 * PAIRS), [], unit, couplings
+    raw_shape = ((chans * planes * cells // LANES, LANES), BF16)
+    *weights, split, join = call(
+        functools.partial(prepare, planes, cells),
+        [((6 * half, 12 * half), BF16)] * (4 * PAIRS) + [((256, 256), BF16)] * 2, [], 40 * unit, couplings,
     )
     direct, turned = weights[: 2 * PAIRS], weights[2 * PAIRS :]
 
     sizes = (half, planes, cells)
     y_own, y_up, y_down = call(
-        functools.partial(unpack_state, True, 0, *sizes), "unpack_y",
-        [planes_of(2 * planes), planes_of(planes + 1), planes_of(planes + 1)], [], unit, got_y, raw_view(head_state),
-    )
-    g_own, g_up, g_down = call(
-        functools.partial(unpack_grad, *sizes), "unpack_g",
-        [planes_of(2 * planes), planes_of(1), planes_of(1)], [], unit, got_g, raw_view(head_grad),
+        functools.partial(unpack_state, True, 0, *sizes),
+        [planes_of(2 * planes), planes_of(planes + 1), planes_of(planes + 1)], [], unit, got_y, raw_view(head_state), split,
+    )
+    g2_own, g_up, g_down = call(
+        functools.partial(unpack_grad, 1, *sizes),
+        [planes_of(planes), planes_of(1), planes_of(1)], [], unit, got_g2, raw_view(head_grad), split,
+    )
+    (g1_own,) = call(
+        functools.partial(unpack_grad, 0, *sizes), [planes_of(planes)], [], unit,
+        got_g1, raw_view(head_grad), split,
     )
     x_own, x_up, x_down = call(
-        functools.partial(unpack_state, False, 1, *sizes), "unpack_x",
-        [planes_of(2 * planes), planes_of(planes + 1), planes_of(planes + 1)], [], unit, got_x, raw_view(batch_in),
+        functools.partial(unpack_state, False, 1, *sizes),
+        [planes_of(2 * planes), planes_of(planes + 1), planes_of(planes + 1)], [], unit, got_x, raw_view(batch_in), split,
     )
     yu, yd = swap(y_up, y_down)
     gu, gd = swap(g_up, g_down)
@@ -419,34 +458,34 @@
     wide = ((3 * planes) * 3 * half, cells)
     near = ((planes + 2) * 3 * half, cells)
     send, second, low_grad, carry = call(
-        functools.partial(backward_first, half, planes), "backward_first",
+        functools.partial(backward_first, half, planes),
         [planes_of(2 * planes), planes_of(planes + 2), planes_of(planes + 2), planes_of(planes, F32)],
         [wide, near, near], 8 * unit,
-        y_own, g_own, yu, yd, gu, gd, direct[3], direct[2], turned[3],
+        y_own, g1_own, g2_own, yu, yd, gu, gd, direct[3], direct[2], turned[3],
     )
     su, sd = swap(send, send)
     mid, low_own = call(
-        functools.partial(forward_first, half, planes), "forward_first",
+        functools.partial(forward_first, half, planes),
         [planes_of(planes + 2), planes_of(planes)], [wide, near], 6 * unit,
         x_own, xu, xd, direct[0], direct[1],
     )
     fu, fd = swap(low_own, low_own)
     state, inner, low, top, iu, id_ = call(
-        functools.partial(backward_second, half, planes), "backward_second",
+        functools.partial(backward_second, half, planes),
         [planes_of(2 * planes), planes_of(planes), planes_of(planes, F32), planes_of(planes), planes_of(1), planes_of(1)],
         [wide, near, wide, near], 12 * unit,
         send, su, sd, second, low_grad, carry, turned[2], direct[1], direct[0], turned[1],
     )
     iu, id_ = swap(iu, id_)
-    raw_out = ((chans * planes * cells // LANES, LANES), BF16)
     (fwd_raw,) = call(
-        functools.partial(forward_second, half, planes), "forward_second", [raw_out], [wide, near], 6 * unit,
-        mid, low_own, fu, fd, direct[2], direct[3],
-    )
-    (state_raw,) = call(functools.partial(pack_state, half, planes), "pack_state", [raw_out], [], unit, state)
-    (grad_raw,) = call(
-        functools.partial(backward_third, half, planes), "backward_third", [raw_out], [near], 2 * unit,
-        inner, iu, id_, low, top, turned[0],
+        functools.partial(forward_second, half, planes), [raw_shape], [wide, near], 6 * unit,
+        mid, low_own, fu, fd, direct[2], direct[3], join,
+    )
+    (state_raw,) = call(functools.partial(pack_state, half, planes), [raw_shape], [], unit, state, join)
+    fwd_raw, state_raw, grad_raw = call(
+        functools.partial(backward_third, half, planes), [raw_shape] * 3,
+        [near, raw_shape[0], pltpu.SemaphoreType.DMA((4,))], 2 * unit,
+        inner, iu, id_, low, top, turned[0], join, fwd_raw, state_raw, far_out=True,
     )
     shape = (chans, planes, cells)
     return from_raw(fwd_raw, *shape), from_raw(state_raw, *shape), from_raw(grad_raw, *shape)

time: 44.8 us -> 45.9 us (1.025); the launches traced: 44.5 us -> 45 us
  starting transfers between devices: 14.9 us -> 15.8 us
  local copies, waits for them, and re-layouts: 3.38 us -> 2.69 us
    ppermute x12, waiting for transfers between devices: 6.55 us -> 11.7 us  [the longest x6 10 us: swap(): from_up = lax.ppermute(up, ('section', 'slab'), ahead)]
    ppermute x3 -> x4, waiting for transfers between devices: 6.17 us -> 1.22 us  [along(): lax.ppermute(value, 'section', [(s, (s + step) % sections) for s in range...]
    unnamed x8 -> x10, local copies, waits for them, and re-layouts: 3.38 us -> 1.54 us
    slice x0 -> x1, local copies, waits for them, and re-layouts: none -> 1.15 us  [shards(): grads_low, grads_high = (grads[middle:], grads[:middle])]
    ppermute x12, starting transfers between devices: 10.8 us -> 11.7 us  [the longest x6 11.6 us: swap(): from_up = lax.ppermute(up, ('section', 'slab'), ahead)]
    pallas_call x10 -> x11, Pallas kernels: 12.9 us -> 12.8 us  [call(): pl.pallas_call(body, out_shape=[jax.ShapeDtypeStruct(shape, dtype) for sh...]
    ppermute x3 -> x4, starting transfers between devices: 4.09 us -> 4.16 us  [along(): lax.ppermute(value, 'section', [(s, (s + step) % sections) for s in range...]
  transfers between devices with their start and end apart: 15 -> 16, of which waited for: 5 -> 6; matrix products, arithmetic and copies ran while one was open for 0% -> 0% of each run, Pallas kernels for 25% -> 25%
where the time goes in v2:
time: 45.9 us; the launch traced here: 45 us
  starting transfers between devices  15.8 us (34%)
  waiting for transfers between devices  13 us (28%)
  Pallas kernels  12.8 us (28%)
  local copies, waits for them, and re-layouts  2.69 us (6%)
  between operations  0.78 us (2%)
    pallas_call x11, Pallas kernels, call(): pl.pallas_call(body, out_shape=[jax.ShapeDtypeStruct(shape, dtype) for sh...  12.8 us
    ppermute x6, starting transfers between devices, swap(): from_up = lax.ppermute(up, ('section', 'slab'), ahead)  11.6 us
    ppermute x6, waiting for transfers between devices, swap(): from_up = lax.ppermute(up, ('section', 'slab'), ahead)  10 us
    ppermute x4, starting transfers between devices, along(): lax.ppermute(value, 'section', [(s, (s + step) % sections) for s in range...  4.16 us
    ppermute x6, waiting for transfers between devices, swap(): from_down = lax.ppermute(down, ('section', 'slab'), behind)  1.72 us
    unnamed x10, local copies, waits for them, and re-layouts  1.54 us
    ppermute x4, waiting for transfers between devices, along(): lax.ppermute(value, 'section', [(s, (s + step) % sections) for s in range...  1.22 us
    slice x1, local copies, waits for them, and re-layouts, shards(): grads_low, grads_high = (grads[middle:], grads[:middle])  1.15 us
  transfers between devices with their start and end apart: 16, of which 6 were waited for; matrix products, arithmetic and copies ran while one was open for 0% of the time, Pallas kernels for 25%

profile of v2, /device:TPU:0, one launch (start us, length us, event | category | flops | bytes accessed | tf_op | source)
XLA Modules:
  0.0 45.0 jit_solution(9362341768773911522)
XLA Ops:
  0.6 1.2 %fusion = (bf16[64,4,2,128]{3,2,1,0:T(2,128)(2,1)S(1)}, bf16[64,4,2,128]{3,2,1,0:T(2,128)(2,1)S(1)}) fusion(bf16[128,4,2,128]{3,2,1,0:T(2,128)(2,1)} %bitcast.49), kind=kLoop, calls=%fused_computation | loop fusion | bytes 524288 | tf_op jit(solution)/shard_map/slice | solution.py:420
  1.8 3.4 %collective-permute-start.2 = (bf16[512,128]{1,0:T(8,128)(2,1)S(1)}, bf16[512,128]{1,0:T(8,128)(2,1)S(1)}, u32[]{:S(2)}, u32[]{:S(2)}) collective-permute-start(bf16[512,128]{1,0:T(8,128)(2,1)S(1)} %bitcast.51), channel_id=1, source_target_pairs={{0,28},{4,0},{8,4},{12,8},{16,12},{20,16},{24,20},{28,24},{1,29},{... | collective-permute-start | bytes 393224 | tf_op jit(solution)/shard_map/ppermute | solution.py:415
  5.2 0.7 %collective-permute-start = (bf16[1024,128]{1,0:T(8,128)(2,1)}, bf16[1024,128]{1,0:T(8,128)(2,1)S(1)}, u32[]{:S(2)}, u32[]{:S(2)}) collective-permute-start(bf16[1024,128]{1,0:T(8,128)(2,1)} %bitcast.52), channel_id=1, source_target_pairs={{0,28},{4,0},{8,4},{12,8},{16,12},{20,16},{24,20},{28,24},{1,29},{... | collective-permute-start | bytes 786440 | tf_op jit(solution)/shard_map/ppermute | solution.py:415
  5.9 0.0 copy-start.1
  5.9 0.0 copy-start
  5.9 0.1 collective-permute-start.1
  5.9 0.0 copy-start.3
  5.9 1.5 %copy-done.3 = bf16[1,4,27,64,64]{4,3,2,1,0:T(8,128)(2,1)S(1)} copy-done((bf16[1,4,27,64,64]{4,3,2,1,0:T(8,128)(2,1)S(1)}, bf16[1,4,27,64,64]{4,3,2,1,0:T(8,128)(2,1)}, u32[]{:S(2)}) %copy-start.3) | copy-done | bytes 884760
  7.5 0.0 copy-start.4
  7.5 1.9 %shard_map.94 = (bf16[384,768]{1,0:T(8,128)(2,1)S(1)}, bf16[384,768]{1,0:T(8,128)(2,1)S(1)}, bf16[384,768]{1,0:T(8,128)(2,1)S(1)}, bf16[384,768]{1,0:T(8,128)(2,...) custom-call(bf16[1,4,27,64,64]{4,3,2,1,0:T(8,128)(2,1)S(1)} %copy-done.3), custom_call_target="tpu_custom_call" | custom-call | flops 4529848320 | bytes 1048576 | tf_op jit(solution)/shard_map/pallas_call | solution.py:373
  9.4 1.2 %collective-permute-done.got_ref = bf16[1024,128]{1,0:T(8,128)(2,1)S(1)} collective-permute-done((bf16[1024,128]{1,0:T(8,128)(2,1)}, bf16[1024,128]{1,0:T(8,128)(2,1)S(1)}, u32[]{:S(2)}, u32[]{:S(2)}) %collective-permute-start) | collective-permute-done | bytes 262176 | tf_op jit(solution)/shard_map/ppermute | solution.py:415
  10.6 0.0 copy-done.1
  10.6 0.3 shard_map.95
  10.9 1.6 %collective-permute-start.3 = (bf16[192,512]{1,0:T(8,128)(2,1)S(1)}, bf16[192,512]{1,0:T(8,128)(2,1)S(1)}, u32[]{:S(2)}, u32[]{:S(2)}) collective-permute-start(bf16[192,512]{1,0:T(8,128)(2,1)S(1)} %get-tuple-element.43), channel_id=1, source_target_pairs={{0,1},{1,2},{2,3},{3,7},{7,6},{6,5},{5,4},{4,0},{8,9},{9,10},{10,1... | collective-permute-start | bytes 589832 | tf_op jit(solution)/shard_map/ppermute | solution.py:410
  12.5 0.0 collective-permute-start.4
  12.5 0.0 copy-done.4
  12.5 0.0 collective-permute-start.11
  12.5 0.0 collective-permute-done.2.got_ref
  12.5 0.0 copy-done
  12.5 0.2 shard_map.97
  12.7 2.0 %collective-permute-start.5 = (bf16[64,512]{1,0:T(8,128)(2,1)S(1)}, bf16[64,512]{1,0:T(8,128)(2,1)S(1)}, u32[]{:S(2)}, u32[]{:S(2)}) collective-permute-start(bf16[64,512]{1,0:T(8,128)(2,1)S(1)} %get-tuple-element.45), channel_id=1, source_target_pairs={{0,1},{1,2},{2,3},{3,7},{7,6},{6,5},{5,4},{4,0},{8,9},{9,10},{10,1... | collective-permute-start | bytes 196616 | tf_op jit(solution)/shard_map/ppermute | solution.py:410
  14.7 0.0 collective-permute-done.1.got_ref
  14.7 0.0 collective-permute-start.6
  14.7 0.2 shard_map.96.g1_ref
  14.9 0.0 copy-start.2
  15.0 3.2 %collective-permute-done.5.gu_ref = bf16[64,512]{1,0:T(8,128)(2,1)S(1)} collective-permute-done((bf16[64,512]{1,0:T(8,128)(2,1)S(1)}, bf16[64,512]{1,0:T(8,128)(2,1)S(1)}, u32[]{:S(2)}, u32[]{:S(2)}) %collective-permute-start.5) | collective-permute-done | bytes 65568 | tf_op jit(solution)/shard_map/ppermute | solution.py:410
  18.1 1.4 %collective-permute-done.6.gd_ref = bf16[64,512]{1,0:T(8,128)(2,1)S(1)} collective-permute-done((bf16[64,512]{1,0:T(8,128)(2,1)S(1)}, bf16[64,512]{1,0:T(8,128)(2,1)S(1)}, u32[]{:S(2)}, u32[]{:S(2)}) %collective-permute-start.6) | collective-permute-done | bytes 65568 | tf_op jit(solution)/shard_map/ppermute | solution.py:411
  19.5 0.0 collective-permute-done.3.yu_ref
  19.5 0.0 collective-permute-done.4.yd_ref
  19.5 2.0 %shard_map.98 = (bf16[256,512]{1,0:T(8,128)(2,1)S(1)}, bf16[256,512]{1,0:T(8,128)(2,1)S(1)}, bf16[256,512]{1,0:T(8,128)(2,1)S(1)}, f32[128,512]{1,0:T(8,128)S(1)}) custom-call(bf16[256,512]{1,0:T(8,128)(2,1)S(1)} %get-tuple-element.41.y_ref, bf16[128,512]{1,0:T(8,128)(2,1)S(1)} %shard_map.96.g1_ref, bf16[128,512]{1,0:T(8,128)(2,1)S(1)} %get-tuple-element.42.g2_ref, ...), custom_call_target="tpu_custom_call" | custom-call | flops 905969664 | bytes 1048576 | tf_op jit(solution)/shard_map/pallas_call | solution.py:373
  21.5 1.6 %collective-permute-start.7 = (bf16[256,512]{1,0:T(8,128)(2,1)S(1)}, bf16[256,512]{1,0:T(8,128)(2,1)S(1)}, u32[]{:S(2)}, u32[]{:S(2)}) collective-permute-start(bf16[256,512]{1,0:T(8,128)(2,1)S(1)} %get-tuple-element.50.mine_ref), channel_id=1, source_target_pairs={{0,1},{1,2},{2,3},{3,7},{7,6},{6,5},{5,4},{4,0},{8,9},{9,10},{10,1... | collective-permute-start | bytes 786440 | tf_op jit(solution)/shard_map/ppermute | solution.py:410
  23.1 0.0 collective-permute-start.8
  23.1 0.0 collective-permute-done.11.got_ref
  23.1 0.0 copy-done.2
  23.2 0.3 shard_map.100
  23.4 2.0 %collective-permute-start.12 = (bf16[192,512]{1,0:T(8,128)(2,1)S(1)}, bf16[192,512]{1,0:T(8,128)(2,1)S(1)}, u32[]{:S(2)}, u32[]{:S(2)}) collective-permute-start(bf16[192,512]{1,0:T(8,128)(2,1)S(1)} %get-tuple-element.67), channel_id=1, source_target_pairs={{0,1},{1,2},{2,3},{3,7},{7,6},{6,5},{5,4},{4,0},{8,9},{9,10},{10,1... | collective-permute-start | bytes 589832 | tf_op jit(solution)/shard_map/ppermute | solution.py:410
  25.5 0.0 collective-permute-start.13
  25.5 6.8 %collective-permute-done.12.up_ref = bf16[192,512]{1,0:T(8,128)(2,1)S(1)} collective-permute-done((bf16[192,512]{1,0:T(8,128)(2,1)S(1)}, bf16[192,512]{1,0:T(8,128)(2,1)S(1)}, u32[]{:S(2)}, u32[]{:S(2)}) %collective-permute-start.12) | collective-permute-done | bytes 196640 | tf_op jit(solution)/shard_map/ppermute | solution.py:410
  32.3 0.2 collective-permute-done.13.down_ref
  32.5 1.6 %shard_map.101 = (bf16[256,512]{1,0:T(8,128)(2,1)S(1)}, bf16[128,512]{1,0:T(8,128)(2,1)S(1)}) custom-call(bf16[256,512]{1,0:T(8,128)(2,1)S(1)} %get-tuple-element.66.own_ref, bf16[192,512]{1,0:T(8,128)(2,1)S(1)} %collective-permute-done.12.up_ref, bf16[192,512]{1,0:T(8,128)(2,1)S(1)} %collective-permute-done.13.down_ref, ...), custom_call_target="tpu_custom_call" | custom-call | flops 679477248 | bytes 1048576 | tf_op jit(solution)/shard_map/pallas_call | solution.py:373
  34.0 2.4 %collective-permute-start.14 = (bf16[128,512]{1,0:T(8,128)(2,1)S(1)}, bf16[128,512]{1,0:T(8,128)(2,1)S(1)}, u32[]{:S(2)}, u32[]{:S(2)}) collective-permute-start(bf16[128,512]{1,0:T(8,128)(2,1)S(1)} %get-tuple-element.70.own_ref), channel_id=1, source_target_pairs={{0,1},{1,2},{2,3},{3,7},{7,6},{6,5},{5,4},{4,0},{8,9},{9,10},{10,1... | collective-permute-start | bytes 393224 | tf_op jit(solution)/shard_map/ppermute | solution.py:410
  36.4 0.0 collective-permute-start.15
  36.4 0.0 collective-permute-done.7.up_ref
  36.4 0.0 collective-permute-done.8.down_ref
  36.4 2.8 %shard_map.99 = (bf16[256,512]{1,0:T(8,128)(2,1)S(1)}, bf16[128,512]{1,0:T(8,128)(2,1)S(1)}, f32[128,512]{1,0:T(8,128)S(1)}, bf16[128,512]{1,0:T(8,128)(2,1)S(1)...) custom-call(bf16[256,512]{1,0:T(8,128)(2,1)S(1)} %get-tuple-element.50.mine_ref, ...), custom_call_target="tpu_custom_call" | custom-call | flops 1358954496 | bytes 1048576 | tf_op jit(solution)/shard_map/pallas_call | solution.py:373
  39.2 0.0 collective-permute-start.10
  39.2 2.0 %collective-permute-start.9 = (bf16[64,512]{1,0:T(8,128)(2,1)S(1)}, bf16[64,512]{1,0:T(8,128)(2,1)S(1)}, u32[]{:S(2)}, u32[]{:S(2)}) collective-permute-start(bf16[64,512]{1,0:T(8,128)(2,1)S(1)} %get-tuple-element.59), channel_id=1, source_target_pairs={{0,1},{1,2},{2,3},{3,7},{7,6},{6,5},{5,4},{4,0},{8,9},{9,10},{10,1... | collective-permute-start | bytes 196616 | tf_op jit(solution)/shard_map/ppermute | solution.py:410
  41.2 0.2 shard_map.103.state_ref
  41.5 0.0 collective-permute-done.14.up_ref
  41.5 0.0 collective-permute-done.15.down_ref
  41.5 1.8 %shard_map.102.fwd_ref = bf16[1024,128]{1,0:T(8,128)(2,1)S(1)} custom-call(bf16[256,512]{1,0:T(8,128)(2,1)S(1)} %get-tuple-element.69.mid_ref, bf16[128,512]{1,0:T(8,128)(2,1)S(1)} %get-tuple-element.70.own_ref, bf16[128,512]{1,0:T(8,128)(2,1)S(1)} %collective-permute-done.14.up_ref, bf16[128,512]{1,0:T(8,128)(2,1)S(1)} %collective-permute-done.15.down_ref, ...), custom_call_target="tpu_custom_call" | custom-call | flops 679477248 | bytes 1048576 | tf_op jit(solution)/shard_map/pallas_call | solution.py:373
  43.3 0.2 collective-permute-done.10.down_ref
  43.5 0.0 collective-permute-done.9.up_ref
  43.5 1.6 %shard_map.104 = (bf16[1024,128]{1,0:T(8,128)(2,1)}, bf16[1024,128]{1,0:T(8,128)(2,1)}, bf16[1024,128]{1,0:T(8,128)(2,1)}) custom-call(bf16[128,512]{1,0:T(8,128)(2,1)S(1)} %get-tuple-element.58.inner_ref, bf16[64,512]{1,0:T(8,128)(2,1)S(1)} %collective-permute-done.9.up_ref, bf16[64,512]{1,0:T(8,128)(2,1)S(1)} %collective-permute-done.10.down_ref, ...), custom_call_target="tpu_custom_call" | custom-call | flops 226492416 | bytes 1048576 | tf_op jit(solution)/shard_map/pallas_call | solution.py:373
Async XLA Ops:
  1.8 10.7 %collective-permute-start.2 = (bf16[512,128]{1,0:T(8,128)(2,1)S(1)}, bf16[512,128]{1,0:T(8,128)(2,1)S(1)}, u32[]{:S(2)}, u32[]{:S(2)}) collective-permute-start(bf16[512,128]{1,0:T(8,128)(2,1)S(1)} %bitcast.51), channel_id=1, source_target_pairs={{0,28},{4,0},{8,4},{12,8},{16,12},{20,16},{24,20},{28,24},{1,29},{... | collective-permute-start | bytes 393224 | tf_op jit(solution)/shard_map/ppermute | solution.py:415
  5.2 5.4 %collective-permute-start = (bf16[1024,128]{1,0:T(8,128)(2,1)}, bf16[1024,128]{1,0:T(8,128)(2,1)S(1)}, u32[]{:S(2)}, u32[]{:S(2)}) collective-permute-start(bf16[1024,128]{1,0:T(8,128)(2,1)} %bitcast.52), channel_id=1, source_target_pairs={{0,28},{4,0},{8,4},{12,8},{16,12},{20,16},{24,20},{28,24},{1,29},{... | collective-permute-start | bytes 786440 | tf_op jit(solution)/shard_map/ppermute | solution.py:415
  5.9 4.7 %copy-start.1 = (bf16[128,2,512]{2,1,0:T(2,128)(2,1)S(1)}, bf16[128,2,512]{2,1,0:T(2,128)(2,1)}, u32[]{:S(2)}) copy-start(bf16[128,2,512]{2,1,0:T(2,128)(2,1)} %param.11) | copy-start | bytes 786436
  5.9 6.6 %copy-start = (bf16[128,2,512]{2,1,0:T(2,128)(2,1)S(1)}, bf16[128,2,512]{2,1,0:T(2,128)(2,1)}, u32[]{:S(2)}) copy-start(bf16[128,2,512]{2,1,0:T(2,128)(2,1)} %param.12) | copy-start | bytes 786436
  5.9 8.9 %collective-permute-start.1 = (bf16[512,128]{1,0:T(8,128)(2,1)S(1)}, bf16[512,128]{1,0:T(8,128)(2,1)S(1)}, u32[]{:S(2)}, u32[]{:S(2)}) collective-permute-start(bf16[512,128]{1,0:T(8,128)(2,1)S(1)} %bitcast.50), channel_id=1, source_target_pairs={{0,28},{4,0},{8,4},{12,8},{16,12},{20,16},{24,20},{28,24},{1,29},{... | collective-permute-start | bytes 393224 | tf_op jit(solution)/shard_map/ppermute | solution.py:415
  5.9 1.5 %copy-start.3 = (bf16[1,4,27,64,64]{4,3,2,1,0:T(8,128)(2,1)S(1)}, bf16[1,4,27,64,64]{4,3,2,1,0:T(8,128)(2,1)}, u32[]{:S(2)}) copy-start(bf16[1,4,27,64,64]{4,3,2,1,0:T(8,128)(2,1)} %kernels_ref.1) | copy-start | bytes 2654212
  7.5 5.0 %copy-start.4 = (bf16[1,128,2,512]{3,2,1,0:T(2,128)(2,1)S(1)}, bf16[1,128,2,512]{3,2,1,0:T(2,128)(2,1)}, u32[]{:S(2)}) copy-start(bf16[1,128,2,512]{3,2,1,0:T(2,128)(2,1)} %param.7) | copy-start | bytes 786436
  10.9 8.6 %collective-permute-start.3 = (bf16[192,512]{1,0:T(8,128)(2,1)S(1)}, bf16[192,512]{1,0:T(8,128)(2,1)S(1)}, u32[]{:S(2)}, u32[]{:S(2)}) collective-permute-start(bf16[192,512]{1,0:T(8,128)(2,1)S(1)} %get-tuple-element.43), channel_id=1, source_target_pairs={{0,1},{1,2},{2,3},{3,7},{7,6},{6,5},{5,4},{4,0},{8,9},{9,10},{10,1... | collective-permute-start | bytes 589832 | tf_op jit(solution)/shard_map/ppermute | solution.py:410
  12.5 7.1 %collective-permute-start.4 = (bf16[192,512]{1,0:T(8,128)(2,1)S(1)}, bf16[192,512]{1,0:T(8,128)(2,1)S(1)}, u32[]{:S(2)}, u32[]{:S(2)}) collective-permute-start(bf16[192,512]{1,0:T(8,128)(2,1)S(1)} %get-tuple-element.44), channel_id=1, source_target_pairs={{1,0},{2,1},{3,2},{7,3},{6,7},{5,6},{4,5},{0,4},{9,8},{10,9},{11,1... | collective-permute-start | bytes 589832 | tf_op jit(solution)/shard_map/ppermute | solution.py:411
  12.5 10.7 %collective-permute-start.11 = (bf16[1024,128]{1,0:T(8,128)(2,1)S(1)}, bf16[1024,128]{1,0:T(8,128)(2,1)S(1)}, u32[]{:S(2)}, u32[]{:S(2)}) collective-permute-start(bf16[1024,128]{1,0:T(8,128)(2,1)S(1)} %bitcast.53), channel_id=1, source_target_pairs={{0,4},{4,8},{8,12},{12,16},{16,20},{20,24},{24,28},{28,0},{1,5},{5... | collective-permute-start | bytes 786440 | tf_op jit(solution)/shard_map/ppermute | solution.py:415
  12.7 5.4 %collective-permute-start.5 = (bf16[64,512]{1,0:T(8,128)(2,1)S(1)}, bf16[64,512]{1,0:T(8,128)(2,1)S(1)}, u32[]{:S(2)}, u32[]{:S(2)}) collective-permute-start(bf16[64,512]{1,0:T(8,128)(2,1)S(1)} %get-tuple-element.45), channel_id=1, source_target_pairs={{0,1},{1,2},{2,3},{3,7},{7,6},{6,5},{5,4},{4,0},{8,9},{9,10},{10,1... | collective-permute-start | bytes 196616 | tf_op jit(solution)/shard_map/ppermute | solution.py:410
  14.7 4.8 %collective-permute-start.6 = (bf16[64,512]{1,0:T(8,128)(2,1)S(1)}, bf16[64,512]{1,0:T(8,128)(2,1)S(1)}, u32[]{:S(2)}, u32[]{:S(2)}) collective-permute-start(bf16[64,512]{1,0:T(8,128)(2,1)S(1)} %get-tuple-element.46), channel_id=1, source_target_pairs={{1,0},{2,1},{3,2},{7,3},{6,7},{5,6},{4,5},{0,4},{9,8},{10,9},{11,1... | collective-permute-start | bytes 196616 | tf_op jit(solution)/shard_map/ppermute | solution.py:411
  14.9 8.2 %copy-start.2 = (bf16[128,2,512]{2,1,0:T(2,128)(2,1)S(1)}, bf16[128,2,512]{2,1,0:T(2,128)(2,1)}, u32[]{:S(2)}) copy-start(bf16[128,2,512]{2,1,0:T(2,128)(2,1)} %param.10) | copy-start | bytes 786436
  21.5 14.9 %collective-permute-start.7 = (bf16[256,512]{1,0:T(8,128)(2,1)S(1)}, bf16[256,512]{1,0:T(8,128)(2,1)S(1)}, u32[]{:S(2)}, u32[]{:S(2)}) collective-permute-start(bf16[256,512]{1,0:T(8,128)(2,1)S(1)} %get-tuple-element.50.mine_ref), channel_id=1, source_target_pairs={{0,1},{1,2},{2,3},{3,7},{7,6},{6,5},{5,4},{4,0},{8,9},{9,10},{10,1... | collective-permute-start | bytes 786440 | tf_op jit(solution)/shard_map/ppermute | solution.py:410
  23.1 13.3 %collective-permute-start.8 = (bf16[256,512]{1,0:T(8,128)(2,1)S(1)}, bf16[256,512]{1,0:T(8,128)(2,1)S(1)}, u32[]{:S(2)}, u32[]{:S(2)}) collective-permute-start(bf16[256,512]{1,0:T(8,128)(2,1)S(1)} %get-tuple-element.50.mine_ref), channel_id=1, source_target_pairs={{1,0},{2,1},{3,2},{7,3},{6,7},{5,6},{4,5},{0,4},{9,8},{10,9},{11,1... | collective-permute-start | bytes 786440 | tf_op jit(solution)/shard_map/ppermute | solution.py:411
  23.4 8.9 %collective-permute-start.12 = (bf16[192,512]{1,0:T(8,128)(2,1)S(1)}, bf16[192,512]{1,0:T(8,128)(2,1)S(1)}, u32[]{:S(2)}, u32[]{:S(2)}) collective-permute-start(bf16[192,512]{1,0:T(8,128)(2,1)S(1)} %get-tuple-element.67), channel_id=1, source_target_pairs={{0,1},{1,2},{2,3},{3,7},{7,6},{6,5},{5,4},{4,0},{8,9},{9,10},{10,1... | collective-permute-start | bytes 589832 | tf_op jit(solution)/shard_map/ppermute | solution.py:410
  25.5 7.0 %collective-permute-start.13 = (bf16[192,512]{1,0:T(8,128)(2,1)S(1)}, bf16[192,512]{1,0:T(8,128)(2,1)S(1)}, u32[]{:S(2)}, u32[]{:S(2)}) collective-permute-start(bf16[192,512]{1,0:T(8,128)(2,1)S(1)} %get-tuple-element.68), channel_id=1, source_target_pairs={{1,0},{2,1},{3,2},{7,3},{6,7},{5,6},{4,5},{0,4},{9,8},{10,9},{11,1... | collective-permute-start | bytes 589832 | tf_op jit(solution)/shard_map/ppermute | solution.py:411
  34.0 7.4 %collective-permute-start.14 = (bf16[128,512]{1,0:T(8,128)(2,1)S(1)}, bf16[128,512]{1,0:T(8,128)(2,1)S(1)}, u32[]{:S(2)}, u32[]{:S(2)}) collective-permute-start(bf16[128,512]{1,0:T(8,128)(2,1)S(1)} %get-tuple-element.70.own_ref), channel_id=1, source_target_pairs={{0,1},{1,2},{2,3},{3,7},{7,6},{6,5},{5,4},{4,0},{8,9},{9,10},{10,1... | collective-permute-start | bytes 393224 | tf_op jit(solution)/shard_map/ppermute | solution.py:410
  36.4 5.1 %collective-permute-start.15 = (bf16[128,512]{1,0:T(8,128)(2,1)S(1)}, bf16[128,512]{1,0:T(8,128)(2,1)S(1)}, u32[]{:S(2)}, u32[]{:S(2)}) collective-permute-start(bf16[128,512]{1,0:T(8,128)(2,1)S(1)} %get-tuple-element.70.own_ref), channel_id=1, source_target_pairs={{1,0},{2,1},{3,2},{7,3},{6,7},{5,6},{4,5},{0,4},{9,8},{10,9},{11,1... | collective-permute-start | bytes 393224 | tf_op jit(solution)/shard_map/ppermute | solution.py:411
  39.2 4.3 %collective-permute-start.10 = (bf16[64,512]{1,0:T(8,128)(2,1)S(1)}, bf16[64,512]{1,0:T(8,128)(2,1)S(1)}, u32[]{:S(2)}, u32[]{:S(2)}) collective-permute-start(bf16[64,512]{1,0:T(8,128)(2,1)S(1)} %get-tuple-element.60), channel_id=1, source_target_pairs={{1,0},{2,1},{3,2},{7,3},{6,7},{5,6},{4,5},{0,4},{9,8},{10,9},{11,1... | collective-permute-start | bytes 196616 | tf_op jit(solution)/shard_map/ppermute | solution.py:411
  39.2 4.3 %collective-permute-start.9 = (bf16[64,512]{1,0:T(8,128)(2,1)S(1)}, bf16[64,512]{1,0:T(8,128)(2,1)S(1)}, u32[]{:S(2)}, u32[]{:S(2)}) collective-permute-start(bf16[64,512]{1,0:T(8,128)(2,1)S(1)} %get-tuple-element.59), channel_id=1, source_target_pairs={{0,1},{1,2},{2,3},{3,7},{7,6},{6,5},{5,4},{4,0},{8,9},{9,10},{10,1... | collective-permute-start | bytes 196616 | tf_op jit(solution)/shard_map/ppermute | solution.py:410

commit v3 on v2

--- a/solution.py
+++ b/solution.py
@@ -36,12 +36,14 @@
     return jnp.where(jnp.full(value.shape, flag), value, jnp.zeros((), value.dtype))
 
 
-def prepare(planes, cells, kernels_ref, *refs):
-    count = 2 * PAIRS
-    out_refs, (split_ref, join_ref) = refs[: 2 * count], refs[2 * count :]
+def matrices(planes, cells, split_ref, join_ref):
     tiles, chans = chunk_sizes(planes, cells)
     split_ref[...] = shuffle(tiles, planes, chans, False)
     join_ref[...] = shuffle(tiles, planes, chans, True)
+
+
+def prepare(kernels_ref, split_ref, *out_refs):
+    count = 2 * PAIRS
     taps, half = kernels_ref.shape[2], kernels_ref.shape[3]
     row = lax.broadcasted_iota(jnp.int32, (half, half), 0)
     col = lax.broadcasted_iota(jnp.int32, (half, half), 1)
@@ -52,15 +54,11 @@
             lax.dot_general(unit, m, (((1,), (1,)), ((), ())), preferred_element_type=F32).astype(BF16)
             for m in mine
         ]
-        blank = jnp.zeros((half, 3 * half), BF16)
         for b in range(3):
-            for kind, pieces in (
-                (0, [mine[9 * a + 3 * b + c] for a in range(3) for c in range(3)]),
-                (count, [turned[26 - (9 * a + 3 * b + c)] for a in range(3) for c in range(3)]),
-            ):
-                line = jnp.concatenate(pieces, axis=1)
-                for j, parts in ((0, [line, blank]), (1, [blank, line])):
-                    out_refs[kind + q][(3 * j + b) * half : (3 * j + b + 1) * half, :] = jnp.concatenate(parts, axis=1)
+            pieces = [mine[9 * a + 3 * b + c] for a in range(3) for c in range(3)]
+            out_refs[q][b * half : (b + 1) * half, :] = jnp.concatenate(pieces, axis=1)
+            pieces = [turned[26 - (9 * a + 3 * b + c)] for a in range(3) for c in range(3)]
+            out_refs[count + q][b * half : (b + 1) * half, :] = jnp.concatenate(pieces, axis=1)
 
 
 def shuffle(tiles, planes, chans, back):
@@ -137,23 +135,14 @@
 
 
 def conv(stack_ref, slot, weight_ref):
-    half = weight_ref.shape[0] // 6
+    half = weight_ref.shape[0] // 3
     cells = stack_ref.shape[1]
     begin = (slot - 1) * 3 * half
-    total = dot(weight_ref[...], stack_ref[begin : begin + 12 * half, :])
+    total = dot(weight_ref[...], stack_ref[begin : begin + 9 * half, :])
     cell = lax.broadcasted_iota(jnp.int32, (half, cells), 1)
-    results = []
-    for j in range(2):
-        rows = [total[(3 * j + b) * half : (3 * j + b + 1) * half] for b in range(3)]
-        above = jnp.where(cell >= WID, pltpu.roll(rows[0], WID, 1), 0.0)
-        below = jnp.where(cell < cells - WID, pltpu.roll(rows[2], cells - WID, 1), 0.0)
-        results.append(above + rows[1] + below)
-    return results
-
-
-def convs(stack_ref, slot, count, weight_ref):
-    for j in range(0, count, 2):
-        yield from conv(stack_ref, slot + j, weight_ref)
+    above = jnp.where(cell >= WID, pltpu.roll(total[:half], WID, 1), 0.0)
+    below = jnp.where(cell < cells - WID, pltpu.roll(total[2 * half :], cells - WID, 1), 0.0)
+    return above + total[half : 2 * half] + below
 
 
 def sigmoid(z):
@@ -217,7 +206,8 @@
         lay(s0, planes + p, rows_of(own_ref, planes + p, half))
     low, high = halos(up_ref, down_ref, planes, half)
     firsts = [low] + [rows_of(own_ref, p, half) for p in range(planes)] + [high]
-    for j, z in enumerate(convs(s0, planes - 1, planes + 2, f_ref)):
+    for j in range(planes + 2):
+        z = conv(s0, planes - 1 + j, f_ref)
         y = (firsts[j].astype(F32) + z * sigmoid(z)).astype(BF16)
         if j == 0:
             y = keep(has_low, y)
@@ -225,7 +215,8 @@
             y = keep(has_high, y)
         mid_ref[j * half : (j + 1) * half, :] = y
         lay(s1, j, y)
-    for p, z in enumerate(convs(s1, 1, planes, g_ref)):
+    for p in range(planes):
+        z = conv(s1, 1 + p, g_ref)
         y = (rows_of(own_ref, planes + p, half).astype(F32) + z * sigmoid(z)).astype(BF16)
         send_ref[p * half : (p + 1) * half, :] = y
 
@@ -238,7 +229,8 @@
         lay(s0, 2 * planes + p, high)
         lay(s0, planes + p, rows_of(own_ref, p, half))
     tops = []
-    for j, z in enumerate(convs(s0, planes - 1, planes + 2, f_ref)):
+    for j in range(planes + 2):
+        z = conv(s0, planes - 1 + j, f_ref)
         y = (rows_of(mid_ref, j, half).astype(F32) + z * sigmoid(z)).astype(BF16)
         if j == 0:
             y = keep(has_low, y)
@@ -248,7 +240,8 @@
             tops.append(y)
         lay(s1, j, y)
     bottoms = []
-    for p, z in enumerate(convs(s1, 1, planes, g_ref)):
+    for p in range(planes):
+        z = conv(s1, 1 + p, g_ref)
         bottoms.append((rows_of(own_ref, p, half).astype(F32) + z * sigmoid(z)).astype(BF16))
     join_planes(tops, join_ref[...], out_ref, 0)
     join_planes(bottoms, join_ref[...], out_ref, out_ref.shape[0] // 2)
@@ -275,7 +268,8 @@
     lowers = [low] + [rows_of(y_ref, planes + p, half) for p in range(planes)] + [high]
     low, high = halos(gu_ref, gd_ref, 0, half)
     grads = [low] + [rows_of(g2_ref, p, half) for p in range(planes)] + [high]
-    for j, z in enumerate(convs(s0, planes - 1, planes + 2, wg_ref)):
+    for j in range(planes + 2):
+        z = conv(s0, planes - 1 + j, wg_ref)
         second, inner = turn(z, lowers[j], grads[j].astype(F32))
         if j == 0:
             second, inner = keep(has_low, second), keep(has_low, inner)
@@ -285,8 +279,9 @@
         low_grad_ref[j * half : (j + 1) * half, :] = grads[j]
         lay(s1, j, second)
         lay(s2, j, inner)
-    for p, (z, term) in enumerate(zip(convs(s1, 1, planes, wf_ref), convs(s2, 1, planes, tg_ref))):
-        carry = rows_of(g1_ref, p, half).astype(F32) + term
+    for p in range(planes):
+        z = conv(s1, 1 + p, wf_ref)
+        carry = rows_of(g1_ref, p, half).astype(F32) + conv(s2, 1 + p, tg_ref)
         first, inner = turn(z, rows_of(y_ref, p, half), carry)
         carry_ref[p * half : (p + 1) * half, :] = carry
         send_ref[p * half : (p + 1) * half, :] = first
@@ -309,9 +304,9 @@
         lay(s2, p, low)
         lay(s2, 2 * planes + p, high)
         lay(s2, planes + p, rows_of(mine_ref, planes + p, half))
-    wide = (planes - 1, planes + 2)
-    for j, (term, z) in enumerate(zip(convs(s2, *wide, tf_ref), convs(s0, *wide, wg_ref))):
-        grad = rows_of(low_grad_ref, j, half).astype(F32) + term
+    for j in range(planes + 2):
+        grad = rows_of(low_grad_ref, j, half).astype(F32) + conv(s2, planes - 1 + j, tf_ref)
+        z = conv(s0, planes - 1 + j, wg_ref)
         second, inner = turn(z, rows_of(second_ref, j, half), grad)
         if j == 0:
             second, inner = keep(has_low, second), keep(has_low, inner)
@@ -323,8 +318,9 @@
         lay(s1, j, second)
         lay(s3, j, inner)
     inners = []
-    for p, (z, term) in enumerate(zip(convs(s1, 1, planes, wf_ref), convs(s3, 1, planes, tg_ref))):
-        carry = rows_of(carry_ref, p, half) + term
+    for p in range(planes):
+        z = conv(s1, 1 + p, wf_ref)
+        carry = rows_of(carry_ref, p, half) + conv(s3, 1 + p, tg_ref)
         first, inner = turn(z, rows_of(mine_ref, p, half), carry)
         state_ref[p * half : (p + 1) * half, :] = first
         top_ref[p * half : (p + 1) * half, :] = carry.astype(BF16)
@@ -340,21 +336,19 @@
 ):
     fwd_copy = pltpu.make_async_copy(fwd_ref, fwd_hbm, sems.at[0])
     state_copy = pltpu.make_async_copy(state_ref, state_hbm, sems.at[1])
+    middle = top_ref.shape[0]
+    top_copy = pltpu.make_async_copy(top_ref, grad_hbm.at[:middle], sems.at[2])
     fwd_copy.start()
     state_copy.start()
+    top_copy.start()
     low, high = halos(up_ref, down_ref, 0, half)
     lay(s0, 0, low)
     lay(s0, planes + 1, high)
     for p in range(planes):
         lay(s0, 1 + p, rows_of(inner_ref, p, half))
-    middle = grad_ref.shape[0] // 2
-    join_planes([rows_of(top_ref, p, half) for p in range(planes)], join_ref[...], grad_ref, 0)
-    top_copy = pltpu.make_async_copy(grad_ref.at[:middle], grad_hbm.at[:middle], sems.at[2])
-    top_copy.start()
-    terms = convs(s0, 1, planes, tf_ref)
-    lows = [(rows_of(low_ref, p, half) + term).astype(BF16) for p, term in enumerate(terms)]
-    join_planes(lows, join_ref[...], grad_ref, middle)
-    low_copy = pltpu.make_async_copy(grad_ref.at[middle:], grad_hbm.at[middle:], sems.at[3])
+    lows = [(rows_of(low_ref, p, half) + conv(s0, 1 + p, tf_ref)).astype(BF16) for p in range(planes)]
+    join_planes(lows, join_ref[...], grad_ref, 0)
+    low_copy = pltpu.make_async_copy(grad_ref, grad_hbm.at[middle:], sems.at[3])
     low_copy.start()
     fwd_copy.wait()
     state_copy.wait()
@@ -362,7 +356,8 @@
     low_copy.wait()
 
 
-def pack_state(half, planes, state_ref, join_ref, out_ref):
+def pack_state(half, planes, state_ref, top_ref, join_ref, out_ref, out_top_ref):
+    join_planes([rows_of(top_ref, p, half) for p in range(planes)], join_ref[...], out_top_ref, 0)
     for h in range(2):
         values = [rows_of(state_ref, h * planes + p, half) for p in range(planes)]
         join_planes(values, join_ref[...], out_ref, h * out_ref.shape[0] // 2)
@@ -428,10 +423,8 @@
 
     unit = 2 * 9 * half * 3 * half * cells
     raw_shape = ((chans * planes * cells // LANES, LANES), BF16)
-    *weights, split, join = call(
-        functools.partial(prepare, planes, cells),
-        [((6 * half, 12 * half), BF16)] * (4 * PAIRS) + [((256, 256), BF16)] * 2, [], 40 * unit, couplings,
-    )
+    split, join = call(functools.partial(matrices, planes, cells), [((256, 256), BF16)] * 2, [], 40 * unit)
+    weights = call(prepare, [((3 * half, 9 * half), BF16)] * (4 * PAIRS), [], 40 * unit, couplings, split)
     direct, turned = weights[: 2 * PAIRS], weights[2 * PAIRS :]
 
     sizes = (half, planes, cells)
@@ -481,11 +474,14 @@
         functools.partial(forward_second, half, planes), [raw_shape], [wide, near], 6 * unit,
         mid, low_own, fu, fd, direct[2], direct[3], join,
     )
-    (state_raw,) = call(functools.partial(pack_state, half, planes), [raw_shape], [], unit, state, join)
+    half_raw = ((raw_shape[0][0] // 2, LANES), BF16)
+    state_raw, top_raw = call(
+        functools.partial(pack_state, half, planes), [raw_shape, half_raw], [], unit, state, top, join
+    )
     fwd_raw, state_raw, grad_raw = call(
         functools.partial(backward_third, half, planes), [raw_shape] * 3,
-        [near, raw_shape[0], pltpu.SemaphoreType.DMA((4,))], 2 * unit,
-        inner, iu, id_, low, top, turned[0], join, fwd_raw, state_raw, far_out=True,
+        [near, half_raw[0], pltpu.SemaphoreType.DMA((4,))], 2 * unit,
+        inner, iu, id_, low, top_raw, turned[0], join, fwd_raw, state_raw, far_out=True,
     )
     shape = (chans, planes, cells)
     return from_raw(fwd_raw, *shape), from_raw(state_raw, *shape), from_raw(grad_raw, *shape)

time: 45.9 us -> 45.2 us (0.985); the launches traced: 45 us -> 45.1 us
  waiting for transfers between devices: 13 us -> 16.5 us
  local copies, waits for them, and re-layouts: 2.69 us -> 1.17 us
  Pallas kernels: 12.8 us -> 11.6 us
  starting transfers between devices: 15.8 us -> 15 us
    ppermute x4, waiting for transfers between devices: 1.22 us -> 3.42 us  [along(): lax.ppermute(value, 'section', [(s, (s + step) % sections) for s in range...]
    ppermute x6, waiting for transfers between devices: 1.72 us -> 3.38 us  [swap(): from_down = lax.ppermute(down, ('section', 'slab'), behind)]
    unnamed x10, local copies, waits for them, and re-layouts: 1.54 us -> 0.02 us
    pallas_call x11 -> x12, Pallas kernels: 12.8 us -> 11.6 us  [call(): pl.pallas_call(body, out_shape=[jax.ShapeDtypeStruct(shape, dtype) for sh...]
    ppermute x6, starting transfers between devices: 11.6 us -> 10.6 us  [swap(): from_up = lax.ppermute(up, ('section', 'slab'), ahead)]
  transfers between devices with their start and end apart: 16 -> 16, of which waited for: 6 -> 8; matrix products, arithmetic and copies ran while one was open for 0% -> 3% of each run, Pallas kernels for 25% -> 22%
where the time goes in v3:
time: 45.2 us; the launch traced here: 45.1 us
  waiting for transfers between devices  16.5 us (37%)
  starting transfers between devices  15 us (33%)
  Pallas kernels  11.6 us (26%)
  local copies, waits for them, and re-layouts  1.17 us (3%)
  between operations  0.79 us (2%)
    pallas_call x12, Pallas kernels, call(): pl.pallas_call(body, out_shape=[jax.ShapeDtypeStruct(shape, dtype) for sh...  11.6 us
    ppermute x6, starting transfers between devices, swap(): from_up = lax.ppermute(up, ('section', 'slab'), ahead)  10.6 us
    ppermute x6, waiting for transfers between devices, swap(): from_up = lax.ppermute(up, ('section', 'slab'), ahead)  9.69 us
    ppermute x4, starting transfers between devices, along(): lax.ppermute(value, 'section', [(s, (s + step) % sections) for s in range...  4.3 us
    ppermute x4, waiting for transfers between devices, along(): lax.ppermute(value, 'section', [(s, (s + step) % sections) for s in range...  3.42 us
    ppermute x6, waiting for transfers between devices, swap(): from_down = lax.ppermute(down, ('section', 'slab'), behind)  3.38 us
    slice x1, local copies, waits for them, and re-layouts, shards(): grads_low, grads_high = (grads[middle:], grads[:middle])  1.15 us
  transfers between devices with their start and end apart: 16, of which 8 were waited for; matrix products, arithmetic and copies ran while one was open for 3% of the time, Pallas kernels for 22%

profile of v3, /device:TPU:0, one launch (start us, length us, event | category | flops | bytes accessed | tf_op | source)
XLA Modules:
  0.0 45.1 jit_solution(5649243165460871851)
XLA Ops:
  0.6 3.4 %collective-permute-start = (bf16[1024,128]{1,0:T(8,128)(2,1)}, bf16[1024,128]{1,0:T(8,128)(2,1)S(1)}, u32[]{:S(2)}, u32[]{:S(2)}) collective-permute-start(bf16[1024,128]{1,0:T(8,128)(2,1)} %bitcast.52), channel_id=1, source_target_pairs={{0,28},{4,0},{8,4},{12,8},{16,12},{20,16},{24,20},{28,24},{1,29},{... | collective-permute-start | bytes 786440 | tf_op jit(solution)/shard_map/ppermute | solution.py:410
  4.0 1.1 %fusion = (bf16[64,4,2,128]{3,2,1,0:T(2,128)(2,1)S(1)}, bf16[64,4,2,128]{3,2,1,0:T(2,128)(2,1)S(1)}) fusion(bf16[128,4,2,128]{3,2,1,0:T(2,128)(2,1)} %bitcast.49), kind=kLoop, calls=%fused_computation | loop fusion | bytes 524288 | tf_op jit(solution)/shard_map/slice | solution.py:415
  5.2 0.7 %collective-permute-start.2 = (bf16[512,128]{1,0:T(8,128)(2,1)S(1)}, bf16[512,128]{1,0:T(8,128)(2,1)S(1)}, u32[]{:S(2)}, u32[]{:S(2)}) collective-permute-start(bf16[512,128]{1,0:T(8,128)(2,1)S(1)} %bitcast.51), channel_id=1, source_target_pairs={{0,28},{4,0},{8,4},{12,8},{16,12},{20,16},{24,20},{28,24},{1,29},{... | collective-permute-start | bytes 393224 | tf_op jit(solution)/shard_map/ppermute | solution.py:410
  5.9 0.0 copy-start
  5.9 0.0 copy-start.4
  5.9 0.0 copy-start.1
  5.9 0.0 copy-start.3
  5.9 0.1 collective-permute-start.1
  6.0 0.1 shard_map.94
  6.1 3.4 %collective-permute-done.2.got_ref = bf16[512,128]{1,0:T(8,128)(2,1)S(1)} collective-permute-done((bf16[512,128]{1,0:T(8,128)(2,1)S(1)}, bf16[512,128]{1,0:T(8,128)(2,1)S(1)}, u32[]{:S(2)}, u32[]{:S(2)}) %collective-permute-start.2) | collective-permute-done | bytes 131104 | tf_op jit(solution)/shard_map/ppermute | solution.py:410
  9.6 0.0 copy-done
  9.6 0.2 shard_map.97
  9.8 1.6 %collective-permute-start.5 = (bf16[64,512]{1,0:T(8,128)(2,1)S(1)}, bf16[64,512]{1,0:T(8,128)(2,1)S(1)}, u32[]{:S(2)}, u32[]{:S(2)}) collective-permute-start(bf16[64,512]{1,0:T(8,128)(2,1)S(1)} %get-tuple-element.47), channel_id=1, source_target_pairs={{0,1},{1,2},{2,3},{3,7},{7,6},{6,5},{5,4},{4,0},{8,9},{9,10},{10,1... | collective-permute-start | bytes 196616 | tf_op jit(solution)/shard_map/ppermute | solution.py:405
  11.4 0.0 collective-permute-start.6
  11.4 0.0 collective-permute-done.got_ref
  11.4 0.0 copy-done.4
  11.4 0.1 collective-permute-start.11
  11.4 0.0 copy-done.1
  11.4 0.3 shard_map.95
  11.7 2.0 %collective-permute-start.3 = (bf16[192,512]{1,0:T(8,128)(2,1)S(1)}, bf16[192,512]{1,0:T(8,128)(2,1)S(1)}, u32[]{:S(2)}, u32[]{:S(2)}) collective-permute-start(bf16[192,512]{1,0:T(8,128)(2,1)S(1)} %get-tuple-element.45), channel_id=1, source_target_pairs={{0,1},{1,2},{2,3},{3,7},{7,6},{6,5},{5,4},{4,0},{8,9},{9,10},{10,1... | collective-permute-start | bytes 589832 | tf_op jit(solution)/shard_map/ppermute | solution.py:405
  13.7 0.0 collective-permute-done.1.got_ref
  13.7 0.0 collective-permute-start.4
  13.7 0.0 copy-done.3
  13.7 1.1 %shard_map.98 = (bf16[192,576]{1,0:T(8,128)(2,1)S(1)}, bf16[192,576]{1,0:T(8,128)(2,1)S(1)}, bf16[192,576]{1,0:T(8,128)(2,1)S(1)}, bf16[192,576]{1,0:T(8,128)(2,...) custom-call(bf16[1,4,27,64,64]{4,3,2,1,0:T(8,128)(2,1)S(1)} %copy-do, ...), custom_call_target="tpu_custom_call" | custom-call | flops 4529848320 | bytes 1048576 | tf_op jit(solution)/shard_map/pallas_call | solution.py:368
  14.8 0.2 shard_map.96.g1_ref
  15.0 0.0 copy-start.2
  15.0 0.0 collective-permute-done.5.gu_ref
  15.1 1.1 %collective-permute-done.6.gd_ref = bf16[64,512]{1,0:T(8,128)(2,1)S(1)} collective-permute-done((bf16[64,512]{1,0:T(8,128)(2,1)S(1)}, bf16[64,512]{1,0:T(8,128)(2,1)S(1)}, u32[]{:S(2)}, u32[]{:S(2)}) %collective-permute-start.6) | collective-permute-done | bytes 65568 | tf_op jit(solution)/shard_map/ppermute | solution.py:406
  16.2 2.3 %collective-permute-done.3.yu_ref = bf16[192,512]{1,0:T(8,128)(2,1)S(1)} collective-permute-done((bf16[192,512]{1,0:T(8,128)(2,1)S(1)}, bf16[192,512]{1,0:T(8,128)(2,1)S(1)}, u32[]{:S(2)}, u32[]{:S(2)}) %collective-permute-start.3) | collective-permute-done | bytes 196640 | tf_op jit(solution)/shard_map/ppermute | solution.py:405
  18.5 1.3 %collective-permute-done.4.yd_ref = bf16[192,512]{1,0:T(8,128)(2,1)S(1)} collective-permute-done((bf16[192,512]{1,0:T(8,128)(2,1)S(1)}, bf16[192,512]{1,0:T(8,128)(2,1)S(1)}, u32[]{:S(2)}, u32[]{:S(2)}) %collective-permute-start.4) | collective-permute-done | bytes 196640 | tf_op jit(solution)/shard_map/ppermute | solution.py:406
  19.8 2.0 %shard_map.99 = (bf16[256,512]{1,0:T(8,128)(2,1)S(1)}, bf16[256,512]{1,0:T(8,128)(2,1)S(1)}, bf16[256,512]{1,0:T(8,128)(2,1)S(1)}, f32[128,512]{1,0:T(8,128)S(1)}) custom-call(bf16[256,512]{1,0:T(8,128)(2,1)S(1)} %get-tuple-element.43.y_ref, bf16[128,512]{1,0:T(8,128)(2,1)S(1)} %shard_map.96.g1_ref, bf16[128,512]{1,0:T(8,128)(2,1)S(1)} %get-tuple-element.44.g2_ref, ...), custom_call_target="tpu_custom_call" | custom-call | flops 905969664 | bytes 1048576 | tf_op jit(solution)/shard_map/pallas_call | solution.py:368
  21.8 1.2 %collective-permute-start.7 = (bf16[256,512]{1,0:T(8,128)(2,1)S(1)}, bf16[256,512]{1,0:T(8,128)(2,1)S(1)}, u32[]{:S(2)}, u32[]{:S(2)}) collective-permute-start(bf16[256,512]{1,0:T(8,128)(2,1)S(1)} %get-tuple-element.52.mine_ref), channel_id=1, source_target_pairs={{0,1},{1,2},{2,3},{3,7},{7,6},{6,5},{5,4},{4,0},{8,9},{9,10},{10,1... | collective-permute-start | bytes 786440 | tf_op jit(solution)/shard_map/ppermute | solution.py:405
  23.0 0.0 collective-permute-start.8
  23.0 0.0 collective-permute-done.11.got_ref
  23.0 0.0 copy-done.2
  23.0 0.3 shard_map.102
  23.3 2.0 %collective-permute-start.12 = (bf16[192,512]{1,0:T(8,128)(2,1)S(1)}, bf16[192,512]{1,0:T(8,128)(2,1)S(1)}, u32[]{:S(2)}, u32[]{:S(2)}) collective-permute-start(bf16[192,512]{1,0:T(8,128)(2,1)S(1)} %get-tuple-element.71), channel_id=1, source_target_pairs={{0,1},{1,2},{2,3},{3,7},{7,6},{6,5},{5,4},{4,0},{8,9},{9,10},{10,1... | collective-permute-start | bytes 589832 | tf_op jit(solution)/shard_map/ppermute | solution.py:405
  25.3 0.0 collective-permute-start.13
  25.3 7.3 %collective-permute-done.12.up_ref = bf16[192,512]{1,0:T(8,128)(2,1)S(1)} collective-permute-done((bf16[192,512]{1,0:T(8,128)(2,1)S(1)}, bf16[192,512]{1,0:T(8,128)(2,1)S(1)}, u32[]{:S(2)}, u32[]{:S(2)}) %collective-permute-start.12) | collective-permute-done | bytes 196640 | tf_op jit(solution)/shard_map/ppermute | solution.py:405
  32.7 0.7 %collective-permute-done.13.down_ref = bf16[192,512]{1,0:T(8,128)(2,1)S(1)} collective-permute-done((bf16[192,512]{1,0:T(8,128)(2,1)S(1)}, bf16[192,512]{1,0:T(8,128)(2,1)S(1)}, u32[]{:S(2)}, u32[]{:S(2)}) %collective-permute-start.13) | collective-permute-done | bytes 196640 | tf_op jit(solution)/shard_map/ppermute | solution.py:406
  33.4 1.5 %shard_map.103 = (bf16[256,512]{1,0:T(8,128)(2,1)S(1)}, bf16[128,512]{1,0:T(8,128)(2,1)S(1)}) custom-call(bf16[256,512]{1,0:T(8,128)(2,1)S(1)} %get-tuple-element.70.own_ref, bf16[192,512]{1,0:T(8,128)(2,1)S(1)} %collective-permute-done.12.up_ref, bf16[192,512]{1,0:T(8,128)(2,1)S(1)} %collective-permute-done.13.down_ref, ...), custom_call_target="tpu_custom_call" | custom-call | flops 679477248 | bytes 1048576 | tf_op jit(solution)/shard_map/pallas_call | solution.py:368
  34.9 1.8 %collective-permute-start.14 = (bf16[128,512]{1,0:T(8,128)(2,1)S(1)}, bf16[128,512]{1,0:T(8,128)(2,1)S(1)}, u32[]{:S(2)}, u32[]{:S(2)}) collective-permute-start(bf16[128,512]{1,0:T(8,128)(2,1)S(1)} %get-tuple-element.74.own_ref), channel_id=1, source_target_pairs={{0,1},{1,2},{2,3},{3,7},{7,6},{6,5},{5,4},{4,0},{8,9},{9,10},{10,1... | collective-permute-start | bytes 393224 | tf_op jit(solution)/shard_map/ppermute | solution.py:405
  36.7 0.0 collective-permute-start.15
  36.7 0.0 collective-permute-done.7.up_ref
  36.7 0.0 collective-permute-done.8.down_ref
  36.7 2.5 %shard_map.100 = (bf16[256,512]{1,0:T(8,128)(2,1)S(1)}, bf16[128,512]{1,0:T(8,128)(2,1)S(1)}, f32[128,512]{1,0:T(8,128)S(1)}, bf16[128,512]{1,0:T(8,128)(2,1)S(1...) custom-call(bf16[256,512]{1,0:T(8,128)(2,1)S(1)} %get-tuple-element.52.mine_ref, ...), custom_call_target="tpu_custom_call" | custom-call | flops 1358954496 | bytes 1048576 | tf_op jit(solution)/shard_map/pallas_call | solution.py:368
  39.2 0.0 collective-permute-start.10
  39.3 2.0 %collective-permute-start.9 = (bf16[64,512]{1,0:T(8,128)(2,1)S(1)}, bf16[64,512]{1,0:T(8,128)(2,1)S(1)}, u32[]{:S(2)}, u32[]{:S(2)}) collective-permute-start(bf16[64,512]{1,0:T(8,128)(2,1)S(1)} %get-tuple-element.61), channel_id=1, source_target_pairs={{0,1},{1,2},{2,3},{3,7},{7,6},{6,5},{5,4},{4,0},{8,9},{9,10},{10,1... | collective-permute-start | bytes 196616 | tf_op jit(solution)/shard_map/ppermute | solution.py:405
  41.3 0.3 shard_map.101
  41.6 0.0 collective-permute-done.14.up_ref
  41.6 0.1 collective-permute-done.15.down_ref
  41.7 1.7 %shard_map.104.fwd_ref = bf16[1024,128]{1,0:T(8,128)(2,1)S(1)} custom-call(bf16[256,512]{1,0:T(8,128)(2,1)S(1)} %get-tuple-element.73.mid_ref, bf16[128,512]{1,0:T(8,128)(2,1)S(1)} %get-tuple-element.74.own_ref, bf16[128,512]{1,0:T(8,128)(2,1)S(1)} %collective-permute-done.14.up_ref, bf16[128,512]{1,0:T(8,128)(2,1)S(1)} %collective-permute-done.15.down_ref, ...), custom_call_target="tpu_custom_call" | custom-call | flops 679477248 | bytes 1048576 | tf_op jit(solution)/shard_map/pallas_call | solution.py:368
  43.4 0.1 collective-permute-done.10.down_ref
  43.5 0.0 collective-permute-done.9.up_ref
  43.5 1.5 %shard_map.105 = (bf16[1024,128]{1,0:T(8,128)(2,1)}, bf16[1024,128]{1,0:T(8,128)(2,1)}, bf16[1024,128]{1,0:T(8,128)(2,1)}) custom-call(bf16[128,512]{1,0:T(8,128)(2,1)S(1)} %get-tuple-element.60.inner_ref, bf16[64,512]{1,0:T(8,128)(2,1)S(1)} %collective-permute-done.9.up_ref, bf16[64,512]{1,0:T(8,128)(2,1)S(1)} %collective-permute-done.10.down_ref, ...), custom_call_target="tpu_custom_call" | custom-call | flops 226492416 | bytes 1048576 | tf_op jit(solution)/shard_map/pallas_call | solution.py:368
Async XLA Ops:
  0.6 10.7 %collective-permute-start = (bf16[1024,128]{1,0:T(8,128)(2,1)}, bf16[1024,128]{1,0:T(8,128)(2,1)S(1)}, u32[]{:S(2)}, u32[]{:S(2)}) collective-permute-start(bf16[1024,128]{1,0:T(8,128)(2,1)} %bitcast.52), channel_id=1, source_target_pairs={{0,28},{4,0},{8,4},{12,8},{16,12},{20,16},{24,20},{28,24},{1,29},{... | collective-permute-start | bytes 786440 | tf_op jit(solution)/shard_map/ppermute | solution.py:410
  5.2 4.4 %collective-permute-start.2 = (bf16[512,128]{1,0:T(8,128)(2,1)S(1)}, bf16[512,128]{1,0:T(8,128)(2,1)S(1)}, u32[]{:S(2)}, u32[]{:S(2)}) collective-permute-start(bf16[512,128]{1,0:T(8,128)(2,1)S(1)} %bitcast.51), channel_id=1, source_target_pairs={{0,28},{4,0},{8,4},{12,8},{16,12},{20,16},{24,20},{28,24},{1,29},{... | collective-permute-start | bytes 393224 | tf_op jit(solution)/shard_map/ppermute | solution.py:410
  5.9 3.6 %copy-start = (bf16[128,2,512]{2,1,0:T(2,128)(2,1)S(1)}, bf16[128,2,512]{2,1,0:T(2,128)(2,1)}, u32[]{:S(2)}) copy-start(bf16[128,2,512]{2,1,0:T(2,128)(2,1)} %param.12) | copy-start | bytes 786436
  5.9 5.4 %copy-start.4 = (bf16[1,128,2,512]{3,2,1,0:T(2,128)(2,1)S(1)}, bf16[1,128,2,512]{3,2,1,0:T(2,128)(2,1)}, u32[]{:S(2)}) copy-start(bf16[1,128,2,512]{3,2,1,0:T(2,128)(2,1)} %param.7) | copy-start | bytes 786436
  5.9 5.5 %copy-start.1 = (bf16[128,2,512]{2,1,0:T(2,128)(2,1)S(1)}, bf16[128,2,512]{2,1,0:T(2,128)(2,1)}, u32[]{:S(2)}) copy-start(bf16[128,2,512]{2,1,0:T(2,128)(2,1)} %param.11) | copy-start | bytes 786436
  5.9 7.8 %copy-start.3 = (bf16[1,4,27,64,64]{4,3,2,1,0:T(8,128)(2,1)S(1)}, bf16[1,4,27,64,64]{4,3,2,1,0:T(8,128)(2,1)}, u32[]{:S(2)}) copy-start(bf16[1,4,27,64,64]{4,3,2,1,0:T(8,128)(2,1)} %kernels_ref.1) | copy-start | bytes 2654212
  5.9 7.8 %collective-permute-start.1 = (bf16[512,128]{1,0:T(8,128)(2,1)S(1)}, bf16[512,128]{1,0:T(8,128)(2,1)S(1)}, u32[]{:S(2)}, u32[]{:S(2)}) collective-permute-start(bf16[512,128]{1,0:T(8,128)(2,1)S(1)} %bitcast.50), channel_id=1, source_target_pairs={{0,28},{4,0},{8,4},{12,8},{16,12},{20,16},{24,20},{28,24},{1,29},{... | collective-permute-start | bytes 393224 | tf_op jit(solution)/shard_map/ppermute | solution.py:410
  9.8 5.3 %collective-permute-start.5 = (bf16[64,512]{1,0:T(8,128)(2,1)S(1)}, bf16[64,512]{1,0:T(8,128)(2,1)S(1)}, u32[]{:S(2)}, u32[]{:S(2)}) collective-permute-start(bf16[64,512]{1,0:T(8,128)(2,1)S(1)} %get-tuple-element.47), channel_id=1, source_target_pairs={{0,1},{1,2},{2,3},{3,7},{7,6},{6,5},{5,4},{4,0},{8,9},{9,10},{10,1... | collective-permute-start | bytes 196616 | tf_op jit(solution)/shard_map/ppermute | solution.py:405
  11.4 4.8 %collective-permute-start.6 = (bf16[64,512]{1,0:T(8,128)(2,1)S(1)}, bf16[64,512]{1,0:T(8,128)(2,1)S(1)}, u32[]{:S(2)}, u32[]{:S(2)}) collective-permute-start(bf16[64,512]{1,0:T(8,128)(2,1)S(1)} %get-tuple-element.48), channel_id=1, source_target_pairs={{1,0},{2,1},{3,2},{7,3},{6,7},{5,6},{4,5},{0,4},{9,8},{10,9},{11,1... | collective-permute-start | bytes 196616 | tf_op jit(solution)/shard_map/ppermute | solution.py:406
  11.4 11.7 %collective-permute-start.11 = (bf16[1024,128]{1,0:T(8,128)(2,1)S(1)}, bf16[1024,128]{1,0:T(8,128)(2,1)S(1)}, u32[]{:S(2)}, u32[]{:S(2)}) collective-permute-start(bf16[1024,128]{1,0:T(8,128)(2,1)S(1)} %bitcast.53), channel_id=1, source_target_pairs={{0,4},{4,8},{8,12},{12,16},{16,20},{20,24},{24,28},{28,0},{1,5},{5... | collective-permute-start | bytes 786440 | tf_op jit(solution)/shard_map/ppermute | solution.py:410
  11.7 6.8 %collective-permute-start.3 = (bf16[192,512]{1,0:T(8,128)(2,1)S(1)}, bf16[192,512]{1,0:T(8,128)(2,1)S(1)}, u32[]{:S(2)}, u32[]{:S(2)}) collective-permute-start(bf16[192,512]{1,0:T(8,128)(2,1)S(1)} %get-tuple-element.45), channel_id=1, source_target_pairs={{0,1},{1,2},{2,3},{3,7},{7,6},{6,5},{5,4},{4,0},{8,9},{9,10},{10,1... | collective-permute-start | bytes 589832 | tf_op jit(solution)/shard_map/ppermute | solution.py:405
  13.7 6.1 %collective-permute-start.4 = (bf16[192,512]{1,0:T(8,128)(2,1)S(1)}, bf16[192,512]{1,0:T(8,128)(2,1)S(1)}, u32[]{:S(2)}, u32[]{:S(2)}) collective-permute-start(bf16[192,512]{1,0:T(8,128)(2,1)S(1)} %get-tuple-element.46), channel_id=1, source_target_pairs={{1,0},{2,1},{3,2},{7,3},{6,7},{5,6},{4,5},{0,4},{9,8},{10,9},{11,1... | collective-permute-start | bytes 589832 | tf_op jit(solution)/shard_map/ppermute | solution.py:406
  15.0 8.0 %copy-start.2 = (bf16[128,2,512]{2,1,0:T(2,128)(2,1)S(1)}, bf16[128,2,512]{2,1,0:T(2,128)(2,1)}, u32[]{:S(2)}) copy-start(bf16[128,2,512]{2,1,0:T(2,128)(2,1)} %param.10) | copy-start | bytes 786436
  21.8 14.9 %collective-permute-start.7 = (bf16[256,512]{1,0:T(8,128)(2,1)S(1)}, bf16[256,512]{1,0:T(8,128)(2,1)S(1)}, u32[]{:S(2)}, u32[]{:S(2)}) collective-permute-start(bf16[256,512]{1,0:T(8,128)(2,1)S(1)} %get-tuple-element.52.mine_ref), channel_id=1, source_target_pairs={{0,1},{1,2},{2,3},{3,7},{7,6},{6,5},{5,4},{4,0},{8,9},{9,10},{10,1... | collective-permute-start | bytes 786440 | tf_op jit(solution)/shard_map/ppermute | solution.py:405
  23.0 13.7 %collective-permute-start.8 = (bf16[256,512]{1,0:T(8,128)(2,1)S(1)}, bf16[256,512]{1,0:T(8,128)(2,1)S(1)}, u32[]{:S(2)}, u32[]{:S(2)}) collective-permute-start(bf16[256,512]{1,0:T(8,128)(2,1)S(1)} %get-tuple-element.52.mine_ref), channel_id=1, source_target_pairs={{1,0},{2,1},{3,2},{7,3},{6,7},{5,6},{4,5},{0,4},{9,8},{10,9},{11,1... | collective-permute-start | bytes 786440 | tf_op jit(solution)/shard_map/ppermute | solution.py:406
  23.3 9.4 %collective-permute-start.12 = (bf16[192,512]{1,0:T(8,128)(2,1)S(1)}, bf16[192,512]{1,0:T(8,128)(2,1)S(1)}, u32[]{:S(2)}, u32[]{:S(2)}) collective-permute-start(bf16[192,512]{1,0:T(8,128)(2,1)S(1)} %get-tuple-element.71), channel_id=1, source_target_pairs={{0,1},{1,2},{2,3},{3,7},{7,6},{6,5},{5,4},{4,0},{8,9},{9,10},{10,1... | collective-permute-start | bytes 589832 | tf_op jit(solution)/shard_map/ppermute | solution.py:405
  25.3 8.0 %collective-permute-start.13 = (bf16[192,512]{1,0:T(8,128)(2,1)S(1)}, bf16[192,512]{1,0:T(8,128)(2,1)S(1)}, u32[]{:S(2)}, u32[]{:S(2)}) collective-permute-start(bf16[192,512]{1,0:T(8,128)(2,1)S(1)} %get-tuple-element.72), channel_id=1, source_target_pairs={{1,0},{2,1},{3,2},{7,3},{6,7},{5,6},{4,5},{0,4},{9,8},{10,9},{11,1... | collective-permute-start | bytes 589832 | tf_op jit(solution)/shard_map/ppermute | solution.py:406
  34.9 6.6 %collective-permute-start.14 = (bf16[128,512]{1,0:T(8,128)(2,1)S(1)}, bf16[128,512]{1,0:T(8,128)(2,1)S(1)}, u32[]{:S(2)}, u32[]{:S(2)}) collective-permute-start(bf16[128,512]{1,0:T(8,128)(2,1)S(1)} %get-tuple-element.74.own_ref), channel_id=1, source_target_pairs={{0,1},{1,2},{2,3},{3,7},{7,6},{6,5},{5,4},{4,0},{8,9},{9,10},{10,1... | collective-permute-start | bytes 393224 | tf_op jit(solution)/shard_map/ppermute | solution.py:405
  36.7 5.0 %collective-permute-start.15 = (bf16[128,512]{1,0:T(8,128)(2,1)S(1)}, bf16[128,512]{1,0:T(8,128)(2,1)S(1)}, u32[]{:S(2)}, u32[]{:S(2)}) collective-permute-start(bf16[128,512]{1,0:T(8,128)(2,1)S(1)} %get-tuple-element.74.own_ref), channel_id=1, source_target_pairs={{1,0},{2,1},{3,2},{7,3},{6,7},{5,6},{4,5},{0,4},{9,8},{10,9},{11,1... | collective-permute-start | bytes 393224 | tf_op jit(solution)/shard_map/ppermute | solution.py:406
  39.2 4.3 %collective-permute-start.10 = (bf16[64,512]{1,0:T(8,128)(2,1)S(1)}, bf16[64,512]{1,0:T(8,128)(2,1)S(1)}, u32[]{:S(2)}, u32[]{:S(2)}) collective-permute-start(bf16[64,512]{1,0:T(8,128)(2,1)S(1)} %get-tuple-element.62), channel_id=1, source_target_pairs={{1,0},{2,1},{3,2},{7,3},{6,7},{5,6},{4,5},{0,4},{9,8},{10,9},{11,1... | collective-permute-start | bytes 196616 | tf_op jit(solution)/shard_map/ppermute | solution.py:406
  39.3 4.3 %collective-permute-start.9 = (bf16[64,512]{1,0:T(8,128)(2,1)S(1)}, bf16[64,512]{1,0:T(8,128)(2,1)S(1)}, u32[]{:S(2)}, u32[]{:S(2)}) collective-permute-start(bf16[64,512]{1,0:T(8,128)(2,1)S(1)} %get-tuple-element.61), channel_id=1, source_target_pairs={{0,1},{1,2},{2,3},{3,7},{7,6},{6,5},{5,4},{4,0},{8,9},{9,10},{10,1... | collective-permute-start | bytes 196616 | tf_op jit(solution)/shard_map/ppermute | solution.py:405

commit v4 on v3

--- a/solution.py
+++ b/solution.py
@@ -174,18 +174,15 @@
     down_ref[base : base + half, :] = pick(odd, other[planes - 1], other[0])
 
 
-def unpack_grad(part, half, planes, cells, got_ref, edge_ref, matrix_ref, own_ref, *send_refs):
+def unpack_grad(half, planes, cells, got_ref, edge_ref, matrix_ref, own_ref, up_ref, down_ref):
     at_edge = lax.axis_index("section") == lax.axis_size("section") - 1
-    rows = got_ref.shape[0]
-    raw = pick(at_edge, edge_ref[part * rows : (part + 1) * rows, :], got_ref[...])
+    raw = pick(at_edge, edge_ref[got_ref.shape[0] :, :], got_ref[...])
     (parts,) = split_planes(raw, matrix_ref[...], half, planes, cells)
     for p in range(planes):
         own_ref[p * half : (p + 1) * half, :] = parts[p]
-    if send_refs:
-        up_ref, down_ref = send_refs
-        odd = is_odd()
-        up_ref[...] = pick(odd, parts[0], parts[planes - 1])
-        down_ref[...] = pick(odd, parts[planes - 1], parts[0])
+    odd = is_odd()
+    up_ref[...] = pick(odd, parts[0], parts[planes - 1])
+    down_ref[...] = pick(odd, parts[planes - 1], parts[0])
 
 
 def halos(up_ref, down_ref, index, half):
@@ -255,8 +252,8 @@
 
 
 def backward_first(
-    half, planes, y_ref, g1_ref, g2_ref, yu_ref, yd_ref, gu_ref, gd_ref, wg_ref, wf_ref, tg_ref,
-    send_ref, second_ref, low_grad_ref, carry_ref, s0, s1, s2,
+    half, planes, y_ref, g2_ref, yu_ref, yd_ref, gu_ref, gd_ref, wg_ref, wf_ref, tg_ref,
+    first_ref, slope_ref, term_ref, second_ref, low_grad_ref, s0, s1, s2,
 ):
     has_low, has_high = slab_place()
     for p in range(planes):
@@ -281,10 +278,24 @@
         lay(s2, j, inner)
     for p in range(planes):
         z = conv(s1, 1 + p, wf_ref)
-        carry = rows_of(g1_ref, p, half).astype(F32) + conv(s2, 1 + p, tg_ref)
-        first, inner = turn(z, rows_of(y_ref, p, half), carry)
+        term_ref[p * half : (p + 1) * half, :] = conv(s2, 1 + p, tg_ref)
+        sig = sigmoid(z)
+        first = (rows_of(y_ref, p, half).astype(F32) - z * sig).astype(BF16)
+        first_ref[p * half : (p + 1) * half, :] = first
+        slope_ref[p * half : (p + 1) * half, :] = sig * (1.0 + z * (1.0 - sig))
+
+
+def backward_carry(
+    half, planes, cells, got_ref, edge_ref, matrix_ref, first_ref, slope_ref, term_ref, send_ref, carry_ref
+):
+    at_edge = lax.axis_index("section") == lax.axis_size("section") - 1
+    raw = pick(at_edge, edge_ref[: got_ref.shape[0], :], got_ref[...])
+    (grads,) = split_planes(raw, matrix_ref[...], half, planes, cells)
+    for p in range(planes):
+        carry = grads[p].astype(F32) + rows_of(term_ref, p, half)
         carry_ref[p * half : (p + 1) * half, :] = carry
-        send_ref[p * half : (p + 1) * half, :] = first
+        send_ref[p * half : (p + 1) * half, :] = rows_of(first_ref, p, half)
+        inner = (rows_of(slope_ref, p, half) * carry).astype(BF16)
         send_ref[(planes + p) * half : (planes + p + 1) * half, :] = inner
 
 
@@ -433,12 +444,8 @@
         [planes_of(2 * planes), planes_of(planes + 1), planes_of(planes + 1)], [], unit, got_y, raw_view(head_state), split,
     )
     g2_own, g_up, g_down = call(
-        functools.partial(unpack_grad, 1, *sizes),
+        functools.partial(unpack_grad, *sizes),
         [planes_of(planes), planes_of(1), planes_of(1)], [], unit, got_g2, raw_view(head_grad), split,
-    )
-    (g1_own,) = call(
-        functools.partial(unpack_grad, 0, *sizes), [planes_of(planes)], [], unit,
-        got_g1, raw_view(head_grad), split,
     )
     x_own, x_up, x_down = call(
         functools.partial(unpack_state, False, 1, *sizes),
@@ -450,11 +457,15 @@
 
     wide = ((3 * planes) * 3 * half, cells)
     near = ((planes + 2) * 3 * half, cells)
-    send, second, low_grad, carry = call(
+    first, slope, term, second, low_grad = call(
         functools.partial(backward_first, half, planes),
-        [planes_of(2 * planes), planes_of(planes + 2), planes_of(planes + 2), planes_of(planes, F32)],
+        [planes_of(planes), planes_of(planes, F32), planes_of(planes, F32), planes_of(planes + 2), planes_of(planes + 2)],
         [wide, near, near], 8 * unit,
-        y_own, g1_own, g2_own, yu, yd, gu, gd, direct[3], direct[2], turned[3],
+        y_own, g2_own, yu, yd, gu, gd, direct[3], direct[2], turned[3],
+    )
+    send, carry = call(
+        functools.partial(backward_carry, *sizes), [planes_of(2 * planes), planes_of(planes, F32)], [],
+        unit, got_g1, raw_view(head_grad), split, first, slope, term,
     )
     su, sd = swap(send, send)
     mid, low_own = call(

time: 45.2 us -> 48.5 us (1.073)
  starting transfers between devices: 15 us -> 16.9 us
  waiting for transfers between devices: 16.5 us -> 17.8 us
    ppermute x6, waiting for transfers between devices: 3.38 us -> 5.5 us  [swap(): from_down = lax.ppermute(down, ('section', 'slab'), behind)]
    ppermute x4, starting transfers between devices: 4.3 us -> 5.5 us  [along(): lax.ppermute(value, 'section', [(s, (s + step) % sections) for s in range...]
    ppermute x6, waiting for transfers between devices: 9.69 us -> 8.76 us  [swap(): from_up = lax.ppermute(up, ('section', 'slab'), ahead)]
    ppermute x6, starting transfers between devices: 10.6 us -> 11.4 us  [swap(): from_up = lax.ppermute(up, ('section', 'slab'), ahead)]
  transfers between devices with their start and end apart: 16 -> 16, of which waited for: 8 -> 8; matrix products, arithmetic and copies ran while one was open for 3% -> 2% of each run, Pallas kernels for 22% -> 21%
where the time goes in v4:
time: 48.5 us; the launch traced here: 48.3 us
  waiting for transfers between devices  17.8 us (37%)
  starting transfers between devices  16.9 us (35%)
  Pallas kernels  11.7 us (24%)
  local copies, waits for them, and re-layouts  1.18 us (2%)
  between operations  0.81 us (2%)
    pallas_call x12, Pallas kernels, call(): pl.pallas_call(body, out_shape=[jax.ShapeDtypeStruct(shape, dtype) for sh...  11.7 us
    ppermute x6, starting transfers between devices, swap(): from_up = lax.ppermute(up, ('section', 'slab'), ahead)  11.4 us
    ppermute x6, waiting for transfers between devices, swap(): from_up = lax.ppermute(up, ('section', 'slab'), ahead)  8.76 us
    ppermute x6, waiting for transfers between devices, swap(): from_down = lax.ppermute(down, ('section', 'slab'), behind)  5.5 us
    ppermute x4, starting transfers between devices, along(): lax.ppermute(value, 'section', [(s, (s + step) % sections) for s in range...  5.5 us
    ppermute x4, waiting for transfers between devices, along(): lax.ppermute(value, 'section', [(s, (s + step) % sections) for s in range...  3.49 us
    slice x1, local copies, waits for them, and re-layouts, shards(): grads_low, grads_high = (grads[middle:], grads[:middle])  1.15 us
  transfers between devices with their start and end apart: 16, of which 8 were waited for; matrix products, arithmetic and copies ran while one was open for 2% of the time, Pallas kernels for 21%

profile of v4, /device:TPU:0, one launch (start us, length us, event | category | flops | bytes accessed | tf_op | source)
XLA Modules:
  0.0 48.3 jit_solution(13558164462836127286)
XLA Ops:
  0.6 3.4 %collective-permute-start.1 = (bf16[1024,128]{1,0:T(8,128)(2,1)}, bf16[1024,128]{1,0:T(8,128)(2,1)S(1)}, u32[]{:S(2)}, u32[]{:S(2)}) collective-permute-start(bf16[1024,128]{1,0:T(8,128)(2,1)} %bitcast.52), channel_id=1, source_target_pairs={{0,28},{4,0},{8,4},{12,8},{16,12},{20,16},{24,20},{28,24},{1,29},{... | collective-permute-start | bytes 786440 | tf_op jit(solution)/shard_map/ppermute | solution.py:421
  4.0 1.1 %fusion = (bf16[64,4,2,128]{3,2,1,0:T(2,128)(2,1)S(1)}, bf16[64,4,2,128]{3,2,1,0:T(2,128)(2,1)S(1)}) fusion(bf16[128,4,2,128]{3,2,1,0:T(2,128)(2,1)} %bitcast.49), kind=kLoop, calls=%fused_computation | loop fusion | bytes 524288 | tf_op jit(solution)/shard_map/slice | solution.py:426
  5.2 0.0 copy-start
  5.2 0.0 copy-start.1
  5.2 0.0 copy-start.4
  5.2 0.0 copy-start.3
  5.2 0.7 %collective-permute-start.2 = (bf16[512,128]{1,0:T(8,128)(2,1)S(1)}, bf16[512,128]{1,0:T(8,128)(2,1)S(1)}, u32[]{:S(2)}, u32[]{:S(2)}) collective-permute-start(bf16[512,128]{1,0:T(8,128)(2,1)S(1)} %bitcast.51), channel_id=1, source_target_pairs={{0,28},{4,0},{8,4},{12,8},{16,12},{20,16},{24,20},{28,24},{1,29},{... | collective-permute-start | bytes 393224 | tf_op jit(solution)/shard_map/ppermute | solution.py:421
  6.0 0.1 shard_map.94
  6.1 3.5 %collective-permute-done.2.got_ref = bf16[512,128]{1,0:T(8,128)(2,1)S(1)} collective-permute-done((bf16[512,128]{1,0:T(8,128)(2,1)S(1)}, bf16[512,128]{1,0:T(8,128)(2,1)S(1)}, u32[]{:S(2)}, u32[]{:S(2)}) %collective-permute-start.2) | collective-permute-done | bytes 131104 | tf_op jit(solution)/shard_map/ppermute | solution.py:421
  9.6 0.0 copy-done
  9.6 0.2 shard_map.96
  9.8 1.6 %collective-permute-start.5 = (bf16[64,512]{1,0:T(8,128)(2,1)S(1)}, bf16[64,512]{1,0:T(8,128)(2,1)S(1)}, u32[]{:S(2)}, u32[]{:S(2)}) collective-permute-start(bf16[64,512]{1,0:T(8,128)(2,1)S(1)} %get-tuple-element.50), channel_id=1, source_target_pairs={{0,1},{1,2},{2,3},{3,7},{7,6},{6,5},{5,4},{4,0},{8,9},{9,10},{10,1... | collective-permute-start | bytes 196616 | tf_op jit(solution)/shard_map/ppermute | solution.py:416
  11.4 1.3 %collective-permute-start = (bf16[512,128]{1,0:T(8,128)(2,1)S(1)}, bf16[512,128]{1,0:T(8,128)(2,1)S(1)}, u32[]{:S(2)}, u32[]{:S(2)}) collective-permute-start(bf16[512,128]{1,0:T(8,128)(2,1)S(1)} %bitcast.50), channel_id=1, source_target_pairs={{0,28},{4,0},{8,4},{12,8},{16,12},{20,16},{24,20},{28,24},{1,29},{... | collective-permute-start | bytes 393224 | tf_op jit(solution)/shard_map/ppermute | solution.py:421
  12.7 0.0 collective-permute-start.6
  12.7 0.0 collective-permute-done.1.got_ref
  12.7 0.0 copy-done.1
  12.7 0.3 shard_map.95
  12.9 2.0 %collective-permute-start.3 = (bf16[192,512]{1,0:T(8,128)(2,1)S(1)}, bf16[192,512]{1,0:T(8,128)(2,1)S(1)}, u32[]{:S(2)}, u32[]{:S(2)}) collective-permute-start(bf16[192,512]{1,0:T(8,128)(2,1)S(1)} %get-tuple-element.48), channel_id=1, source_target_pairs={{0,1},{1,2},{2,3},{3,7},{7,6},{6,5},{5,4},{4,0},{8,9},{9,10},{10,1... | collective-permute-start | bytes 589832 | tf_op jit(solution)/shard_map/ppermute | solution.py:416
  15.0 0.0 collective-permute-start.4
  15.0 0.0 collective-permute-done.5.gu_ref
  15.0 0.0 copy-done.4
  15.0 0.1 collective-permute-start.11
  15.0 0.0 copy-done.3
  15.1 1.1 %shard_map.97 = (bf16[192,576]{1,0:T(8,128)(2,1)S(1)}, bf16[192,576]{1,0:T(8,128)(2,1)S(1)}, bf16[192,576]{1,0:T(8,128)(2,1)S(1)}, bf16[192,576]{1,0:T(8,128)(2,...) custom-call(bf16[1,4,27,64,64]{4,3,2,1,0:T(8,128)(2,1)S(1)} %copy-do, ...), custom_call_target="tpu_custom_call" | custom-call | flops 4529848320 | bytes 1048576 | tf_op jit(solution)/shard_map/pallas_call | solution.py:379
  16.2 1.4 %collective-permute-done.6.gd_ref = bf16[64,512]{1,0:T(8,128)(2,1)S(1)} collective-permute-done((bf16[64,512]{1,0:T(8,128)(2,1)S(1)}, bf16[64,512]{1,0:T(8,128)(2,1)S(1)}, u32[]{:S(2)}, u32[]{:S(2)}) %collective-permute-start.6) | collective-permute-done | bytes 65568 | tf_op jit(solution)/shard_map/ppermute | solution.py:417
  17.6 1.9 %collective-permute-done.3.yu_ref = bf16[192,512]{1,0:T(8,128)(2,1)S(1)} collective-permute-done((bf16[192,512]{1,0:T(8,128)(2,1)S(1)}, bf16[192,512]{1,0:T(8,128)(2,1)S(1)}, u32[]{:S(2)}, u32[]{:S(2)}) %collective-permute-start.3) | collective-permute-done | bytes 196640 | tf_op jit(solution)/shard_map/ppermute | solution.py:416
  19.5 1.4 %collective-permute-done.4.yd_ref = bf16[192,512]{1,0:T(8,128)(2,1)S(1)} collective-permute-done((bf16[192,512]{1,0:T(8,128)(2,1)S(1)}, bf16[192,512]{1,0:T(8,128)(2,1)S(1)}, u32[]{:S(2)}, u32[]{:S(2)}) %collective-permute-start.4) | collective-permute-done | bytes 196640 | tf_op jit(solution)/shard_map/ppermute | solution.py:417
  21.0 0.0 copy-start.2
  21.0 2.0 %shard_map.98 = (bf16[128,512]{1,0:T(8,128)(2,1)S(1)}, f32[128,512]{1,0:T(8,128)S(1)}, f32[128,512]{1,0:T(8,128)S(1)}, bf16[256,512]{1,0:T(8,128)(2,1)S(1)}, bf16[256,512]{1,0:T(8,128)(2,1)S(1)}) custom-call(bf16[256,512]{1,0:T(8,128)(2,1)S(1)} %get-tuple-element.46.y_ref, bf16[128,512]{1,0:T(8,128)(2,1)S(1)} %get-tuple-element.47.g2_ref, ...), custom_call_target="tpu_custom_call" | custom-call | flops 905969664 | bytes 1048576 | tf_op jit(solution)/shard_map/pallas_call | solution.py:379
  22.9 0.0 collective-permute-done.got_ref
  23.0 0.2 shard_map.99
  23.2 1.6 %collective-permute-start.7 = (bf16[256,512]{1,0:T(8,128)(2,1)S(1)}, bf16[256,512]{1,0:T(8,128)(2,1)S(1)}, u32[]{:S(2)}, u32[]{:S(2)}) collective-permute-start(bf16[256,512]{1,0:T(8,128)(2,1)S(1)} %get-tuple-element.58.mine_ref), channel_id=1, source_target_pairs={{0,1},{1,2},{2,3},{3,7},{7,6},{6,5},{5,4},{4,0},{8,9},{9,10},{10,1... | collective-permute-start | bytes 786440 | tf_op jit(solution)/shard_map/ppermute | solution.py:416
  24.8 0.0 collective-permute-start.8
  24.8 0.0 collective-permute-done.11.got_ref
  24.8 0.0 copy-done.2
  24.8 0.3 shard_map.102
  25.0 2.0 %collective-permute-start.12 = (bf16[192,512]{1,0:T(8,128)(2,1)S(1)}, bf16[192,512]{1,0:T(8,128)(2,1)S(1)}, u32[]{:S(2)}, u32[]{:S(2)}) collective-permute-start(bf16[192,512]{1,0:T(8,128)(2,1)S(1)} %get-tuple-element.77), channel_id=1, source_target_pairs={{0,1},{1,2},{2,3},{3,7},{7,6},{6,5},{5,4},{4,0},{8,9},{9,10},{10,1... | collective-permute-start | bytes 589832 | tf_op jit(solution)/shard_map/ppermute | solution.py:416
  27.1 0.0 collective-permute-start.13
  27.1 6.8 %collective-permute-done.12.up_ref = bf16[192,512]{1,0:T(8,128)(2,1)S(1)} collective-permute-done((bf16[192,512]{1,0:T(8,128)(2,1)S(1)}, bf16[192,512]{1,0:T(8,128)(2,1)S(1)}, u32[]{:S(2)}, u32[]{:S(2)}) %collective-permute-start.12) | collective-permute-done | bytes 196640 | tf_op jit(solution)/shard_map/ppermute | solution.py:416
  33.9 0.4 collective-permute-done.13.down_ref
  34.3 1.5 %shard_map.103 = (bf16[256,512]{1,0:T(8,128)(2,1)S(1)}, bf16[128,512]{1,0:T(8,128)(2,1)S(1)}) custom-call(bf16[256,512]{1,0:T(8,128)(2,1)S(1)} %get-tuple-element.76.own_ref, bf16[192,512]{1,0:T(8,128)(2,1)S(1)} %collective-permute-done.12.up_ref, bf16[192,512]{1,0:T(8,128)(2,1)S(1)} %collective-permute-done.13.down_ref, ...), custom_call_target="tpu_custom_call" | custom-call | flops 679477248 | bytes 1048576 | tf_op jit(solution)/shard_map/pallas_call | solution.py:379
  35.8 2.1 %collective-permute-start.14 = (bf16[128,512]{1,0:T(8,128)(2,1)S(1)}, bf16[128,512]{1,0:T(8,128)(2,1)S(1)}, u32[]{:S(2)}, u32[]{:S(2)}) collective-permute-start(bf16[128,512]{1,0:T(8,128)(2,1)S(1)} %get-tuple-element.80.own_ref), channel_id=1, source_target_pairs={{0,1},{1,2},{2,3},{3,7},{7,6},{6,5},{5,4},{4,0},{8,9},{9,10},{10,1... | collective-permute-start | bytes 393224 | tf_op jit(solution)/shard_map/ppermute | solution.py:416
  38.0 0.0 collective-permute-start.15
  38.0 0.0 collective-permute-done.7.up_ref
  38.0 0.0 collective-permute-done.8.down_ref
  38.0 2.5 %shard_map.100 = (bf16[256,512]{1,0:T(8,128)(2,1)S(1)}, bf16[128,512]{1,0:T(8,128)(2,1)S(1)}, f32[128,512]{1,0:T(8,128)S(1)}, bf16[128,512]{1,0:T(8,128)(2,1)S(1...) custom-call(bf16[256,512]{1,0:T(8,128)(2,1)S(1)} %get-tuple-element.58.mine_ref, ...), custom_call_target="tpu_custom_call" | custom-call | flops 1358954496 | bytes 1048576 | tf_op jit(solution)/shard_map/pallas_call | solution.py:379
  40.5 2.0 %collective-permute-start.9 = (bf16[64,512]{1,0:T(8,128)(2,1)S(1)}, bf16[64,512]{1,0:T(8,128)(2,1)S(1)}, u32[]{:S(2)}, u32[]{:S(2)}) collective-permute-start(bf16[64,512]{1,0:T(8,128)(2,1)S(1)} %get-tuple-element.67), channel_id=1, source_target_pairs={{0,1},{1,2},{2,3},{3,7},{7,6},{6,5},{5,4},{4,0},{8,9},{9,10},{10,1... | collective-permute-start | bytes 196616 | tf_op jit(solution)/shard_map/ppermute | solution.py:416
  42.5 0.0 collective-permute-start.10
  42.5 0.3 shard_map.101
  42.8 0.0 collective-permute-done.14.up_ref
  42.8 0.8 %collective-permute-done.15.down_ref = bf16[128,512]{1,0:T(8,128)(2,1)S(1)} collective-permute-done((bf16[128,512]{1,0:T(8,128)(2,1)S(1)}, bf16[128,512]{1,0:T(8,128)(2,1)S(1)}, u32[]{:S(2)}, u32[]{:S(2)}) %collective-permute-start.15) | collective-permute-done | bytes 131104 | tf_op jit(solution)/shard_map/ppermute | solution.py:417
  43.6 1.7 %shard_map.104.fwd_ref = bf16[1024,128]{1,0:T(8,128)(2,1)S(1)} custom-call(bf16[256,512]{1,0:T(8,128)(2,1)S(1)} %get-tuple-element.79.mid_ref, bf16[128,512]{1,0:T(8,128)(2,1)S(1)} %get-tuple-element.80.own_ref, bf16[128,512]{1,0:T(8,128)(2,1)S(1)} %collective-permute-done.14.up_ref, bf16[128,512]{1,0:T(8,128)(2,1)S(1)} %collective-permute-done.15.down_ref, ...), custom_call_target="tpu_custom_call" | custom-call | flops 679477248 | bytes 1048576 | tf_op jit(solution)/shard_map/pallas_call | solution.py:379
  45.3 0.0 collective-permute-done.9.up_ref
  45.3 1.5 %collective-permute-done.10.down_ref = bf16[64,512]{1,0:T(8,128)(2,1)S(1)} collective-permute-done((bf16[64,512]{1,0:T(8,128)(2,1)S(1)}, bf16[64,512]{1,0:T(8,128)(2,1)S(1)}, u32[]{:S(2)}, u32[]{:S(2)}) %collective-permute-start.10) | collective-permute-done | bytes 65568 | tf_op jit(solution)/shard_map/ppermute | solution.py:417
  46.8 1.5 %shard_map.105 = (bf16[1024,128]{1,0:T(8,128)(2,1)}, bf16[1024,128]{1,0:T(8,128)(2,1)}, bf16[1024,128]{1,0:T(8,128)(2,1)}) custom-call(bf16[128,512]{1,0:T(8,128)(2,1)S(1)} %get-tuple-element.66.inner_ref, bf16[64,512]{1,0:T(8,128)(2,1)S(1)} %collective-permute-done.9.up_ref, bf16[64,512]{1,0:T(8,128)(2,1)S(1)} %collective-permute-done.10.down_ref, ...), custom_call_target="tpu_custom_call" | custom-call | flops 226492416 | bytes 1048576 | tf_op jit(solution)/shard_map/pallas_call | solution.py:379
Async XLA Ops:
  0.6 12.0 %collective-permute-start.1 = (bf16[1024,128]{1,0:T(8,128)(2,1)}, bf16[1024,128]{1,0:T(8,128)(2,1)S(1)}, u32[]{:S(2)}, u32[]{:S(2)}) collective-permute-start(bf16[1024,128]{1,0:T(8,128)(2,1)} %bitcast.52), channel_id=1, source_target_pairs={{0,28},{4,0},{8,4},{12,8},{16,12},{20,16},{24,20},{28,24},{1,29},{... | collective-permute-start | bytes 786440 | tf_op jit(solution)/shard_map/ppermute | solution.py:421
  5.2 4.4 %copy-start = (bf16[128,2,512]{2,1,0:T(2,128)(2,1)S(1)}, bf16[128,2,512]{2,1,0:T(2,128)(2,1)}, u32[]{:S(2)}) copy-start(bf16[128,2,512]{2,1,0:T(2,128)(2,1)} %param.12) | copy-start | bytes 786436
  5.2 7.5 %copy-start.1 = (bf16[128,2,512]{2,1,0:T(2,128)(2,1)S(1)}, bf16[128,2,512]{2,1,0:T(2,128)(2,1)}, u32[]{:S(2)}) copy-start(bf16[128,2,512]{2,1,0:T(2,128)(2,1)} %param.11) | copy-start | bytes 786436
  5.2 9.8 %copy-start.4 = (bf16[1,128,2,512]{3,2,1,0:T(2,128)(2,1)S(1)}, bf16[1,128,2,512]{3,2,1,0:T(2,128)(2,1)}, u32[]{:S(2)}) copy-start(bf16[1,128,2,512]{3,2,1,0:T(2,128)(2,1)} %param.7) | copy-start | bytes 786436
  5.2 9.8 %copy-start.3 = (bf16[1,4,27,64,64]{4,3,2,1,0:T(8,128)(2,1)S(1)}, bf16[1,4,27,64,64]{4,3,2,1,0:T(8,128)(2,1)}, u32[]{:S(2)}) copy-start(bf16[1,4,27,64,64]{4,3,2,1,0:T(8,128)(2,1)} %kernels_ref.1) | copy-start | bytes 2654212
  5.2 4.3 %collective-permute-start.2 = (bf16[512,128]{1,0:T(8,128)(2,1)S(1)}, bf16[512,128]{1,0:T(8,128)(2,1)S(1)}, u32[]{:S(2)}, u32[]{:S(2)}) collective-permute-start(bf16[512,128]{1,0:T(8,128)(2,1)S(1)} %bitcast.51), channel_id=1, source_target_pairs={{0,28},{4,0},{8,4},{12,8},{16,12},{20,16},{24,20},{28,24},{1,29},{... | collective-permute-start | bytes 393224 | tf_op jit(solution)/shard_map/ppermute | solution.py:421
  9.8 5.2 %collective-permute-start.5 = (bf16[64,512]{1,0:T(8,128)(2,1)S(1)}, bf16[64,512]{1,0:T(8,128)(2,1)S(1)}, u32[]{:S(2)}, u32[]{:S(2)}) collective-permute-start(bf16[64,512]{1,0:T(8,128)(2,1)S(1)} %get-tuple-element.50), channel_id=1, source_target_pairs={{0,1},{1,2},{2,3},{3,7},{7,6},{6,5},{5,4},{4,0},{8,9},{9,10},{10,1... | collective-permute-start | bytes 196616 | tf_op jit(solution)/shard_map/ppermute | solution.py:416
  11.4 11.6 %collective-permute-start = (bf16[512,128]{1,0:T(8,128)(2,1)S(1)}, bf16[512,128]{1,0:T(8,128)(2,1)S(1)}, u32[]{:S(2)}, u32[]{:S(2)}) collective-permute-start(bf16[512,128]{1,0:T(8,128)(2,1)S(1)} %bitcast.50), channel_id=1, source_target_pairs={{0,28},{4,0},{8,4},{12,8},{16,12},{20,16},{24,20},{28,24},{1,29},{... | collective-permute-start | bytes 393224 | tf_op jit(solution)/shard_map/ppermute | solution.py:421
  12.7 5.0 %collective-permute-start.6 = (bf16[64,512]{1,0:T(8,128)(2,1)S(1)}, bf16[64,512]{1,0:T(8,128)(2,1)S(1)}, u32[]{:S(2)}, u32[]{:S(2)}) collective-permute-start(bf16[64,512]{1,0:T(8,128)(2,1)S(1)} %get-tuple-element.51), channel_id=1, source_target_pairs={{1,0},{2,1},{3,2},{7,3},{6,7},{5,6},{4,5},{0,4},{9,8},{10,9},{11,1... | collective-permute-start | bytes 196616 | tf_op jit(solution)/shard_map/ppermute | solution.py:417
  12.9 6.6 %collective-permute-start.3 = (bf16[192,512]{1,0:T(8,128)(2,1)S(1)}, bf16[192,512]{1,0:T(8,128)(2,1)S(1)}, u32[]{:S(2)}, u32[]{:S(2)}) collective-permute-start(bf16[192,512]{1,0:T(8,128)(2,1)S(1)} %get-tuple-element.48), channel_id=1, source_target_pairs={{0,1},{1,2},{2,3},{3,7},{7,6},{6,5},{5,4},{4,0},{8,9},{9,10},{10,1... | collective-permute-start | bytes 589832 | tf_op jit(solution)/shard_map/ppermute | solution.py:416
  15.0 6.0 %collective-permute-start.4 = (bf16[192,512]{1,0:T(8,128)(2,1)S(1)}, bf16[192,512]{1,0:T(8,128)(2,1)S(1)}, u32[]{:S(2)}, u32[]{:S(2)}) collective-permute-start(bf16[192,512]{1,0:T(8,128)(2,1)S(1)} %get-tuple-element.49), channel_id=1, source_target_pairs={{1,0},{2,1},{3,2},{7,3},{6,7},{5,6},{4,5},{0,4},{9,8},{10,9},{11,1... | collective-permute-start | bytes 589832 | tf_op jit(solution)/shard_map/ppermute | solution.py:417
  15.0 9.8 %collective-permute-start.11 = (bf16[1024,128]{1,0:T(8,128)(2,1)S(1)}, bf16[1024,128]{1,0:T(8,128)(2,1)S(1)}, u32[]{:S(2)}, u32[]{:S(2)}) collective-permute-start(bf16[1024,128]{1,0:T(8,128)(2,1)S(1)} %bitcast.53), channel_id=1, source_target_pairs={{0,4},{4,8},{8,12},{12,16},{16,20},{20,24},{24,28},{28,0},{1,5},{5... | collective-permute-start | bytes 786440 | tf_op jit(solution)/shard_map/ppermute | solution.py:421
  21.0 3.8 %copy-start.2 = (bf16[128,2,512]{2,1,0:T(2,128)(2,1)S(1)}, bf16[128,2,512]{2,1,0:T(2,128)(2,1)}, u32[]{:S(2)}) copy-start(bf16[128,2,512]{2,1,0:T(2,128)(2,1)} %param.10) | copy-start | bytes 786436
  23.2 14.8 %collective-permute-start.7 = (bf16[256,512]{1,0:T(8,128)(2,1)S(1)}, bf16[256,512]{1,0:T(8,128)(2,1)S(1)}, u32[]{:S(2)}, u32[]{:S(2)}) collective-permute-start(bf16[256,512]{1,0:T(8,128)(2,1)S(1)} %get-tuple-element.58.mine_ref), channel_id=1, source_target_pairs={{0,1},{1,2},{2,3},{3,7},{7,6},{6,5},{5,4},{4,0},{8,9},{9,10},{10,1... | collective-permute-start | bytes 786440 | tf_op jit(solution)/shard_map/ppermute | solution.py:416
  24.8 13.2 %collective-permute-start.8 = (bf16[256,512]{1,0:T(8,128)(2,1)S(1)}, bf16[256,512]{1,0:T(8,128)(2,1)S(1)}, u32[]{:S(2)}, u32[]{:S(2)}) collective-permute-start(bf16[256,512]{1,0:T(8,128)(2,1)S(1)} %get-tuple-element.58.mine_ref), channel_id=1, source_target_pairs={{1,0},{2,1},{3,2},{7,3},{6,7},{5,6},{4,5},{0,4},{9,8},{10,9},{11,1... | collective-permute-start | bytes 786440 | tf_op jit(solution)/shard_map/ppermute | solution.py:417
  25.0 8.9 %collective-permute-start.12 = (bf16[192,512]{1,0:T(8,128)(2,1)S(1)}, bf16[192,512]{1,0:T(8,128)(2,1)S(1)}, u32[]{:S(2)}, u32[]{:S(2)}) collective-permute-start(bf16[192,512]{1,0:T(8,128)(2,1)S(1)} %get-tuple-element.77), channel_id=1, source_target_pairs={{0,1},{1,2},{2,3},{3,7},{7,6},{6,5},{5,4},{4,0},{8,9},{9,10},{10,1... | collective-permute-start | bytes 589832 | tf_op jit(solution)/shard_map/ppermute | solution.py:416
  27.1 7.2 %collective-permute-start.13 = (bf16[192,512]{1,0:T(8,128)(2,1)S(1)}, bf16[192,512]{1,0:T(8,128)(2,1)S(1)}, u32[]{:S(2)}, u32[]{:S(2)}) collective-permute-start(bf16[192,512]{1,0:T(8,128)(2,1)S(1)} %get-tuple-element.78), channel_id=1, source_target_pairs={{1,0},{2,1},{3,2},{7,3},{6,7},{5,6},{4,5},{0,4},{9,8},{10,9},{11,1... | collective-permute-start | bytes 589832 | tf_op jit(solution)/shard_map/ppermute | solution.py:417
  35.8 7.0 %collective-permute-start.14 = (bf16[128,512]{1,0:T(8,128)(2,1)S(1)}, bf16[128,512]{1,0:T(8,128)(2,1)S(1)}, u32[]{:S(2)}, u32[]{:S(2)}) collective-permute-start(bf16[128,512]{1,0:T(8,128)(2,1)S(1)} %get-tuple-element.80.own_ref), channel_id=1, source_target_pairs={{0,1},{1,2},{2,3},{3,7},{7,6},{6,5},{5,4},{4,0},{8,9},{9,10},{10,1... | collective-permute-start | bytes 393224 | tf_op jit(solution)/shard_map/ppermute | solution.py:416
  38.0 5.6 %collective-permute-start.15 = (bf16[128,512]{1,0:T(8,128)(2,1)S(1)}, bf16[128,512]{1,0:T(8,128)(2,1)S(1)}, u32[]{:S(2)}, u32[]{:S(2)}) collective-permute-start(bf16[128,512]{1,0:T(8,128)(2,1)S(1)} %get-tuple-element.80.own_ref), channel_id=1, source_target_pairs={{1,0},{2,1},{3,2},{7,3},{6,7},{5,6},{4,5},{0,4},{9,8},{10,9},{11,1... | collective-permute-start | bytes 393224 | tf_op jit(solution)/shard_map/ppermute | solution.py:417
  40.5 4.8 %collective-permute-start.9 = (bf16[64,512]{1,0:T(8,128)(2,1)S(1)}, bf16[64,512]{1,0:T(8,128)(2,1)S(1)}, u32[]{:S(2)}, u32[]{:S(2)}) collective-permute-start(bf16[64,512]{1,0:T(8,128)(2,1)S(1)} %get-tuple-element.67), channel_id=1, source_target_pairs={{0,1},{1,2},{2,3},{3,7},{7,6},{6,5},{5,4},{4,0},{8,9},{9,10},{10,1... | collective-permute-start | bytes 196616 | tf_op jit(solution)/shard_map/ppermute | solution.py:416
  42.5 4.3 %collective-permute-start.10 = (bf16[64,512]{1,0:T(8,128)(2,1)S(1)}, bf16[64,512]{1,0:T(8,128)(2,1)S(1)}, u32[]{:S(2)}, u32[]{:S(2)}) collective-permute-start(bf16[64,512]{1,0:T(8,128)(2,1)S(1)} %get-tuple-element.68), channel_id=1, source_target_pairs={{1,0},{2,1},{3,2},{7,3},{6,7},{5,6},{4,5},{0,4},{9,8},{10,9},{11,1... | collective-permute-start | bytes 196616 | tf_op jit(solution)/shard_map/ppermute | solution.py:417
